TPU v7x, 512 devices: a whole 4x8x8 slice. The times are simulated.
512 devices in a mesh: dp: 16 (over z_lo, x, core), expert: 32 (over y, z_hi).
Axes of the slice: x: 4, y: 8, z: 8 (z_hi: 4, z_lo: 2; z = z_hi * 2 + z_lo), core: 2. Of those that a mesh axis runs over, the one named last changes fastest.
Arguments:
- tokens: bfloat16 [65536, 4096], P(('dp', 'expert')), may hold values from -6 to 6
- output_gradient: bfloat16 [65536, 4096], P(('dp', 'expert')), may hold values from -6 to 6
- slot: int32 [65536, 4], P(('dp', 'expert')), may hold values from -1 to 7, as said below
- gate_weight: float32 [65536, 4], P(('dp', 'expert')), may hold values from 0.2 to 1
- gate_up_weight: bfloat16 [32, 4096, 384], P('expert', 'dp'), may hold values from -0.09375 to 0.09375
- down_weight: bfloat16 [32, 192, 4096], P('expert', None, 'dp'), may hold values from -0.15625 to 0.15625
Outputs:
- grad_tokens: bfloat16 [65536, 4096], P(('dp', 'expert'))
- grad_gate_up: bfloat16 [32, 4096, 384], P('expert', 'dp')
Inputs may be any that keep to these rules, and one draw needn't show every extreme that they name: `slot`: within the tokens of one block of 128 and one window expert, the values other than -1 are 0, 1, ..., k - 1, each once; one window expert, the same one in every block, takes all 8 slots in every block, and each of the other window experts takes at most 4 slots in that block.
All inputs are finite; a program needn't handle non-finite values.
Results may differ from a plain program's by a relative error of at most 0.022.
Values may be sent and summed in bfloat16 or wider, within the bound.
No kernel may reach another device: no remote copies, remote signals or barrier semaphores. Data moves between devices by JAX's collectives and lax.ppermute only.
A program may use at most 64 MiB of HBM per device.

v0:
```python
import jax
import jax.numpy as jnp
from jax import lax
from jax.sharding import PartitionSpec as P

GROUP = 8
CAP = 8


def sum_gate_up(x_mat, dgu):
    part_gu = lax.dot_general(
        x_mat, dgu, (((0,), (0,)), ((), ())), preferred_element_type=jnp.float32
    )
    return lax.psum_scatter(
        part_gu.astype(jnp.bfloat16), "dp", scatter_dimension=0, tiled=True
    ).astype(jnp.float32)


def on_device(tokens, output_gradient, slot, gate_weight, gate_up_weight, down_weight):
    expert_windows = slot.shape[1]
    width = tokens.shape[1]
    positions = jnp.arange(CAP, dtype=jnp.int32)
    selector = jnp.transpose(slot)[:, None, :] == positions[None, :, None]
    picked_experts = selector.astype(jnp.bfloat16)
    sent_x = jnp.einsum(
        "ect,td->ecd", picked_experts, tokens, preferred_element_type=jnp.float32
    ).astype(jnp.bfloat16)
    picked_dy = jnp.einsum(
        "ect,td->ecd", picked_experts, output_gradient, preferred_element_type=jnp.float32
    )
    selected_gate = jnp.sum(
        jnp.where(selector, jnp.transpose(gate_weight)[:, None, :], 0.0), axis=2
    )
    sent_g = (picked_dy * selected_gate[..., None]).astype(jnp.bfloat16)
    copies_x = jnp.repeat(sent_x, GROUP, axis=0)
    copies_g = jnp.repeat(sent_g, GROUP, axis=0)
    recv_x, received_gradient = (
        lax.all_to_all(copies_x, "expert", split_axis=0, concat_axis=0, tiled=True),
        lax.all_to_all(copies_g, "expert", split_axis=0, concat_axis=0, tiled=True),
    )
    full_gu = lax.all_gather(gate_up_weight[0], "dp", axis=0, tiled=True)
    full_down = lax.all_gather(down_weight[0], "dp", axis=1, tiled=True)
    x_mat = recv_x.reshape(-1, width)
    joined = jnp.dot(x_mat, full_gu, preferred_element_type=jnp.float32)
    half = full_gu.shape[1] // 2
    pre = joined[:, :half]
    up_part = joined[:, half:]
    sig = jax.nn.sigmoid(pre)
    act = pre * sig
    g_mat = received_gradient.reshape(-1, width)
    dh_rows = lax.dot_general(
        g_mat, full_down, (((1,), (1,)), ((), ())), preferred_element_type=jnp.float32
    )
    dgate = dh_rows * up_part * sig * (1.0 + pre * (1.0 - sig))
    dup = dh_rows * act
    dgu = jnp.concatenate([dgate, dup], axis=1).astype(jnp.bfloat16)
    dx_part = lax.dot_general(
        dgu, full_gu, (((1,), (1,)), ((), ())), preferred_element_type=jnp.float32
    ).astype(jnp.bfloat16)
    back = lax.all_to_all(
        dx_part.reshape(recv_x.shape), "expert", split_axis=0, concat_axis=0, tiled=True
    )
    gu_sum = sum_gate_up(x_mat, dgu)
    summed = jnp.sum(back.astype(jnp.float32).reshape(expert_windows, GROUP, CAP, width), axis=1)
    grad_tokens = jnp.einsum("ect,ecd->td", selector.astype(jnp.float32), summed).astype(
        jnp.bfloat16
    )
    return (grad_tokens, gu_sum.astype(jnp.bfloat16)[None])


def solution(mesh):
    in_specs = (
        P(("dp", "expert"), None),
        P(("dp", "expert"), None),
        P(("dp", "expert"), None),
        P(("dp", "expert"), None),
        P("expert", "dp", None),
        P("expert", None, "dp"),
    )
    out_specs = (P(("dp", "expert"), None), P("expert", "dp", None))
    return jax.shard_map(
        on_device, mesh=mesh, in_specs=in_specs, out_specs=out_specs, check_vma=False
    )
```

profile of v0, /device:TPU:16, one launch (start us, length us, event | category | flops | bytes accessed | tf_op | source)
XLA Modules:
  0.0 324.4 jit_solution(12294352834393318903)
XLA Ops:
  7.2 0.0 all-gather.7.cloned.1.call-start
  7.2 0.7 all-gather.7.cloned.1.call-update
  7.9 0.5 copy-done
  8.4 0.9 convolution_convert_fusion.2
  9.3 1.6 broadcast_in_dim.28
  10.9 16.2 %all-to-all-start.1 = ((bf16[32,8,4096]{2,1,0:T(8,128)(2,1)}), bf16[32,8,4096]{2,1,0:T(8,128)(2,1)S(1)}, u32[]{:S(2)}, u32[]{:S(2)}) async-start(bf16[32,8,4096]{2,1,0:T(8,128)(2,1)} %bitcast.42), calls=%async_computation.1 | async-start | bytes 4194304 | tf_op jit(solution)/shard_map/all_to_all | solution.py:38
  27.2 0.1 select_reduce_fusion
  27.2 1.5 fusion.2
  28.7 54.9 %all-to-all-done.1 = bf16[32,8,4096]{2,1,0:T(8,128)(2,1)S(1)} async-done(((bf16[32,8,4096]{2,1,0:T(8,128)(2,1)}), bf16[32,8,4096]{2,1,0:T(8,128)(2,1)S(1)}, u32[]{:S(2)}, u32[]{:S(2)}) %all-to-all-start.1) | async-done | bytes 2097184 | tf_op jit(solution)/shard_map/all_to_all | solution.py:38
  83.7 1.6 broadcast_in_dim.27
  85.3 15.4 %all-to-all-start = ((bf16[32,8,4096]{2,1,0:T(8,128)(2,1)}), bf16[32,8,4096]{2,1,0:T(8,128)(2,1)}, u32[]{:S(2)}, u32[]{:S(2)}) async-start(bf16[32,8,4096]{2,1,0:T(8,128)(2,1)} %bitcast.41), calls=%async_computation | async-start | bytes 4194304 | tf_op jit(solution)/shard_map/all_to_all | solution.py:39
  100.6 0.0 all-gather.5.cloned.1.call-start
  100.7 0.7 all-gather.5.cloned.1.call-update
  101.4 0.0 reduce-scatter.2.cloned.1.call-start
  101.4 2.0 all-gather.7.cloned.1.call-done
  103.4 4.0 %fusion.4 = f32[256,384]{0,1:T(8,128)} fusion(bf16[1,4096,384]{2,1,0:T(8,128)(2,1)} %all-gather.7.cloned.1.call-done, bf16[32,8,4096]{2,1,0:T(8,128)(2,1)S(1)} %all-to-all-done.1), kind=kOutput, calls=%fused_computation.10 | convolution fusion | flops 805306368 | bytes 5636096 | tf_op jit(solution)/shard_map/dot_general | solution.py:44
  107.4 87.8 %all-gather.5.cloned.1.call-done = bf16[1,192,4096]{2,1,0:T(8,128)(2,1)} async-done(((bf16[1,192,256]{2,1,0:T(8,128)(2,1)}), bf16[1,192,4096]{2,1,0:T(8,128)(2,1)}) %all-gather.5.cloned.1.call-update) | async-done | bytes 1572880 | tf_op jit(solution)/shard_map/all_gather | solution.py:42
  195.2 2.9 fusion.15
  198.2 3.0 convolution_convert_fusion
  201.2 3.2 fusion
  204.4 64.3 %all_to_all.15 = bf16[32,8,4096]{2,1,0:T(8,128)(2,1)S(1)} all-to-all(bf16[32,8,4096]{2,1,0:T(8,128)(2,1)S(1)} %fusion), channel_id=1, replica_groups=mesh['dp'=16,'expert'=32] {'expert'}, dimensions={0} | all-to-all | bytes 4194304 | tf_op jit(solution)/shard_map/all_to_all | solution.py:60
  268.6 0.3 convert_reduce_fusion
  269.0 1.5 fusion.1
  270.4 47.4 %reduce-scatter.2.cloned.1.call-done = bf16[256,384]{1,0:T(8,128)(2,1)} async-done(((bf16[4096,384]{1,0:T(8,128)(2,1)}), bf16[256,384]{1,0:T(8,128)(2,1)}) %reduce-scatter.2.cloned.1.call-update) | async-done | bytes 196624 | tf_op jit(solution)/shard_map/reduce_scatter | solution.py:14
  (7 shorter events, 0.0 us)
Async XLA Ops:
  7.2 1.2 copy-start
  7.2 96.2 %all-gather.7.cloned.1.call-start = ((), (), s32[]{:S(2)}) async-start(), calls=%async_computation.6 | async-start | bytes 3342336 | tf_op jit(solution)/shard_map/all_gather | solution.py:41
  10.9 16.2 %copy-start.1 = (s32[128,4]{0,1:T(4,128)S(1)}, s32[128,4]{0,1:T(4,128)}, u32[]{:S(2)}) copy-start(s32[128,4]{0,1:T(4,128)} %param.8) | copy-start | bytes 6148
  10.9 16.2 %copy-start.2 = (f32[128,4]{0,1:T(4,128)S(1)}, f32[128,4]{0,1:T(4,128)}, u32[]{:S(2)}) copy-start(f32[128,4]{0,1:T(4,128)} %param.9) | copy-start | bytes 6148
  10.9 72.7 %all-to-all-start.1 = ((bf16[32,8,4096]{2,1,0:T(8,128)(2,1)}), bf16[32,8,4096]{2,1,0:T(8,128)(2,1)S(1)}, u32[]{:S(2)}, u32[]{:S(2)}) async-start(bf16[32,8,4096]{2,1,0:T(8,128)(2,1)} %bitcast.42), calls=%async_computation.1 | async-start | bytes 4194304 | tf_op jit(solution)/shard_map/all_to_all | solution.py:38
  85.3 110.0 %all-to-all-start = ((bf16[32,8,4096]{2,1,0:T(8,128)(2,1)}), bf16[32,8,4096]{2,1,0:T(8,128)(2,1)}, u32[]{:S(2)}, u32[]{:S(2)}) async-start(bf16[32,8,4096]{2,1,0:T(8,128)(2,1)} %bitcast.41), calls=%async_computation | async-start | bytes 4194304 | tf_op jit(solution)/shard_map/all_to_all | solution.py:39
  100.6 94.6 %all-gather.5.cloned.1.call-start = ((), (), s32[]{:S(2)}) async-start(), calls=%async_computation.5 | async-start | bytes 1671168 | tf_op jit(solution)/shard_map/all_gather | solution.py:42
  101.4 216.5 %reduce-scatter.2.cloned.1.call-start = ((), (), s32[]{:S(2)}) async-start(), calls=%async_computation.4 | async-start | bytes 3342336 | tf_op jit(solution)/shard_map/reduce_scatter | solution.py:14
Sparse Core Ops, SparseCore 0:
  10.2 93.2 all-gather.6
  105.5 89.6 all-gather.4
  201.3 116.4 reduce-scatter.1
where the time goes:
time: 325 us; the launch traced here: 324 us
  waiting for transfers between devices  194 us (60%)
  blocking collectives  64.3 us (20%)
  starting transfers between devices  31.7 us (10%)
  matrix products  17 us (5%)
  between operations  13.8 us (4%)
  local copies, waits for them, and re-layouts  3.68 us (1%)
    all_gather x1, waiting for transfers between devices, on_device(): full_down = lax.all_gather(down_weight[0], 'dp', axis=1, tiled=True)  87.8 us
    all_to_all x1, blocking collectives, on_device(): lax.all_to_all(dx_part.reshape(recv_x.shape), 'expert', split_axis=0, con...  64.3 us
    all_to_all x1, waiting for transfers between devices, on_device(): lax.all_to_all(copies_x, 'expert', split_axis=0, concat_axis=0, tiled=True)  54.9 us
    reduce_scatter x1, waiting for transfers between devices, sum_gate_up(): lax.psum_scatter(part_gu.astype(jnp.bfloat16), 'dp', scatter_dimension=0,...  47.4 us
    all_to_all x1, starting transfers between devices, on_device(): lax.all_to_all(copies_x, 'expert', split_axis=0, concat_axis=0, tiled=True)  16.2 us
    all_to_all x1, starting transfers between devices, on_device(): lax.all_to_all(copies_g, 'expert', split_axis=0, concat_axis=0, tiled=True)  15.4 us
  transfers between devices with their start and end apart: 5, of which 4 were waited for; matrix products, arithmetic and copies ran while one was open for 5% of the time, Pallas kernels for 0%

commit v1 on v0

v1 whole, which is shorter than its diff:
```python
import jax
import jax.numpy as jnp
from jax import lax
from jax.sharding import Mesh, PartitionSpec as P

FINE = ("zl", "x", "c", "yh", "yl", "zh")
EXPERT = ("yh", "yl", "zh")
CAP = 8
LANE = 128


def f32_dot(a, b, dims):
    return lax.dot_general(a, b, (dims, ((), ())), preferred_element_type=jnp.float32)


def a2a(v, axes):
    return lax.all_to_all(v, axes, split_axis=0, concat_axis=0, tiled=True)


def swap_pairs(v, axis):
    return lax.ppermute(v, axis, [(0, 1), (1, 0)])


def on_device(tokens, output_gradient, slot, gate_weight, gate_up_weight, down_weight):
    n_win = slot.shape[1]
    width = tokens.shape[1]
    n_half = width // (2 * LANE)
    hid = down_weight.shape[1]
    n_yl, n_zh = lax.axis_size("yl"), lax.axis_size("zh")

    w_own = jnp.concatenate([gate_up_weight[0], jnp.transpose(down_weight[0])], axis=1)
    w_pair = a2a(w_own.reshape(n_yl, LANE, 3 * hid), "yl")
    w_mine = jnp.transpose(w_pair.reshape(n_yl, LANE, 3, hid), (1, 2, 0, 3)).reshape(LANE, 3 * n_yl * hid)
    w_full = lax.all_gather(w_mine, ("zl", "x", "c"), axis=0, tiled=True)
    gu_cols = 2 * n_yl * hid
    w_gu, w_down = w_full[:, :gu_cols], w_full[:, gu_cols:]

    positions = jnp.arange(CAP, dtype=jnp.int32)
    selector = jnp.transpose(slot)[:, None, :] == positions[None, :, None]
    picked = selector.astype(jnp.bfloat16)
    rows_x = jnp.einsum("ect,td->ecd", picked, tokens, preferred_element_type=jnp.float32).astype(jnp.bfloat16)
    rows_dy = jnp.einsum("ect,td->ecd", picked, output_gradient, preferred_element_type=jnp.float32)
    gate = jnp.sum(jnp.where(selector, jnp.transpose(gate_weight)[:, None, :], 0.0), axis=2)
    rows_g = (rows_dy * gate[..., None]).astype(jnp.bfloat16)
    rows = jnp.concatenate([rows_x, rows_g], axis=1).reshape(n_win, 2 * CAP, n_half, n_yl, LANE)
    rows = jnp.transpose(rows, (0, 3, 1, 2, 4)).reshape(n_win, n_yl, 1, 2 * CAP, n_half * LANE)
    rows = jnp.broadcast_to(rows, (n_win, n_yl, n_zh, 2 * CAP, n_half * LANE))
    recv = a2a(rows.reshape(-1, 2 * CAP, n_half * LANE), EXPERT)
    n_src = recv.shape[0]
    x_mat = recv[:, :CAP].reshape(n_src * CAP, n_half * LANE)
    g_mat = recv[:, CAP:].reshape(n_src * CAP, n_half * LANE)

    part = jnp.concatenate(
        [f32_dot(x_mat, w_gu, ((1,), (0,))), f32_dot(g_mat, w_down, ((1,), (0,)))], axis=1
    ).astype(jnp.bfloat16)
    total = part.astype(jnp.float32) + swap_pairs(part, "yl").astype(jnp.float32)
    pre, up, dh = jnp.split(total, 3, axis=1)
    sig = jax.nn.sigmoid(pre)
    dgate = dh * up * sig * (1.0 + pre * (1.0 - sig))
    dup = dh * (pre * sig)
    dgu = jnp.concatenate([dgate, dup], axis=1).astype(jnp.bfloat16)

    dx = f32_dot(dgu, w_gu, ((1,), (1,))).astype(jnp.bfloat16)
    pgu = f32_dot(x_mat, dgu, ((0,), (0,))).astype(jnp.bfloat16)

    n_c = lax.axis_size("c")
    pgu = jnp.transpose(pgu.reshape(-1, n_c, LANE, gu_cols), (1, 0, 2, 3))
    both = a2a(pgu, "c").astype(jnp.float32)
    chip = (both[0] + both[1]).astype(jnp.bfloat16)
    summed = jnp.sum(a2a(chip, ("zl", "x")).astype(jnp.float32), axis=0).astype(jnp.bfloat16)
    summed = jnp.transpose(summed.reshape(LANE, 2, n_yl, hid), (2, 0, 1, 3)).reshape(n_yl, LANE, 2 * hid)
    grad_gu = a2a(summed, "yl").reshape(1, n_yl * LANE, 2 * hid)

    back = a2a(dx.reshape(n_src, CAP, n_half * LANE), EXPERT)
    back = jnp.sum(back.reshape(n_win, n_yl, n_zh, CAP, n_half, LANE).astype(jnp.float32), axis=2)
    back = jnp.transpose(back, (0, 2, 3, 1, 4)).reshape(n_win, CAP, width)
    grad_tokens = jnp.einsum("ect,ecd->td", selector.astype(jnp.float32), back).astype(jnp.bfloat16)
    return grad_tokens, grad_gu


def solution(mesh):
    fine = Mesh(mesh.devices.reshape(2, 4, 2, 4, 2, 4), FINE)
    dp, ex = FINE[:3], FINE[3:]
    in_specs = (P(FINE, None), P(FINE, None), P(FINE, None), P(FINE, None), P(ex, dp, None), P(ex, None, dp))
    out_specs = (P(FINE, None), P(ex, dp, None))
    return jax.shard_map(on_device, mesh=fine, in_specs=in_specs, out_specs=out_specs, check_vma=False)
```

time: 325 us -> 235 us (0.72)
  the two profiles are of different devices: /device:TPU:16 before, /device:TPU:6 now
where the time goes in v1:
time: 235 us; the launch traced here: 233 us
  waiting for transfers between devices  86.7 us (37%)
  blocking collectives  81.9 us (35%)
  starting transfers between devices  27.6 us (12%)
  between operations  14.2 us (6%)
  matrix products  12 us (5%)
  local copies, waits for them, and re-layouts  5.39 us (2%)
  other arithmetic  5.32 us (2%)
    all_to_all x3, blocking collectives, a2a(): return lax.all_to_all(v, axes, split_axis=0, concat_axis=0, tiled=True)  81.9 us
    all_to_all x3, waiting for transfers between devices, a2a(): return lax.all_to_all(v, axes, split_axis=0, concat_axis=0, tiled=True)  44.7 us
    all_gather x1, waiting for transfers between devices, on_device(): w_full = lax.all_gather(w_mine, ('zl', 'x', 'c'), axis=0, tiled=True)  27.6 us
    all_to_all x3, starting transfers between devices, a2a(): return lax.all_to_all(v, axes, split_axis=0, concat_axis=0, tiled=True)  24.6 us
    ppermute x1, waiting for transfers between devices, swap_pairs(): return lax.ppermute(v, axis, [(0, 1), (1, 0)])  14.4 us
    dot_general x4, matrix products, f32_dot(): lax.dot_general(a, b, (dims, ((), ())), preferred_element_type=jnp.float32)  9.98 us
  transfers between devices with their start and end apart: 5, of which 5 were waited for; matrix products, arithmetic and copies ran while one was open for 4% of the time, Pallas kernels for 0%

profile of v1, /device:TPU:6, one launch (start us, length us, event | category | flops | bytes accessed | tf_op | source)
XLA Modules:
  0.0 233.2 jit_solution(11912355092772392866)
XLA Ops:
  7.2 1.1 copy.35
  8.3 1.1 pad_maximum_fusion.3
  9.6 8.2 %all_to_all.30 = bf16[2,128,576]{1,2,0:T(8,128)(2,1)S(1)} all-to-all(bf16[2,128,576]{1,2,0:T(8,128)(2,1)S(1)} %copy.28), channel_id=1, replica_groups=mesh['zl'=2,'x'=4,'c'=2,'yh'=4,'yl'=2,'zh'=4] {'yl'}, dimensions={0} | all-to-all | bytes 589824 | tf_op jit(solution)/shard_map/all_to_all | solution.py:17
  17.8 0.7 copy.29
  20.2 67.5 %all_to_all.31 = bf16[32,16,2048]{2,1,0:T(8,128)(2,1)S(1)} all-to-all(bf16[32,16,2048]{2,1,0:T(8,128)(2,1)S(1)} %bitcast.53), channel_id=1, replica_groups=mesh['zl'=2,'x'=4,'c'=2,'yh'=4,'yl'=2,'zh'=4] {'yh','yl','zh'}, dimensions={0} | all-to-all | bytes 4194304 | tf_op jit(solution)/shard_map/all_to_all | solution.py:17
  87.7 27.6 %all-gather.2.cloned.1.call-done = bf16[2048,1152]{0,1:T(8,128)(2,1)} async-done(((bf16[128,1152]{0,1:T(8,128)(2,1)}), bf16[2048,1152]{0,1:T(8,128)(2,1)}) %all-gather.2.cloned.1.call-update) | async-done | bytes 4718608 | tf_op jit(solution)/shard_map/all_gather | solution.py:34
  115.3 2.1 fusion.19
  117.5 2.9 %fusion.16 = bf16[256,768]{1,0:T(8,128)(2,1)S(1)} fusion(bf16[2048,1152]{0,1:T(8,128)(2,1)} %all-gather.2.cloned.1.call-done, bf16[32,16,2048]{2,1,0:T(8,128)(2,1)S(1)} %all_to_all.31), kind=kOutput, calls=%fused_computation.19 | convolution fusion | flops 805502976 | bytes 4587520 | tf_op jit(solution)/shard_map/dot_general | solution.py:13
  120.5 3.0 %collective-permute-start = (bf16[256,1152]{1,0:T(8,128)(2,1)S(1)}, bf16[256,1152]{1,0:T(8,128)(2,1)S(1)}, u32[]{:S(2)}, u32[]{:S(2)}) collective-permute-start(bf16[256,1152]{1,0:T(8,128)(2,1)S(1)} %pad_maximum_fusion), channel_id=1, source_target_pairs={{0,4},{4,0},{1,5},{5,1},{2,6},{6,2},{3,7},{7,3},{8,12},{12,8},{9,1... | collective-permute-start | bytes 1769480 | tf_op jit(solution)/shard_map/ppermute | solution.py:21
  123.5 14.4 %collective-permute-done = bf16[256,1152]{1,0:T(8,128)(2,1)S(1)} collective-permute-done((bf16[256,1152]{1,0:T(8,128)(2,1)S(1)}, bf16[256,1152]{1,0:T(8,128)(2,1)S(1)}, u32[]{:S(2)}, u32[]{:S(2)}) %collective-permute-start) | collective-permute-done | bytes 589856 | tf_op jit(solution)/shard_map/ppermute | solution.py:21
  138.2 1.0 convolution_convert_fusion.1
  139.5 6.3 %all_to_all.32 = bf16[2,8,128,768]{3,2,1,0:T(8,128)(2,1)S(1)} all-to-all(bf16[2,8,128,768]{3,2,1,0:T(8,128)(2,1)S(1)} %bitcast.52), channel_id=1, replica_groups=mesh['zl'=2,'x'=4,'c'=2,'yh'=4,'yl'=2,'zh'=4] {'c'}, dimensions={0} | all-to-all | bytes 6291456 | tf_op jit(solution)/shard_map/all_to_all | solution.py:17
  146.5 1.5 fusion.13
  147.9 9.3 %all-to-all-start.4 = ((bf16[8,128,768]{2,1,0:T(8,128)(2,1)}), bf16[8,128,768]{2,1,0:T(8,128)(2,1)S(1)}, u32[]{:S(2)}, u32[]{:S(2)}) async-start(bf16[8,128,768]{2,1,0:T(8,128)(2,1)} %fusion.13), calls=%async_computation.4 | async-start | bytes 3145728 | tf_op jit(solution)/shard_map/all_to_all | solution.py:17
  157.2 3.9 %fusion.10 = bf16[32,8,2048]{2,1,0:T(8,128)(2,1)} fusion(bf16[2048,1152]{0,1:T(8,128)(2,1)} %all-gather.2.cloned.1.call-done, bf16[256,384]{1,0:T(8,128)(2,1)S(1)} %get-tuple-element.3, bf16[256,384]{1,0:T(8,128)(2,1)S(1)} %get-tuple-element.2), kind=kOutput, calls=%fused_computation.14 | convolution fusion | flops 806617088 | bytes 4587520 | tf_op jit(solution)/shard_map/dot_general | solution.py:13
  161.1 15.5 %all-to-all-done.4 = bf16[8,128,768]{2,1,0:T(8,128)(2,1)S(1)} async-done(((bf16[8,128,768]{2,1,0:T(8,128)(2,1)}), bf16[8,128,768]{2,1,0:T(8,128)(2,1)S(1)}, u32[]{:S(2)}, u32[]{:S(2)}) %all-to-all-start.4) | async-done | bytes 1572896 | tf_op jit(solution)/shard_map/all_to_all | solution.py:17
  176.6 11.9 %all-to-all-start.2 = ((bf16[32,8,2048]{2,1,0:T(8,128)(2,1)}), bf16[32,8,2048]{2,1,0:T(8,128)(2,1)}, u32[]{:S(2)}, u32[]{:S(2)}) async-start(bf16[32,8,2048]{2,1,0:T(8,128)(2,1)} %fusion.10), calls=%async_computation.2 | async-start | bytes 2097152 | tf_op jit(solution)/shard_map/all_to_all | solution.py:17
  188.9 0.7 copy.33
  189.6 27.7 %all-to-all-done.2 = bf16[32,8,2048]{2,1,0:T(8,128)(2,1)} async-done(((bf16[32,8,2048]{2,1,0:T(8,128)(2,1)}), bf16[32,8,2048]{2,1,0:T(8,128)(2,1)}, u32[]{:S(2)}, u32[]{:S(2)}) %all-to-all-start.2) | async-done | bytes 1048608 | tf_op jit(solution)/shard_map/all_to_all | solution.py:17
  217.3 3.4 %all-to-all-start.5 = ((bf16[2,128,384]{1,2,0:T(8,128)(2,1)}), bf16[2,128,384]{1,2,0:T(8,128)(2,1)S(1)}, u32[]{:S(2)}, u32[]{:S(2)}) async-start(bf16[2,128,384]{1,2,0:T(8,128)(2,1)} %bitcast.24), calls=%async_computation.5 | async-start | bytes 393216 | tf_op jit(solution)/shard_map/all_to_all | solution.py:17
  220.7 1.4 convert_reduce_fusion
  222.5 1.5 fusion
  224.0 1.5 all-to-all-done.5
  225.5 0.8 copy.34
  (28 shorter events, 4.1 us)
Async XLA Ops:
  7.2 11.5 %copy-start = (bf16[128,4096]{1,0:T(8,128)(2,1)S(1)}, bf16[128,4096]{1,0:T(8,128)(2,1)}, u32[]{:S(2)}) copy-start(bf16[128,4096]{1,0:T(8,128)(2,1)} %param.6) | copy-start | bytes 3145732
  7.2 11.4 %copy-start.3 = (f32[128,4]{0,1:T(4,128)S(1)}, f32[128,4]{0,1:T(4,128)}, u32[]{:S(2)}) copy-start(f32[128,4]{0,1:T(4,128)} %param.9) | copy-start | bytes 6148
  7.2 11.4 %copy-start.2 = (s32[128,4]{0,1:T(4,128)S(1)}, s32[128,4]{0,1:T(4,128)}, u32[]{:S(2)}) copy-start(s32[128,4]{0,1:T(4,128)} %param.8) | copy-start | bytes 6148
  7.2 108.1 %all-gather.2.cloned.1.call-start = ((), (), s32[]{:S(2)}) async-start(), calls=%async_computation.6 | async-start | bytes 5013504 | tf_op jit(solution)/shard_map/all_gather | solution.py:34
  8.3 10.6 %copy-start.1 = (bf16[128,4096]{1,0:T(8,128)(2,1)S(1)}, bf16[128,4096]{1,0:T(8,128)(2,1)}, u32[]{:S(2)}) copy-start(bf16[128,4096]{1,0:T(8,128)(2,1)} %param.7) | copy-start | bytes 3145732
  120.5 17.4 %collective-permute-start = (bf16[256,1152]{1,0:T(8,128)(2,1)S(1)}, bf16[256,1152]{1,0:T(8,128)(2,1)S(1)}, u32[]{:S(2)}, u32[]{:S(2)}) collective-permute-start(bf16[256,1152]{1,0:T(8,128)(2,1)S(1)} %pad_maximum_fusion), channel_id=1, source_target_pairs={{0,4},{4,0},{1,5},{5,1},{2,6},{6,2},{3,7},{7,3},{8,12},{12,8},{9,1... | collective-permute-start | bytes 1769480 | tf_op jit(solution)/shard_map/ppermute | solution.py:21
  147.9 28.6 %all-to-all-start.4 = ((bf16[8,128,768]{2,1,0:T(8,128)(2,1)}), bf16[8,128,768]{2,1,0:T(8,128)(2,1)S(1)}, u32[]{:S(2)}, u32[]{:S(2)}) async-start(bf16[8,128,768]{2,1,0:T(8,128)(2,1)} %fusion.13), calls=%async_computation.4 | async-start | bytes 3145728 | tf_op jit(solution)/shard_map/all_to_all | solution.py:17
  176.6 40.7 %all-to-all-start.2 = ((bf16[32,8,2048]{2,1,0:T(8,128)(2,1)}), bf16[32,8,2048]{2,1,0:T(8,128)(2,1)}, u32[]{:S(2)}, u32[]{:S(2)}) async-start(bf16[32,8,2048]{2,1,0:T(8,128)(2,1)} %fusion.10), calls=%async_computation.2 | async-start | bytes 2097152 | tf_op jit(solution)/shard_map/all_to_all | solution.py:17
  217.3 8.2 %all-to-all-start.5 = ((bf16[2,128,384]{1,2,0:T(8,128)(2,1)}), bf16[2,128,384]{1,2,0:T(8,128)(2,1)S(1)}, u32[]{:S(2)}, u32[]{:S(2)}) async-start(bf16[2,128,384]{1,2,0:T(8,128)(2,1)} %bitcast.24), calls=%async_computation.5 | async-start | bytes 393216 | tf_op jit(solution)/shard_map/all_to_all | solution.py:17
Sparse Core Ops, SparseCore 0:
  18.7 96.6 all-gather.1

commit v2 on v1

--- a/solution.py
+++ b/solution.py
@@ -28,10 +28,12 @@
     hid = down_weight.shape[1]
     n_yl, n_zh = lax.axis_size("yl"), lax.axis_size("zh")
 
+    n_zl = lax.axis_size("zl")
     w_own = jnp.concatenate([gate_up_weight[0], jnp.transpose(down_weight[0])], axis=1)
-    w_pair = a2a(w_own.reshape(n_yl, LANE, 3 * hid), "yl")
-    w_mine = jnp.transpose(w_pair.reshape(n_yl, LANE, 3, hid), (1, 2, 0, 3)).reshape(LANE, 3 * n_yl * hid)
-    w_full = lax.all_gather(w_mine, ("zl", "x", "c"), axis=0, tiled=True)
+    w_sent = jnp.broadcast_to(w_own.reshape(1, n_yl, LANE, 3 * hid), (n_zl, n_yl, LANE, 3 * hid))
+    w_pair = a2a(w_sent.reshape(n_zl * n_yl, LANE, 3 * hid), ("zl", "yl"))
+    w_mine = jnp.transpose(w_pair.reshape(n_zl, n_yl, LANE, 3, hid), (0, 2, 3, 1, 4))
+    w_full = lax.all_gather(w_mine.reshape(n_zl * LANE, 3 * n_yl * hid), ("x", "c"), axis=0, tiled=True)
     gu_cols = 2 * n_yl * hid
     w_gu, w_down = w_full[:, :gu_cols], w_full[:, gu_cols:]
 
@@ -42,8 +44,9 @@
     rows_dy = jnp.einsum("ect,td->ecd", picked, output_gradient, preferred_element_type=jnp.float32)
     gate = jnp.sum(jnp.where(selector, jnp.transpose(gate_weight)[:, None, :], 0.0), axis=2)
     rows_g = (rows_dy * gate[..., None]).astype(jnp.bfloat16)
-    rows = jnp.concatenate([rows_x, rows_g], axis=1).reshape(n_win, 2 * CAP, n_half, n_yl, LANE)
-    rows = jnp.transpose(rows, (0, 3, 1, 2, 4)).reshape(n_win, n_yl, 1, 2 * CAP, n_half * LANE)
+    n_xc = n_half // n_zl
+    rows = jnp.concatenate([rows_x, rows_g], axis=1).reshape(n_win, 2 * CAP, n_zl, n_xc, n_yl, LANE)
+    rows = jnp.transpose(rows, (0, 4, 1, 3, 2, 5)).reshape(n_win, n_yl, 1, 2 * CAP, n_half * LANE)
     rows = jnp.broadcast_to(rows, (n_win, n_yl, n_zh, 2 * CAP, n_half * LANE))
     recv = a2a(rows.reshape(-1, 2 * CAP, n_half * LANE), EXPERT)
     n_src = recv.shape[0]
@@ -63,17 +66,15 @@
     dx = f32_dot(dgu, w_gu, ((1,), (1,))).astype(jnp.bfloat16)
     pgu = f32_dot(x_mat, dgu, ((0,), (0,))).astype(jnp.bfloat16)
 
-    n_c = lax.axis_size("c")
-    pgu = jnp.transpose(pgu.reshape(-1, n_c, LANE, gu_cols), (1, 0, 2, 3))
-    both = a2a(pgu, "c").astype(jnp.float32)
-    chip = (both[0] + both[1]).astype(jnp.bfloat16)
-    summed = jnp.sum(a2a(chip, ("zl", "x")).astype(jnp.float32), axis=0).astype(jnp.bfloat16)
-    summed = jnp.transpose(summed.reshape(LANE, 2, n_yl, hid), (2, 0, 1, 3)).reshape(n_yl, LANE, 2 * hid)
-    grad_gu = a2a(summed, "yl").reshape(1, n_yl * LANE, 2 * hid)
+    summed = lax.psum_scatter(pgu, ("x", "c"), scatter_dimension=0, tiled=True)
+    summed = jnp.transpose(summed.reshape(n_zl, LANE, 2, n_yl, hid), (0, 3, 1, 2, 4))
+    summed = a2a(summed.reshape(n_zl * n_yl, LANE, 2 * hid), ("zl", "yl"))
+    grad_gu = jnp.sum(summed.reshape(n_zl, n_yl * LANE, 2 * hid).astype(jnp.float32), axis=0)
+    grad_gu = grad_gu.astype(jnp.bfloat16)[None]
 
     back = a2a(dx.reshape(n_src, CAP, n_half * LANE), EXPERT)
-    back = jnp.sum(back.reshape(n_win, n_yl, n_zh, CAP, n_half, LANE).astype(jnp.float32), axis=2)
-    back = jnp.transpose(back, (0, 2, 3, 1, 4)).reshape(n_win, CAP, width)
+    back = jnp.sum(back.reshape(n_win, n_yl, n_zh, CAP, n_xc, n_zl, LANE).astype(jnp.float32), axis=2)
+    back = jnp.transpose(back, (0, 2, 4, 3, 1, 5)).reshape(n_win, CAP, width)
     grad_tokens = jnp.einsum("ect,ecd->td", selector.astype(jnp.float32), back).astype(jnp.bfloat16)
     return grad_tokens, grad_gu
 

time: 235 us -> 175 us (0.74)
  waiting for transfers between devices: 86.7 us -> 38.4 us
  starting transfers between devices: 27.6 us -> 20.4 us
  blocking collectives: 81.9 us -> 78.1 us
  other arithmetic: 5.32 us -> 2.37 us
    all_to_all x3 -> x2, waiting for transfers between devices: 44.7 us -> 4.47 us  [a2a(): return lax.all_to_all(v, axes, split_axis=0, concat_axis=0, tiled=True)]
    all_gather x1, waiting for transfers between devices: 27.6 us -> 0.01 us  [on_device(): lax.all_gather(w_mine.reshape(n_zl * LANE, 3 * n_yl * hid), ('x', 'c'), a...]
    reduce_scatter x0 -> x1, waiting for transfers between devices: none -> 24.8 us  [on_device(): summed = lax.psum_scatter(pgu, ('x', 'c'), scatter_dimension=0, tiled=True)]
    all_to_all x3 -> x2, starting transfers between devices: 24.6 us -> 16 us  [a2a(): return lax.all_to_all(v, axes, split_axis=0, concat_axis=0, tiled=True)]
    ppermute x1, waiting for transfers between devices: 14.4 us -> 9.1 us  [swap_pairs(): return lax.ppermute(v, axis, [(0, 1), (1, 0)])]
    all_to_all x3 -> x2, blocking collectives: 81.9 us -> 78.1 us  [a2a(): return lax.all_to_all(v, axes, split_axis=0, concat_axis=0, tiled=True)]
  transfers between devices with their start and end apart: 5 -> 5, of which waited for: 5 -> 4; matrix products, arithmetic and copies ran while one was open for 4% -> 6% of each run, Pallas kernels for 0% -> 0%
where the time goes in v2:
time: 175 us; the launch traced here: 174 us
  blocking collectives  78.1 us (45%)
  waiting for transfers between devices  38.4 us (22%)
  starting transfers between devices  20.4 us (12%)
  between operations  14.2 us (8%)
  matrix products  13.6 us (8%)
  local copies, waits for them, and re-layouts  7.05 us (4%)
  other arithmetic  2.37 us (1%)
    all_to_all x2, blocking collectives, a2a(): return lax.all_to_all(v, axes, split_axis=0, concat_axis=0, tiled=True)  78.1 us
    reduce_scatter x1, waiting for transfers between devices, on_device(): summed = lax.psum_scatter(pgu, ('x', 'c'), scatter_dimension=0, tiled=True)  24.8 us
    all_to_all x2, starting transfers between devices, a2a(): return lax.all_to_all(v, axes, split_axis=0, concat_axis=0, tiled=True)  16 us
    dot_general x4, matrix products, f32_dot(): lax.dot_general(a, b, (dims, ((), ())), preferred_element_type=jnp.float32)  11.6 us
    ppermute x1, waiting for transfers between devices, swap_pairs(): return lax.ppermute(v, axis, [(0, 1), (1, 0)])  9.1 us
    all_to_all x2, waiting for transfers between devices, a2a(): return lax.all_to_all(v, axes, split_axis=0, concat_axis=0, tiled=True)  4.47 us
    ppermute x1, starting transfers between devices, swap_pairs(): return lax.ppermute(v, axis, [(0, 1), (1, 0)])  4.26 us
  transfers between devices with their start and end apart: 5, of which 4 were waited for; matrix products, arithmetic and copies ran while one was open for 6% of the time, Pallas kernels for 0%

profile of v2, /device:TPU:6, one launch (start us, length us, event | category | flops | bytes accessed | tf_op | source)
XLA Modules:
  0.0 174.1 jit_solution(14301689987578444293)
XLA Ops:
  7.2 1.1 copy.37
  8.3 1.0 maximum_bitcast_fusion
  9.6 13.9 %all_to_all.20 = bf16[4,128,576]{1,2,0:T(8,128)(2,1)S(1)} all-to-all(bf16[4,128,576]{1,2,0:T(8,128)(2,1)S(1)} %bitcast.58), channel_id=1, replica_groups=mesh['zl'=2,'x'=4,'c'=2,'yh'=4,'yl'=2,'zh'=4] {'zl','yl'}, dimensions={0} | all-to-all | bytes 1179648 | tf_op jit(solution)/shard_map/all_to_all | solution.py:17
  23.5 0.6 copy.32
  24.1 0.9 copy.41
  25.8 0.4 reshape.52
  26.1 0.4 copy.42
  26.5 0.4 broadcast_in_dim.35
  27.2 64.2 %all_to_all.21 = bf16[32,16,2048]{2,1,0:T(8,128)(2,1)S(1)} all-to-all(bf16[32,16,2048]{2,1,0:T(8,128)(2,1)S(1)} %bitcast.55), channel_id=1, replica_groups=mesh['zl'=2,'x'=4,'c'=2,'yh'=4,'yl'=2,'zh'=4] {'yh','yl','zh'}, dimensions={0} | all-to-all | bytes 4194304 | tf_op jit(solution)/shard_map/all_to_all | solution.py:17
  91.4 2.1 %fusion.17 = bf16[256,384]{1,0:T(8,128)(2,1)S(1)} fusion(bf16[2048,1152]{0,1:T(8,128)(2,1)} %all-gather.2.cloned.1.call-done, bf16[32,16,2048]{2,1,0:T(8,128)(2,1)S(1)} %all_to_all.21), kind=kOutput, calls=%fused_computation.17 | convolution fusion | flops 402751488 | bytes 2818048 | tf_op jit(solution)/shard_map/dot_general | solution.py:13
  93.6 2.9 %fusion.14 = bf16[256,768]{1,0:T(8,128)(2,1)S(1)} fusion(bf16[2048,1152]{0,1:T(8,128)(2,1)} %all-gather.2.cloned.1.call-done, bf16[32,16,2048]{2,1,0:T(8,128)(2,1)S(1)} %all_to_all.21), kind=kOutput, calls=%fused_computation.15 | convolution fusion | flops 805502976 | bytes 4587520 | tf_op jit(solution)/shard_map/dot_general | solution.py:13
  96.6 4.3 %collective-permute-start = (bf16[256,1152]{1,0:T(8,128)(2,1)S(1)}, bf16[256,1152]{1,0:T(8,128)(2,1)S(1)}, u32[]{:S(2)}, u32[]{:S(2)}) collective-permute-start(bf16[256,1152]{1,0:T(8,128)(2,1)S(1)} %pad_maximum_fusion), channel_id=1, source_target_pairs={{0,4},{4,0},{1,5},{5,1},{2,6},{6,2},{3,7},{7,3},{8,12},{12,8},{9,1... | collective-permute-start | bytes 1769480 | tf_op jit(solution)/shard_map/ppermute | solution.py:21
  100.8 9.1 %collective-permute-done = bf16[256,1152]{1,0:T(8,128)(2,1)S(1)} collective-permute-done((bf16[256,1152]{1,0:T(8,128)(2,1)S(1)}, bf16[256,1152]{1,0:T(8,128)(2,1)S(1)}, u32[]{:S(2)}, u32[]{:S(2)}) %collective-permute-start) | collective-permute-done | bytes 589856 | tf_op jit(solution)/shard_map/ppermute | solution.py:21
  110.3 2.7 %convolution_convert_fusion.1 = bf16[2048,768]{1,0:T(8,128)(2,1)} fusion(bf16[32,16,2048]{2,1,0:T(8,128)(2,1)S(1)} %all_to_all.21, bf16[256,384]{1,0:T(8,128)(2,1)S(1)} %get-tuple-element.3, bf16[256,384]{1,0:T(8,128)(2,1)S(1)} %get-tuple-element.2), kind=kOutput, calls=%fused_computation.5 | convolution fusion | flops 807665664 | bytes 4587520 | tf_op jit(solution)/shard_map/dot_general | solution.py:13
  113.0 3.9 %fusion.9 = bf16[32,8,2048]{2,1,0:T(8,128)(2,1)} fusion(bf16[2048,1152]{0,1:T(8,128)(2,1)} %all-gather.2.cloned.1.call-done, bf16[256,384]{1,0:T(8,128)(2,1)S(1)} %get-tuple-element.3, bf16[256,384]{1,0:T(8,128)(2,1)S(1)} %get-tuple-element.2), kind=kOutput, calls=%fused_computation.11 | convolution fusion | flops 806617088 | bytes 4587520 | tf_op jit(solution)/shard_map/dot_general | solution.py:13
  116.9 9.4 %all-to-all-start.2 = ((bf16[32,8,2048]{2,1,0:T(8,128)(2,1)}), bf16[32,8,2048]{2,1,0:T(8,128)(2,1)S(1)}, u32[]{:S(2)}, u32[]{:S(2)}) async-start(bf16[32,8,2048]{2,1,0:T(8,128)(2,1)} %fusion.9), calls=%async_computation.2 | async-start | bytes 2097152 | tf_op jit(solution)/shard_map/all_to_all | solution.py:17
  126.3 24.8 %reduce-scatter.2.cloned.1.call-done = bf16[256,768]{1,0:T(8,128)(2,1)} async-done(((bf16[2048,768]{1,0:T(8,128)(2,1)}), bf16[256,768]{1,0:T(8,128)(2,1)}) %reduce-scatter.2.cloned.1.call-update) | async-done | bytes 393232 | tf_op jit(solution)/shard_map/reduce_scatter | solution.py:69
  151.1 1.2 copy.34
  152.4 0.8 copy.35
  153.2 0.7 all-to-all-done.2
  153.9 6.6 %all-to-all-start.3 = ((bf16[4,128,384]{1,2,0:T(8,128)(2,1)}), bf16[4,128,384]{1,2,0:T(8,128)(2,1)S(1)}, u32[]{:S(2)}, u32[]{:S(2)}) async-start(bf16[4,128,384]{1,2,0:T(8,128)(2,1)} %bitcast.21), calls=%async_computation.4 | async-start | bytes 786432 | tf_op jit(solution)/shard_map/all_to_all | solution.py:17
  161.1 1.5 fusion
  162.5 3.8 %all-to-all-done.3 = bf16[4,128,384]{1,2,0:T(8,128)(2,1)S(1)} async-done(((bf16[4,128,384]{1,2,0:T(8,128)(2,1)}), bf16[4,128,384]{1,2,0:T(8,128)(2,1)S(1)}, u32[]{:S(2)}, u32[]{:S(2)}) %all-to-all-start.3) | async-done | bytes 393248 | tf_op jit(solution)/shard_map/all_to_all | solution.py:17
  166.6 0.7 bitcast_reduce_fusion
  (28 shorter events, 2.7 us)
Async XLA Ops:
  7.2 18.0 %copy-start = (bf16[128,4096]{1,0:T(8,128)(2,1)S(1)}, bf16[128,4096]{1,0:T(8,128)(2,1)}, u32[]{:S(2)}) copy-start(bf16[128,4096]{1,0:T(8,128)(2,1)} %param.6) | copy-start | bytes 3145732
  7.2 84.2 %all-gather.2.cloned.1.call-start = ((), (), s32[]{:S(2)}) async-start(), calls=%async_computation.5 | async-start | bytes 5308416 | tf_op jit(solution)/shard_map/all_gather | solution.py:36
  9.6 15.5 %copy-start.2 = (s32[128,4]{0,1:T(4,128)S(1)}, s32[128,4]{0,1:T(4,128)}, u32[]{:S(2)}) copy-start(s32[128,4]{0,1:T(4,128)} %param.8) | copy-start | bytes 6148
  9.6 15.5 %copy-start.3 = (f32[128,4]{0,1:T(4,128)S(1)}, f32[128,4]{0,1:T(4,128)}, u32[]{:S(2)}) copy-start(f32[128,4]{0,1:T(4,128)} %param.9) | copy-start | bytes 6148
  23.5 2.0 %copy-start.1 = (bf16[128,4096]{1,0:T(8,128)(2,1)S(1)}, bf16[128,4096]{1,0:T(8,128)(2,1)}, u32[]{:S(2)}) copy-start(bf16[128,4096]{1,0:T(8,128)(2,1)} %param.7) | copy-start | bytes 3145732
  25.0 126.1 %reduce-scatter.2.cloned.1.call-start = ((), (), s32[]{:S(2)}) async-start(), calls=%async_computation.6 | async-start | bytes 3538944 | tf_op jit(solution)/shard_map/reduce_scatter | solution.py:69
  96.6 13.4 %collective-permute-start = (bf16[256,1152]{1,0:T(8,128)(2,1)S(1)}, bf16[256,1152]{1,0:T(8,128)(2,1)S(1)}, u32[]{:S(2)}, u32[]{:S(2)}) collective-permute-start(bf16[256,1152]{1,0:T(8,128)(2,1)S(1)} %pad_maximum_fusion), channel_id=1, source_target_pairs={{0,4},{4,0},{1,5},{5,1},{2,6},{6,2},{3,7},{7,3},{8,12},{12,8},{9,1... | collective-permute-start | bytes 1769480 | tf_op jit(solution)/shard_map/ppermute | solution.py:21
  116.9 37.0 %all-to-all-start.2 = ((bf16[32,8,2048]{2,1,0:T(8,128)(2,1)}), bf16[32,8,2048]{2,1,0:T(8,128)(2,1)S(1)}, u32[]{:S(2)}, u32[]{:S(2)}) async-start(bf16[32,8,2048]{2,1,0:T(8,128)(2,1)} %fusion.9), calls=%async_computation.2 | async-start | bytes 2097152 | tf_op jit(solution)/shard_map/all_to_all | solution.py:17
  153.9 12.5 %all-to-all-start.3 = ((bf16[4,128,384]{1,2,0:T(8,128)(2,1)}), bf16[4,128,384]{1,2,0:T(8,128)(2,1)S(1)}, u32[]{:S(2)}, u32[]{:S(2)}) async-start(bf16[4,128,384]{1,2,0:T(8,128)(2,1)} %bitcast.21), calls=%async_computation.4 | async-start | bytes 786432 | tf_op jit(solution)/shard_map/all_to_all | solution.py:17
Sparse Core Ops, SparseCore 0:
  25.1 45.7 all-gather.1
  113.1 37.9 reduce-scatter.1

commit v3 on v2

v3 whole, which is shorter than its diff:
```python
import jax
import jax.numpy as jnp
from jax import lax
from jax.experimental import pallas as pl
from jax.experimental.pallas import tpu as pltpu
from jax.sharding import Mesh, PartitionSpec as P

FINE = ("zl", "x", "c", "yh", "yl", "zh")
EXPERT = ("yh", "yl", "zh")
CAP = 8
LANE = 128


def f32_dot(a, b, dims):
    return lax.dot_general(a, b, (dims, ((), ())), preferred_element_type=jnp.float32)


def a2a(v, axes):
    return lax.all_to_all(v, axes, split_axis=0, concat_axis=0, tiled=True)


def swap(v, flip):
    return lax.ppermute(v, ("zl", "yl"), [(i, i ^ flip) for i in range(4)])


def part_kernel(gu_cols, w_ref, first_ref, rest_ref, part_ref, acc_gu, acc_dh):
    step = pl.program_id(0)

    def products(rows_ref):
        n_src, _, depth = rows_ref.shape
        x = rows_ref[:, :CAP, :].reshape(n_src * CAP, depth)
        g = rows_ref[:, CAP:, :].reshape(n_src * CAP, depth)
        gu = jnp.dot(x, w_ref[:, :gu_cols], preferred_element_type=jnp.float32)
        return gu, jnp.dot(g, w_ref[:, gu_cols:], preferred_element_type=jnp.float32)

    @pl.when(step == 0)
    def _():
        acc_gu[...], acc_dh[...] = products(first_ref)

    @pl.when(step > 0)
    def _():
        gu, dh = products(rest_ref)
        acc_gu[...] += gu
        acc_dh[...] += dh

    @pl.when(step == pl.num_programs(0) - 1)
    def _():
        part_ref[:, :gu_cols] = acc_gu[...].astype(part_ref.dtype)
        part_ref[:, gu_cols:] = acc_dh[...].astype(part_ref.dtype)


def row_specs(first, rest):
    n_src, rows, depth = first.shape
    return [
        pl.BlockSpec((n_src, rows, depth), lambda k: (0, 0, 0)),
        pl.BlockSpec((n_src, rows, depth), lambda k: (0, 0, jnp.maximum(k - 1, 0))),
    ]


def partial_products(w_full, first, rest, gu_cols):
    n_src, _, depth = first.shape
    width, cols = w_full.shape
    m = n_src * CAP
    return pl.pallas_call(
        lambda *refs: part_kernel(gu_cols, *refs),
        grid=(width // depth,),
        in_specs=[pl.BlockSpec((depth, cols), lambda k: (k, 0)), *row_specs(first, rest)],
        out_specs=pl.BlockSpec((m, cols), lambda k: (0, 0)),
        out_shape=jax.ShapeDtypeStruct((m, cols), jnp.bfloat16),
        scratch_shapes=[pltpu.VMEM((m, gu_cols), jnp.float32), pltpu.VMEM((m, cols - gu_cols), jnp.float32)],
        name="partial_products",
    )(w_full, first, rest)


def pgu_kernel(dgu_ref, first_ref, rest_ref, pgu_ref):
    def product(rows_ref):
        n_src, _, depth = rows_ref.shape
        x = rows_ref[:, :CAP, :].reshape(n_src * CAP, depth)
        pgu_ref[...] = f32_dot(x, dgu_ref[...], ((0,), (0,))).astype(pgu_ref.dtype)

    pl.when(pl.program_id(0) == 0)(lambda: product(first_ref))
    pl.when(pl.program_id(0) > 0)(lambda: product(rest_ref))


def weight_products(dgu, first, rest):
    depth = first.shape[2]
    width = depth + rest.shape[2]
    m, cols = dgu.shape
    return pl.pallas_call(
        pgu_kernel,
        grid=(width // depth,),
        in_specs=[pl.BlockSpec((m, cols), lambda k: (0, 0)), *row_specs(first, rest)],
        out_specs=pl.BlockSpec((depth, cols), lambda k: (k, 0)),
        out_shape=jax.ShapeDtypeStruct((width, cols), jnp.bfloat16),
        name="weight_products",
    )(dgu, first, rest)


def dx_kernel(dgu_ref, w_ref, dx_ref):
    gu_cols = dgu_ref.shape[1]
    dx_ref[...] = f32_dot(dgu_ref[...], w_ref[:, :gu_cols], ((1,), (1,))).astype(dx_ref.dtype)


def input_products(dgu, w_full, depth=512):
    m, cols = dgu.shape
    width, all_cols = w_full.shape
    return pl.pallas_call(
        dx_kernel,
        grid=(width // depth,),
        in_specs=[pl.BlockSpec((m, cols), lambda k: (0, 0)), pl.BlockSpec((depth, all_cols), lambda k: (k, 0))],
        out_specs=pl.BlockSpec((m, depth), lambda k: (0, k)),
        out_shape=jax.ShapeDtypeStruct((m, width), jnp.bfloat16),
        name="input_products",
    )(dgu, w_full)


def on_device(tokens, output_gradient, slot, gate_weight, gate_up_weight, down_weight):
    n_win = slot.shape[1]
    width = tokens.shape[1]
    n_half = width // (2 * LANE)
    hid = down_weight.shape[1]
    n_yl, n_zh = lax.axis_size("yl"), lax.axis_size("zh")

    n_zl = lax.axis_size("zl")
    n_xc = n_half // n_zl
    positions = jnp.arange(CAP, dtype=jnp.int32)
    selector = jnp.transpose(slot)[:, None, :] == positions[None, :, None]
    picked = selector.astype(jnp.bfloat16)
    rows_x = jnp.einsum("ect,td->ecd", picked, tokens, preferred_element_type=jnp.float32).astype(jnp.bfloat16)
    rows_dy = jnp.einsum("ect,td->ecd", picked, output_gradient, preferred_element_type=jnp.float32)
    gate = jnp.sum(jnp.where(selector, jnp.transpose(gate_weight)[:, None, :], 0.0), axis=2)
    rows_g = (rows_dy * gate[..., None]).astype(jnp.bfloat16)
    rows = jnp.concatenate([rows_x, rows_g], axis=1).reshape(n_win, 2 * CAP, n_zl, n_xc, n_yl, LANE)
    rows = jnp.transpose(rows, (0, 4, 1, 3, 2, 5)).reshape(n_win, n_yl, 1, 2 * CAP, n_half * LANE)
    rows = jnp.broadcast_to(rows, (n_win, n_yl, n_zh, 2 * CAP, n_half * LANE))
    rows = rows.reshape(-1, 2 * CAP, n_half * LANE)
    cut = n_half * LANE // 4
    first = a2a(rows[:, :, :cut], EXPERT)

    zl, yl = lax.axis_index("zl"), lax.axis_index("yl")
    w_own = jnp.concatenate([gate_up_weight[0], jnp.transpose(down_weight[0])], axis=1)
    kept = lax.dynamic_slice_in_dim(w_own, yl * LANE, LANE, axis=0)
    given = lax.dynamic_slice_in_dim(w_own, (1 - yl) * LANE, LANE, axis=0)
    w_got = [kept, swap(given, 1), swap(kept, 2), swap(given, 3)]

    def w_of(zl_src, yl_src):
        same_zl, same_yl = zl == zl_src, yl == yl_src
        return jnp.where(same_zl, jnp.where(same_yl, w_got[0], w_got[1]), jnp.where(same_yl, w_got[2], w_got[3]))

    w_rows = []
    for zl_src in range(n_zl):
        w0, w1 = w_of(zl_src, 0), w_of(zl_src, 1)
        w_rows.append(jnp.concatenate([w0[:, : 2 * hid], w1[:, : 2 * hid], w0[:, 2 * hid :], w1[:, 2 * hid :]], axis=1))
    w_mine = jnp.concatenate(w_rows, axis=0)
    first, rows_rest, w_mine = lax.optimization_barrier((first, rows[:, :, cut:], w_mine))
    w_full = lax.all_gather(w_mine, ("x", "c"), axis=0, tiled=True)
    gu_cols = 2 * n_yl * hid
    rest = a2a(rows_rest, EXPERT)
    n_src = first.shape[0]

    part = partial_products(w_full, first, rest, gu_cols)
    total = part.astype(jnp.float32) + swap(part, 1).astype(jnp.float32)
    dgu = []
    for i in range(n_yl):
        pre, up = total[:, 2 * i * hid : (2 * i + 1) * hid], total[:, (2 * i + 1) * hid : (2 * i + 2) * hid]
        dh = total[:, gu_cols + i * hid : gu_cols + (i + 1) * hid]
        sig = jax.nn.sigmoid(pre)
        dgu += [dh * up * sig * (1.0 + pre * (1.0 - sig)), dh * (pre * sig)]
    dgu = jnp.concatenate(dgu, axis=1).astype(jnp.bfloat16)

    pgu = weight_products(dgu, first, rest)
    dx = input_products(dgu, w_full)

    summed = lax.psum_scatter(pgu, ("x", "c"), scatter_dimension=0, tiled=True)
    summed = jnp.transpose(summed.reshape(n_zl, LANE, n_yl, 2 * hid), (0, 2, 1, 3))
    summed = a2a(summed.reshape(n_zl * n_yl, LANE, 2 * hid), ("zl", "yl"))
    grad_gu = jnp.sum(summed.reshape(n_zl, n_yl * LANE, 2 * hid).astype(jnp.float32), axis=0)
    grad_gu = grad_gu.astype(jnp.bfloat16)[None]

    back = a2a(dx.reshape(n_src, CAP, n_half * LANE), EXPERT)
    back = jnp.sum(back.reshape(n_win, n_yl, n_zh, CAP, n_xc, n_zl, LANE).astype(jnp.float32), axis=2)
    back = jnp.transpose(back, (0, 2, 4, 3, 1, 5)).reshape(n_win, CAP, width)
    grad_tokens = jnp.einsum("ect,ecd->td", selector.astype(jnp.float32), back).astype(jnp.bfloat16)
    return grad_tokens, grad_gu


def solution(mesh):
    fine = Mesh(mesh.devices.reshape(2, 4, 2, 4, 2, 4), FINE)
    dp, ex = FINE[:3], FINE[3:]
    in_specs = (P(FINE, None), P(FINE, None), P(FINE, None), P(FINE, None), P(ex, dp, None), P(ex, None, dp))
    out_specs = (P(FINE, None), P(ex, dp, None))
    return jax.shard_map(on_device, mesh=fine, in_specs=in_specs, out_specs=out_specs, check_vma=False)
```

time: 175 us -> 193 us (1.10)
  blocking collectives: 78.1 us -> 50.4 us
  starting transfers between devices: 20.4 us -> 42.4 us
  Pallas kernels: 0 us -> 15.5 us
  waiting for transfers between devices: 38.4 us -> 49.5 us
  matrix products: 13.6 us -> 2.67 us
  other arithmetic: 2.37 us -> 7.86 us
  local copies, waits for them, and re-layouts: 7.05 us -> 8.99 us
    all_to_all x2 -> x1, blocking collectives: 78.1 us -> 50.4 us  [a2a(): return lax.all_to_all(v, axes, split_axis=0, concat_axis=0, tiled=True)]
    pallas_call x0 -> x3, Pallas kernels: none -> 15.5 us  [the longest x1 5.55 us: partial_products(): pl.pallas_call(lambda *refs: part_kernel(gu_cols, *refs), grid=(width //...]
    all_to_all x2 -> x3, starting transfers between devices: 16 us -> 28.5 us  [a2a(): return lax.all_to_all(v, axes, split_axis=0, concat_axis=0, tiled=True)]
    dot_general x4 -> x0, matrix products: 11.6 us -> none  [f32_dot(): lax.dot_general(a, b, (dims, ((), ())), preferred_element_type=jnp.float32)]
    ppermute x1 -> x4, waiting for transfers between devices: 9.1 us -> 20 us  [swap(): return lax.ppermute(v, ('zl', 'yl'), [(i, i ^ flip) for i in range(4)])]
    ppermute x1 -> x4, starting transfers between devices: 4.26 us -> 13.9 us  [swap(): return lax.ppermute(v, ('zl', 'yl'), [(i, i ^ flip) for i in range(4)])]
    concatenate x1 -> x3, other arithmetic: 0.05 us -> 3.41 us  [the longest x1 1.65 us: on_device(): jnp.concatenate([gate_up_weight[0], jnp.transpose(down_weight[0])], axis=1)]
    slice x0 -> x10, local copies, waits for them, and re-layouts: none -> 2.2 us  [the longest x1 1.28 us: on_device(): rows[:, :, cut:]]
  transfers between devices with their start and end apart: 5 -> 9, of which waited for: 4 -> 7; matrix products, arithmetic and copies ran while one was open for 6% -> 5% of each run, Pallas kernels for 0% -> 3%
where the time goes in v3:
time: 193 us; the launch traced here: 192 us
  blocking collectives  50.4 us (26%)
  waiting for transfers between devices  49.5 us (26%)
  starting transfers between devices  42.4 us (22%)
  Pallas kernels  15.5 us (8%)
  between operations  14.3 us (7%)
  local copies, waits for them, and re-layouts  8.99 us (5%)
  other arithmetic  7.86 us (4%)
  matrix products  2.67 us (1%)
    all_to_all x1, blocking collectives, a2a(): return lax.all_to_all(v, axes, split_axis=0, concat_axis=0, tiled=True)  50.4 us
    all_to_all x3, starting transfers between devices, a2a(): return lax.all_to_all(v, axes, split_axis=0, concat_axis=0, tiled=True)  28.5 us
    reduce_scatter x1, waiting for transfers between devices, on_device(): summed = lax.psum_scatter(pgu, ('x', 'c'), scatter_dimension=0, tiled=True)  23 us
    ppermute x4, waiting for transfers between devices, swap(): return lax.ppermute(v, ('zl', 'yl'), [(i, i ^ flip) for i in range(4)])  20 us
    ppermute x4, starting transfers between devices, swap(): return lax.ppermute(v, ('zl', 'yl'), [(i, i ^ flip) for i in range(4)])  13.9 us
    all_to_all x3, waiting for transfers between devices, a2a(): return lax.all_to_all(v, axes, split_axis=0, concat_axis=0, tiled=True)  6.47 us
    pallas_call x1, Pallas kernels, partial_products(): pl.pallas_call(lambda *refs: part_kernel(gu_cols, *refs), grid=(width //...  5.55 us
    pallas_call x1, Pallas kernels, weight_products(): pl.pallas_call(pgu_kernel, grid=(width // depth,), in_specs=[pl.BlockSpec...  5.04 us
  transfers between devices with their start and end apart: 9, of which 7 were waited for; matrix products, arithmetic and copies ran while one was open for 5% of the time, Pallas kernels for 3%

profile of v3, /device:TPU:6, one launch (start us, length us, event | category | flops | bytes accessed | tf_op | source)
XLA Modules:
  0.0 191.8 jit_solution(8335687956747368288)
XLA Ops:
  10.5 1.2 broadcast_in_dim.28
  11.7 1.3 broadcast_in_dim.29
  13.9 16.1 %all-to-all-start = ((bf16[32,16,512]{2,1,0:T(8,128)(2,1)}), bf16[32,16,512]{2,1,0:T(8,128)(2,1)}, u32[]{:S(2)}, u32[]{:S(2)}) async-start(bf16[32,16,512]{2,1,0:T(8,128)(2,1)} %slice.64), calls=%async_computation | async-start | bytes 1048576 | tf_op jit(solution)/shard_map/all_to_all | solution.py:19
  30.1 1.7 fusion.10
  31.8 3.6 %collective-permute-start = (bf16[128,576]{1,0:T(8,128)(2,1)}, bf16[128,576]{1,0:T(8,128)(2,1)S(1)}, u32[]{:S(2)}, u32[]{:S(2)}) collective-permute-start(bf16[128,576]{1,0:T(8,128)(2,1)} %get-tuple-element.16), channel_id=1, source_target_pairs={{0,4},{4,0},{256,260},{260,256},{1,5},{5,1},{257,261},{261,257},{2... | collective-permute-start | bytes 442376 | tf_op jit(solution)/shard_map/ppermute | solution.py:23
  35.4 3.1 %collective-permute-start.2 = (bf16[128,576]{1,0:T(8,128)(2,1)}, bf16[128,576]{1,0:T(8,128)(2,1)}, u32[]{:S(2)}, u32[]{:S(2)}) collective-permute-start(bf16[128,576]{1,0:T(8,128)(2,1)} %get-tuple-element.16), channel_id=1, source_target_pairs={{0,260},{4,256},{256,4},{260,0},{1,261},{5,257},{257,5},{261,1},{2... | collective-permute-start | bytes 442376 | tf_op jit(solution)/shard_map/ppermute | solution.py:23
  38.5 2.5 %collective-permute-start.1 = (bf16[128,576]{1,0:T(8,128)(2,1)S(1)}, bf16[128,576]{1,0:T(8,128)(2,1)}, u32[]{:S(2)}, u32[]{:S(2)}) collective-permute-start(bf16[128,576]{1,0:T(8,128)(2,1)S(1)} %get-tuple-element.17), channel_id=1, source_target_pairs={{0,256},{4,260},{256,0},{260,4},{1,257},{5,261},{257,1},{261,5},{2... | collective-permute-start | bytes 442376 | tf_op jit(solution)/shard_map/ppermute | solution.py:23
  41.0 1.3 slice.65
  42.3 5.5 %collective-permute-done = bf16[128,576]{1,0:T(8,128)(2,1)S(1)} collective-permute-done((bf16[128,576]{1,0:T(8,128)(2,1)}, bf16[128,576]{1,0:T(8,128)(2,1)S(1)}, u32[]{:S(2)}, u32[]{:S(2)}) %collective-permute-start) | collective-permute-done | bytes 147488 | tf_op jit(solution)/shard_map/ppermute | solution.py:23
  47.8 3.4 %collective-permute-done.2 = bf16[128,576]{1,0:T(8,128)(2,1)} collective-permute-done((bf16[128,576]{1,0:T(8,128)(2,1)}, bf16[128,576]{1,0:T(8,128)(2,1)}, u32[]{:S(2)}, u32[]{:S(2)}) %collective-permute-start.2) | collective-permute-done | bytes 147488 | tf_op jit(solution)/shard_map/ppermute | solution.py:23
  55.0 50.4 %all_to_all.20.refs_2_.rest_ref = bf16[32,16,1536]{2,1,0:T(8,128)(2,1)} all-to-all(bf16[32,16,1536]{2,1,0:T(8,128)(2,1)S(1)} %copy-done.1), channel_id=1, replica_groups=mesh['zl'=2,'x'=4,'c'=2,'yh'=4,'yl'=2,'zh'=4] {'yh','yl','zh'}, dimensions={0} | all-to-all | bytes 3145728 | tf_op jit(solution)/shard_map/all_to_all | solution.py:19
  105.4 5.5 %partial_products.1 = bf16[256,1152]{1,0:T(8,128)(2,1)} custom-call(bf16[2048,1152]{1,0:T(8,128)(2,1)} %all-gather.2.cloned.1.call-done.refs_0_.w_ref, bf16[32,16,512]{2,1,0:T(8,128)(2,1)} %all-to-all-done.refs_1_.first_ref, bf16[32,16,1536]{2,1,0:T(8,128)(2,1)} %all_to_all.20.refs_2_.rest_ref), custom_call_target="tpu_custom_call" | custom-call | tf_op jit(solution)/shard_map/partial_products/pallas_call | solution.py:64
  111.0 4.7 %collective-permute-start.3 = (bf16[256,1152]{1,0:T(8,128)(2,1)}, bf16[256,1152]{1,0:T(8,128)(2,1)S(1)}, u32[]{:S(2)}, u32[]{:S(2)}) collective-permute-start(bf16[256,1152]{1,0:T(8,128)(2,1)} %partial_products.1), channel_id=1, source_target_pairs={{0,4},{4,0},{256,260},{260,256},{1,5},{5,1},{257,261},{261,257},{2... | collective-permute-start | bytes 1769480 | tf_op jit(solution)/shard_map/ppermute | solution.py:23
  115.6 10.3 %collective-permute-done.3 = bf16[256,1152]{1,0:T(8,128)(2,1)S(1)} collective-permute-done((bf16[256,1152]{1,0:T(8,128)(2,1)}, bf16[256,1152]{1,0:T(8,128)(2,1)S(1)}, u32[]{:S(2)}, u32[]{:S(2)}) %collective-permute-start.3) | collective-permute-done | bytes 589856 | tf_op jit(solution)/shard_map/ppermute | solution.py:23
  125.9 1.2 convert_add_fusion
  128.3 5.0 %weight_products.1 = bf16[2048,768]{1,0:T(8,128)(2,1)} custom-call(bf16[256,768]{1,0:T(8,128)(2,1)} %pad_maximum_fusion.2.dgu_ref, bf16[32,16,512]{2,1,0:T(8,128)(2,1)} %all-to-all-done.refs_1_.first_ref, bf16[32,16,1536]{2,1,0:T(8,128)(2,1)} %all_to_all.20.refs_2_.rest_ref), custom_call_target="tpu_custom_call" | custom-call | tf_op jit(solution)/shard_map/weight_products/pallas_call | solution.py:89
  133.4 4.9 %input_products.1 = bf16[256,2048]{1,0:T(8,128)(2,1)} custom-call(bf16[256,768]{1,0:T(8,128)(2,1)} %pad_maximum_fusion.2.dgu_ref, bf16[2048,1152]{1,0:T(8,128)(2,1)} %all-gather.2.cloned.1.call-done.refs_0_.w_ref), custom_call_target="tpu_custom_call" | custom-call | tf_op jit(solution)/shard_map/input_products/pallas_call | solution.py:107
  138.3 7.3 %all-to-all-start.2 = ((bf16[32,8,2048]{2,1,0:T(8,128)(2,1)}), bf16[32,8,2048]{2,1,0:T(8,128)(2,1)S(1)}, u32[]{:S(2)}, u32[]{:S(2)}) async-start(bf16[32,8,2048]{2,1,0:T(8,128)(2,1)} %bitcast.35), calls=%async_computation.2 | async-start | bytes 2097152 | tf_op jit(solution)/shard_map/all_to_all | solution.py:19
  145.6 23.0 %reduce-scatter.2.cloned.1.call-done = bf16[256,768]{1,0:T(8,128)(2,1)} async-done(((bf16[2048,768]{1,0:T(8,128)(2,1)}), bf16[256,768]{1,0:T(8,128)(2,1)}) %reduce-scatter.2.cloned.1.call-update) | async-done | bytes 393232 | tf_op jit(solution)/shard_map/reduce_scatter | solution.py:174
  168.7 1.1 reshape.37
  170.5 2.7 %all-to-all-done.2 = bf16[32,8,2048]{2,1,0:T(8,128)(2,1)S(1)} async-done(((bf16[32,8,2048]{2,1,0:T(8,128)(2,1)}), bf16[32,8,2048]{2,1,0:T(8,128)(2,1)S(1)}, u32[]{:S(2)}, u32[]{:S(2)}) %all-to-all-start.2) | async-done | bytes 1048608 | tf_op jit(solution)/shard_map/all_to_all | solution.py:19
  173.2 5.1 %all-to-all-start.3 = ((bf16[4,128,384]{2,1,0:T(8,128)(2,1)}), bf16[4,128,384]{2,1,0:T(8,128)(2,1)S(1)}, u32[]{:S(2)}, u32[]{:S(2)}) async-start(bf16[4,128,384]{2,1,0:T(8,128)(2,1)} %bitcast.14), calls=%async_computation.4 | async-start | bytes 786432 | tf_op jit(solution)/shard_map/all_to_all | solution.py:19
  178.9 1.5 fusion
  180.4 3.8 %all-to-all-done.3 = bf16[4,128,384]{2,1,0:T(8,128)(2,1)S(1)} async-done(((bf16[4,128,384]{2,1,0:T(8,128)(2,1)}), bf16[4,128,384]{2,1,0:T(8,128)(2,1)S(1)}, u32[]{:S(2)}, u32[]{:S(2)}) %all-to-all-start.3) | async-done | bytes 393248 | tf_op jit(solution)/shard_map/all_to_all | solution.py:19
  (44 shorter events, 11.4 us)
Async XLA Ops:
  7.2 1.3 copy-start
  7.2 2.2 %copy-start.4 = (s32[128,4]{0,1:T(4,128)S(1)}, s32[128,4]{0,1:T(4,128)}, u32[]{:S(2)}) copy-start(s32[128,4]{0,1:T(4,128)} %param.8) | copy-start | bytes 6148
  7.2 2.2 %copy-start.2 = (bf16[128,4096]{1,0:T(8,128)(2,1)S(1)}, bf16[128,4096]{1,0:T(8,128)(2,1)}, u32[]{:S(2)}) copy-start(bf16[128,4096]{1,0:T(8,128)(2,1)} %param.7) | copy-start | bytes 3145732
  13.0 17.0 %copy-start.3 = (bf16[1,192,256]{2,1,0:T(8,128)(2,1)S(1)}, bf16[1,192,256]{2,1,0:T(8,128)(2,1)}, u32[]{:S(2)}) copy-start(bf16[1,192,256]{2,1,0:T(8,128)(2,1)} %param.11) | copy-start | bytes 294916
  13.9 40.5 %all-to-all-start = ((bf16[32,16,512]{2,1,0:T(8,128)(2,1)}), bf16[32,16,512]{2,1,0:T(8,128)(2,1)}, u32[]{:S(2)}, u32[]{:S(2)}) async-start(bf16[32,16,512]{2,1,0:T(8,128)(2,1)} %slice.64), calls=%async_computation | async-start | bytes 1048576 | tf_op jit(solution)/shard_map/all_to_all | solution.py:19
  29.9 75.5 %all-gather.2.cloned.1.call-start = ((), (), s32[]{:S(2)}) async-start(), calls=%async_computation.5 | async-start | bytes 5308416 | tf_op jit(solution)/shard_map/all_gather | solution.py:156
  31.8 16.0 %collective-permute-start = (bf16[128,576]{1,0:T(8,128)(2,1)}, bf16[128,576]{1,0:T(8,128)(2,1)S(1)}, u32[]{:S(2)}, u32[]{:S(2)}) collective-permute-start(bf16[128,576]{1,0:T(8,128)(2,1)} %get-tuple-element.16), channel_id=1, source_target_pairs={{0,4},{4,0},{256,260},{260,256},{1,5},{5,1},{257,261},{261,257},{2... | collective-permute-start | bytes 442376 | tf_op jit(solution)/shard_map/ppermute | solution.py:23
  35.4 15.8 %collective-permute-start.2 = (bf16[128,576]{1,0:T(8,128)(2,1)}, bf16[128,576]{1,0:T(8,128)(2,1)}, u32[]{:S(2)}, u32[]{:S(2)}) collective-permute-start(bf16[128,576]{1,0:T(8,128)(2,1)} %get-tuple-element.16), channel_id=1, source_target_pairs={{0,260},{4,256},{256,4},{260,0},{1,261},{5,257},{257,5},{261,1},{2... | collective-permute-start | bytes 442376 | tf_op jit(solution)/shard_map/ppermute | solution.py:23
  38.5 13.5 %collective-permute-start.1 = (bf16[128,576]{1,0:T(8,128)(2,1)S(1)}, bf16[128,576]{1,0:T(8,128)(2,1)}, u32[]{:S(2)}, u32[]{:S(2)}) collective-permute-start(bf16[128,576]{1,0:T(8,128)(2,1)S(1)} %get-tuple-element.17), channel_id=1, source_target_pairs={{0,256},{4,260},{256,0},{260,4},{1,257},{5,261},{257,1},{261,5},{2... | collective-permute-start | bytes 442376 | tf_op jit(solution)/shard_map/ppermute | solution.py:23
  53.4 1.6 copy-start.1
  54.4 114.3 %reduce-scatter.2.cloned.1.call-start = ((), (), s32[]{:S(2)}) async-start(), calls=%async_computation.6 | async-start | bytes 3538944 | tf_op jit(solution)/shard_map/reduce_scatter | solution.py:174
  111.0 14.9 %collective-permute-start.3 = (bf16[256,1152]{1,0:T(8,128)(2,1)}, bf16[256,1152]{1,0:T(8,128)(2,1)S(1)}, u32[]{:S(2)}, u32[]{:S(2)}) collective-permute-start(bf16[256,1152]{1,0:T(8,128)(2,1)} %partial_products.1), channel_id=1, source_target_pairs={{0,4},{4,0},{256,260},{260,256},{1,5},{5,1},{257,261},{261,257},{2... | collective-permute-start | bytes 1769480 | tf_op jit(solution)/shard_map/ppermute | solution.py:23
  138.3 34.9 %all-to-all-start.2 = ((bf16[32,8,2048]{2,1,0:T(8,128)(2,1)}), bf16[32,8,2048]{2,1,0:T(8,128)(2,1)S(1)}, u32[]{:S(2)}, u32[]{:S(2)}) async-start(bf16[32,8,2048]{2,1,0:T(8,128)(2,1)} %bitcast.35), calls=%async_computation.2 | async-start | bytes 2097152 | tf_op jit(solution)/shard_map/all_to_all | solution.py:19
  173.2 11.0 %all-to-all-start.3 = ((bf16[4,128,384]{2,1,0:T(8,128)(2,1)}), bf16[4,128,384]{2,1,0:T(8,128)(2,1)S(1)}, u32[]{:S(2)}, u32[]{:S(2)}) async-start(bf16[4,128,384]{2,1,0:T(8,128)(2,1)} %bitcast.14), calls=%async_computation.4 | async-start | bytes 786432 | tf_op jit(solution)/shard_map/all_to_all | solution.py:19
Sparse Core Ops, SparseCore 0:
  54.5 36.4 all-gather.1
  133.5 35.0 reduce-scatter.1

commit v4 on v2

--- a/solution.py
+++ b/solution.py
@@ -1,6 +1,8 @@
 import jax
 import jax.numpy as jnp
 from jax import lax
+from jax.experimental import pallas as pl
+from jax.experimental.pallas import tpu as pltpu
 from jax.sharding import Mesh, PartitionSpec as P
 
 FINE = ("zl", "x", "c", "yh", "yl", "zh")
@@ -17,8 +19,66 @@
     return lax.all_to_all(v, axes, split_axis=0, concat_axis=0, tiled=True)
 
 
-def swap_pairs(v, axis):
+def swap(v, axis):
     return lax.ppermute(v, axis, [(0, 1), (1, 0)])
+
+
+def split_kernel(core_ref, rows_ref, kept_ref, given_ref):
+    n_src, _, depth = rows_ref.shape
+    x = rows_ref[:, :CAP, :].reshape(n_src * CAP, depth)
+    low, high = x[:, : depth // 2].T, x[:, depth // 2 :].T
+
+    @pl.when(core_ref[0] == 0)
+    def _():
+        kept_ref[...], given_ref[...] = low, high
+
+    @pl.when(core_ref[0] != 0)
+    def _():
+        kept_ref[...], given_ref[...] = high, low
+
+
+def split_rows(core, recv, depth):
+    n_src, rows, width = recv.shape
+    out = jax.ShapeDtypeStruct((width // 2, n_src * CAP), recv.dtype)
+    out_spec = pl.BlockSpec((depth // 2, n_src * CAP), lambda k: (k, 0))
+    return pl.pallas_call(
+        split_kernel,
+        grid=(width // depth,),
+        in_specs=[
+            pl.BlockSpec(memory_space=pltpu.SMEM),
+            pl.BlockSpec((n_src, rows, depth), lambda k: (0, 0, k)),
+        ],
+        out_specs=[out_spec, out_spec],
+        out_shape=[out, out],
+        name="split_rows",
+    )(core.reshape(1), recv)
+
+
+def pgu_kernel(xa_ref, xb_ref, dgu_a_ref, dgu_b_ref, pgu_ref):
+    acc = jnp.dot(xa_ref[...], dgu_a_ref[...], preferred_element_type=jnp.float32)
+    acc += jnp.dot(xb_ref[...], dgu_b_ref[...], preferred_element_type=jnp.float32)
+    n_zl, n_yl, lanes, cols = pgu_ref.shape
+    for i in range(n_zl):
+        for j in range(n_yl):
+            block = acc[i * lanes : (i + 1) * lanes, j * cols : (j + 1) * cols]
+            pgu_ref[i, j] = block.astype(pgu_ref.dtype)
+
+
+def weight_products(xt_a, xt_b, dgu_a, dgu_b, n_zl, n_yl):
+    width, m = xt_a.shape
+    cols = dgu_a.shape[1] // n_yl
+    x_spec = pl.BlockSpec((n_zl * LANE, m), lambda k: (k, 0))
+    dgu_spec = pl.BlockSpec(dgu_a.shape, lambda k: (0, 0))
+    n_x = width // (n_zl * LANE)
+    out = pl.pallas_call(
+        pgu_kernel,
+        grid=(n_x,),
+        in_specs=[x_spec, x_spec, dgu_spec, dgu_spec],
+        out_specs=pl.BlockSpec((None, n_zl, n_yl, LANE, cols), lambda k: (k, 0, 0, 0, 0)),
+        out_shape=jax.ShapeDtypeStruct((n_x, n_zl, n_yl, LANE, cols), jnp.bfloat16),
+        name="weight_products",
+    )(xt_a, xt_b, dgu_a, dgu_b)
+    return out.reshape(-1, cols)
 
 
 def on_device(tokens, output_gradient, slot, gate_weight, gate_up_weight, down_weight):
@@ -26,14 +86,16 @@
     width = tokens.shape[1]
     n_half = width // (2 * LANE)
     hid = down_weight.shape[1]
-    n_yl, n_zh = lax.axis_size("yl"), lax.axis_size("zh")
+    n_yl, n_zh, n_c = lax.axis_size("yl"), lax.axis_size("zh"), lax.axis_size("c")
 
     n_zl = lax.axis_size("zl")
     w_own = jnp.concatenate([gate_up_weight[0], jnp.transpose(down_weight[0])], axis=1)
     w_sent = jnp.broadcast_to(w_own.reshape(1, n_yl, LANE, 3 * hid), (n_zl, n_yl, LANE, 3 * hid))
     w_pair = a2a(w_sent.reshape(n_zl * n_yl, LANE, 3 * hid), ("zl", "yl"))
-    w_mine = jnp.transpose(w_pair.reshape(n_zl, n_yl, LANE, 3, hid), (0, 2, 3, 1, 4))
-    w_full = lax.all_gather(w_mine.reshape(n_zl * LANE, 3 * n_yl * hid), ("x", "c"), axis=0, tiled=True)
+    w_pair = w_pair.reshape(n_zl, n_yl, LANE, 3 * hid)
+    w_mine = [w_pair[:, i, :, : 2 * hid] for i in range(n_yl)] + [w_pair[:, i, :, 2 * hid :] for i in range(n_yl)]
+    w_mine = jnp.concatenate(w_mine, axis=2).reshape(n_zl * LANE, 3 * n_yl * hid)
+    w_full = lax.all_gather(w_mine, ("x", "c"), axis=0, tiled=True)
     gu_cols = 2 * n_yl * hid
     w_gu, w_down = w_full[:, :gu_cols], w_full[:, gu_cols:]
 
@@ -56,18 +118,24 @@
     part = jnp.concatenate(
         [f32_dot(x_mat, w_gu, ((1,), (0,))), f32_dot(g_mat, w_down, ((1,), (0,)))], axis=1
     ).astype(jnp.bfloat16)
-    total = part.astype(jnp.float32) + swap_pairs(part, "yl").astype(jnp.float32)
-    pre, up, dh = jnp.split(total, 3, axis=1)
-    sig = jax.nn.sigmoid(pre)
-    dgate = dh * up * sig * (1.0 + pre * (1.0 - sig))
-    dup = dh * (pre * sig)
-    dgu = jnp.concatenate([dgate, dup], axis=1).astype(jnp.bfloat16)
+
+    xt_kept, xt_given = split_rows(lax.axis_index("c"), recv, n_c * n_zl * LANE)
+    part_other, xt_kept, xt_got = lax.optimization_barrier((swap(part, "yl"), xt_kept, swap(xt_given, "c")))
+
+    total = part.astype(jnp.float32) + part_other.astype(jnp.float32)
+    dgu = []
+    for i in range(n_yl):
+        pre, up = total[:, 2 * i * hid : (2 * i + 1) * hid], total[:, (2 * i + 1) * hid : (2 * i + 2) * hid]
+        dh = total[:, gu_cols + i * hid : gu_cols + (i + 1) * hid]
+        sig = jax.nn.sigmoid(pre)
+        dgu += [dh * up * sig * (1.0 + pre * (1.0 - sig)), dh * (pre * sig)]
+    dgu = jnp.concatenate(dgu, axis=1).astype(jnp.bfloat16)
 
     dx = f32_dot(dgu, w_gu, ((1,), (1,))).astype(jnp.bfloat16)
-    pgu = f32_dot(x_mat, dgu, ((0,), (0,))).astype(jnp.bfloat16)
+    dx, dgu_other = lax.optimization_barrier((dx, swap(dgu, "c")))
+    pgu = weight_products(xt_kept, xt_got, dgu, dgu_other, n_zl, n_yl)
 
-    summed = lax.psum_scatter(pgu, ("x", "c"), scatter_dimension=0, tiled=True)
-    summed = jnp.transpose(summed.reshape(n_zl, LANE, 2, n_yl, hid), (0, 3, 1, 2, 4))
+    summed = lax.psum_scatter(pgu, "x", scatter_dimension=0, tiled=True)
     summed = a2a(summed.reshape(n_zl * n_yl, LANE, 2 * hid), ("zl", "yl"))
     grad_gu = jnp.sum(summed.reshape(n_zl, n_yl * LANE, 2 * hid).astype(jnp.float32), axis=0)
     grad_gu = grad_gu.astype(jnp.bfloat16)[None]

time: 175 us -> 180 us (1.029)
  blocking collectives: 78.1 us -> 117 us
  waiting for transfers between devices: 38.4 us -> 8.01 us
  Pallas kernels: 0 us -> 8.32 us
  starting transfers between devices: 20.4 us -> 14.4 us
  matrix products: 13.6 us -> 8.83 us
    all_to_all x2 -> x3, blocking collectives: 78.1 us -> 117 us  [a2a(): return lax.all_to_all(v, axes, split_axis=0, concat_axis=0, tiled=True)]
    reduce_scatter x1, waiting for transfers between devices: 24.8 us -> 0.01 us  [on_device(): summed = lax.psum_scatter(pgu, 'x', scatter_dimension=0, tiled=True)]
    all_to_all x2 -> x1, starting transfers between devices: 16 us -> 5.7 us  [a2a(): return lax.all_to_all(v, axes, split_axis=0, concat_axis=0, tiled=True)]
    pallas_call x0 -> x2, Pallas kernels: none -> 8.32 us  [the longest x1 4.5 us: weight_products(): pl.pallas_call(pgu_kernel, grid=(n_x,), in_specs=[x_spec, x_spec, dgu_spe...]
    ppermute x1 -> x3, waiting for transfers between devices: 9.1 us -> 4.16 us  [swap(): return lax.ppermute(v, axis, [(0, 1), (1, 0)])]
    dot_general x4 -> x3, matrix products: 11.6 us -> 6.85 us  [f32_dot(): lax.dot_general(a, b, (dims, ((), ())), preferred_element_type=jnp.float32)]
    ppermute x1 -> x3, starting transfers between devices: 4.26 us -> 8.64 us  [swap(): return lax.ppermute(v, axis, [(0, 1), (1, 0)])]
    all_to_all x2 -> x1, waiting for transfers between devices: 4.47 us -> 3.81 us  [a2a(): return lax.all_to_all(v, axes, split_axis=0, concat_axis=0, tiled=True)]
  transfers between devices with their start and end apart: 5 -> 6, of which waited for: 4 -> 4; matrix products, arithmetic and copies ran while one was open for 6% -> 3% of each run, Pallas kernels for 0% -> 2%
where the time goes in v4:
time: 180 us
  blocking collectives  117 us (65%)
  starting transfers between devices  14.4 us (8%)
  between operations  14.3 us (8%)
  matrix products  8.83 us (5%)
  Pallas kernels  8.32 us (5%)
  waiting for transfers between devices  8.01 us (4%)
  local copies, waits for them, and re-layouts  5.68 us (3%)
  other arithmetic  3.48 us (2%)
    all_to_all x3, blocking collectives, a2a(): return lax.all_to_all(v, axes, split_axis=0, concat_axis=0, tiled=True)  117 us
    ppermute x3, starting transfers between devices, swap(): return lax.ppermute(v, axis, [(0, 1), (1, 0)])  8.64 us
    dot_general x3, matrix products, f32_dot(): lax.dot_general(a, b, (dims, ((), ())), preferred_element_type=jnp.float32)  6.85 us
    all_to_all x1, starting transfers between devices, a2a(): return lax.all_to_all(v, axes, split_axis=0, concat_axis=0, tiled=True)  5.7 us
    pallas_call x1, Pallas kernels, weight_products(): pl.pallas_call(pgu_kernel, grid=(n_x,), in_specs=[x_spec, x_spec, dgu_spe...  4.5 us
    ppermute x3, waiting for transfers between devices, swap(): return lax.ppermute(v, axis, [(0, 1), (1, 0)])  4.16 us
    pallas_call x1, Pallas kernels, split_rows(): pl.pallas_call(split_kernel, grid=(width // depth,), in_specs=[pl.BlockSp...  3.83 us
    all_to_all x1, waiting for transfers between devices, a2a(): return lax.all_to_all(v, axes, split_axis=0, concat_axis=0, tiled=True)  3.81 us
  transfers between devices with their start and end apart: 6, of which 4 were waited for; matrix products, arithmetic and copies ran while one was open for 3% of the time, Pallas kernels for 2%

profile of v4, /device:TPU:6, one launch (start us, length us, event | category | flops | bytes accessed | tf_op | source)
XLA Modules:
  0.0 179.6 jit_solution(11389066446121464616)
XLA Ops:
  7.2 1.1 copy.32
  8.3 1.0 maximum_bitcast_fusion
  9.6 13.9 %all_to_all.20 = bf16[4,128,576]{1,2,0:T(8,128)(2,1)S(1)} all-to-all(bf16[4,128,576]{1,2,0:T(8,128)(2,1)S(1)} %bitcast.53), channel_id=1, replica_groups=mesh['zl'=2,'x'=4,'c'=2,'yh'=4,'yl'=2,'zh'=4] {'zl','yl'}, dimensions={0} | all-to-all | bytes 1179648 | tf_op jit(solution)/shard_map/all_to_all | solution.py:19
  24.1 1.0 concatenate.39
  26.3 0.4 copy.38
  27.3 64.2 %all_to_all.21.rows_ref = bf16[32,16,2048]{2,1,0:T(8,128)(2,1)S(1)} all-to-all(bf16[32,16,2048]{2,1,0:T(8,128)(2,1)S(1)} %bitcast.48), channel_id=1, replica_groups=mesh['zl'=2,'x'=4,'c'=2,'yh'=4,'yl'=2,'zh'=4] {'yh','yl','zh'}, dimensions={0} | all-to-all | bytes 4194304 | tf_op jit(solution)/shard_map/all_to_all | solution.py:19
  91.5 2.9 %fusion.14 = bf16[256,384]{1,0:T(8,128)(2,1)S(1)} fusion(bf16[2048,1152]{1,0:T(8,128)(2,1)} %all-gather.2.cloned.1.call-done, bf16[32,16,2048]{2,1,0:T(8,128)(2,1)S(1)} %all_to_all.21.rows_ref), kind=kOutput, calls=%fused_computation.15 | convolution fusion | flops 402751488 | bytes 2818048 | tf_op jit(solution)/shard_map/dot_general | solution.py:15
  94.4 2.9 %fusion.11 = bf16[256,768]{1,0:T(8,128)(2,1)S(1)} fusion(bf16[2048,1152]{1,0:T(8,128)(2,1)} %all-gather.2.cloned.1.call-done, bf16[32,16,2048]{2,1,0:T(8,128)(2,1)S(1)} %all_to_all.21.rows_ref), kind=kOutput, calls=%fused_computation.13 | convolution fusion | flops 805502976 | bytes 4587520 | tf_op jit(solution)/shard_map/dot_general | solution.py:15
  97.4 0.9 pad_maximum_fusion
  98.2 4.5 %collective-permute-start = (bf16[256,1152]{1,0:T(8,128)(2,1)}, bf16[256,1152]{1,0:T(8,128)(2,1)S(1)}, u32[]{:S(2)}, u32[]{:S(2)}) collective-permute-start(bf16[256,1152]{1,0:T(8,128)(2,1)} %pad_maximum_fusion), channel_id=1, source_target_pairs={{0,4},{4,0},{1,5},{5,1},{2,6},{6,2},{3,7},{7,3},{8,12},{12,8},{9,1... | collective-permute-start | bytes 1769480 | tf_op jit(solution)/shard_map/ppermute | solution.py:23
  102.8 3.8 %split_rows.1 = (bf16[1024,256]{1,0:T(8,128)(2,1)}, bf16[1024,256]{1,0:T(8,128)(2,1)}) custom-call(s32[1]{0:T(128)} %bitcast.19.core_ref, bf16[32,16,2048]{2,1,0:T(8,128)(2,1)} %copy-done.1), custom_call_target="tpu_custom_call" | custom-call | tf_op jit(solution)/shard_map/split_rows/pallas_call | solution.py:44
  106.6 1.9 %collective-permute-start.1 = (bf16[1024,256]{1,0:T(8,128)(2,1)}, bf16[1024,256]{1,0:T(8,128)(2,1)S(1)}, u32[]{:S(2)}, u32[]{:S(2)}) collective-permute-start(bf16[1024,256]{1,0:T(8,128)(2,1)} %get-tuple-element.10), channel_id=1, source_target_pairs={{0,32},{32,0},{1,33},{33,1},{2,34},{34,2},{3,35},{35,3},{4,36},{36... | collective-permute-start | bytes 1572872 | tf_op jit(solution)/shard_map/ppermute | solution.py:23
  108.5 2.1 %collective-permute-done.1.xb_ref = bf16[1024,256]{1,0:T(8,128)(2,1)S(1)} collective-permute-done((bf16[1024,256]{1,0:T(8,128)(2,1)}, bf16[1024,256]{1,0:T(8,128)(2,1)S(1)}, u32[]{:S(2)}, u32[]{:S(2)}) %collective-permute-start.1) | collective-permute-done | bytes 524320 | tf_op jit(solution)/shard_map/ppermute | solution.py:23
  110.6 1.4 collective-permute-done
  112.7 2.2 %collective-permute-start.2 = (bf16[256,768]{1,0:T(8,128)(2,1)S(1)}, bf16[256,768]{1,0:T(8,128)(2,1)S(1)}, u32[]{:S(2)}, u32[]{:S(2)}) collective-permute-start(bf16[256,768]{1,0:T(8,128)(2,1)S(1)} %pad_maximum_fusion.2.dgu_a_ref), channel_id=1, source_target_pairs={{0,32},{32,0},{1,33},{33,1},{2,34},{34,2},{3,35},{35,3},{4,36},{36... | collective-permute-start | bytes 1179656 | tf_op jit(solution)/shard_map/ppermute | solution.py:23
  114.9 1.0 fusion.6
  116.0 0.6 collective-permute-done.2.dgu_b_ref
  116.6 0.8 copy-done.7
  117.4 4.5 %weight_products.1 = bf16[4,2,2,128,384]{4,3,2,1,0:T(8,128)(2,1)} custom-call(bf16[1024,256]{1,0:T(8,128)(2,1)} %get-tuple-element.13.xa_ref, bf16[1024,256]{1,0:T(8,128)(2,1)} %copy-done.6, bf16[256,768]{1,0:T(8,128)(2,1)} %copy-done.2, bf16[256,768]{1,0:T(8,128)(2,1)} %copy-done.7), custom_call_target="tpu_custom_call" | custom-call | tf_op jit(solution)/shard_map/weight_products/pallas_call | solution.py:73
  121.9 38.5 %all_to_all.22 = bf16[32,8,2048]{2,1,0:T(8,128)(2,1)S(1)} all-to-all(bf16[32,8,2048]{2,1,0:T(8,128)(2,1)S(1)} %bitcast.57), channel_id=1, replica_groups=mesh['zl'=2,'x'=4,'c'=2,'yh'=4,'yl'=2,'zh'=4] {'yh','yl','zh'}, dimensions={0} | all-to-all | bytes 2097152 | tf_op jit(solution)/shard_map/all_to_all | solution.py:19
  160.4 5.7 %all-to-all-start.3 = ((bf16[4,128,384]{2,1,0:T(8,128)(2,1)}), bf16[4,128,384]{2,1,0:T(8,128)(2,1)S(1)}, u32[]{:S(2)}, u32[]{:S(2)}) async-start(bf16[4,128,384]{2,1,0:T(8,128)(2,1)} %bitcast.63), calls=%async_computation.4 | async-start | bytes 786432 | tf_op jit(solution)/shard_map/all_to_all | solution.py:19
  166.7 1.5 fusion
  168.2 3.8 %all-to-all-done.3 = bf16[4,128,384]{2,1,0:T(8,128)(2,1)S(1)} async-done(((bf16[4,128,384]{2,1,0:T(8,128)(2,1)}), bf16[4,128,384]{2,1,0:T(8,128)(2,1)S(1)}, u32[]{:S(2)}, u32[]{:S(2)}) %all-to-all-start.3) | async-done | bytes 393248 | tf_op jit(solution)/shard_map/all_to_all | solution.py:19
  172.0 0.7 bitcast_reduce_fusion
  (48 shorter events, 4.0 us)
Async XLA Ops:
  7.2 18.1 %copy-start = (bf16[128,4096]{1,0:T(8,128)(2,1)S(1)}, bf16[128,4096]{1,0:T(8,128)(2,1)}, u32[]{:S(2)}) copy-start(bf16[128,4096]{1,0:T(8,128)(2,1)} %param.6) | copy-start | bytes 3145732
  7.2 84.3 %all-gather.2.cloned.1.call-start = ((), (), s32[]{:S(2)}) async-start(), calls=%async_computation.5 | async-start | bytes 5308416 | tf_op jit(solution)/shard_map/all_gather | solution.py:98
  23.4 1.8 copy-start.8
  23.4 1.8 copy-start.9
  23.7 1.9 %copy-start.3 = (bf16[128,4096]{1,0:T(8,128)(2,1)S(1)}, bf16[128,4096]{1,0:T(8,128)(2,1)}, u32[]{:S(2)}) copy-start(bf16[128,4096]{1,0:T(8,128)(2,1)} %param.7) | copy-start | bytes 3145732
  25.1 135.3 %reduce-scatter.2.cloned.1.call-start = ((), (), s32[]{:S(2)}) async-start(), calls=%async_computation.6 | async-start | bytes 1966080 | tf_op jit(solution)/shard_map/reduce_scatter | solution.py:138
  91.5 5.9 %copy-start.1 = (bf16[32,16,2048]{2,1,0:T(8,128)(2,1)}, bf16[32,16,2048]{2,1,0:T(8,128)(2,1)S(1)}, u32[]{:S(2)}) copy-start(bf16[32,16,2048]{2,1,0:T(8,128)(2,1)S(1)} %all_to_all.21.rows_ref) | copy-start | bytes 6291460
  94.4 3.0 %copy-start.4 = (bf16[256,384]{1,0:T(8,128)(2,1)}, bf16[256,384]{1,0:T(8,128)(2,1)S(1)}, u32[]{:S(2)}) copy-start(bf16[256,384]{1,0:T(8,128)(2,1)S(1)} %fusion.14) | copy-start | bytes 589828
  98.2 13.8 %copy-start.5 = (bf16[256,384]{1,0:T(8,128)(2,1)S(1)}, bf16[256,384]{1,0:T(8,128)(2,1)}, u32[]{:S(2)}) copy-start(bf16[256,384]{1,0:T(8,128)(2,1)} %copy-done.4) | copy-start | bytes 589828
  98.2 13.8 %collective-permute-start = (bf16[256,1152]{1,0:T(8,128)(2,1)}, bf16[256,1152]{1,0:T(8,128)(2,1)S(1)}, u32[]{:S(2)}, u32[]{:S(2)}) collective-permute-start(bf16[256,1152]{1,0:T(8,128)(2,1)} %pad_maximum_fusion), channel_id=1, source_target_pairs={{0,4},{4,0},{1,5},{5,1},{2,6},{6,2},{3,7},{7,3},{8,12},{12,8},{9,1... | collective-permute-start | bytes 1769480 | tf_op jit(solution)/shard_map/ppermute | solution.py:23
  106.6 4.0 %collective-permute-start.1 = (bf16[1024,256]{1,0:T(8,128)(2,1)}, bf16[1024,256]{1,0:T(8,128)(2,1)S(1)}, u32[]{:S(2)}, u32[]{:S(2)}) collective-permute-start(bf16[1024,256]{1,0:T(8,128)(2,1)} %get-tuple-element.10), channel_id=1, source_target_pairs={{0,32},{32,0},{1,33},{33,1},{2,34},{34,2},{3,35},{35,3},{4,36},{36... | collective-permute-start | bytes 1572872 | tf_op jit(solution)/shard_map/ppermute | solution.py:23
  110.6 1.9 %copy-start.6 = (bf16[1024,256]{1,0:T(8,128)(2,1)}, bf16[1024,256]{1,0:T(8,128)(2,1)S(1)}, u32[]{:S(2)}) copy-start(bf16[1024,256]{1,0:T(8,128)(2,1)S(1)} %collective-permute-done.1.xb_ref) | copy-start | bytes 1572868
  112.1 2.9 %copy-start.10 = (bf16[2048,1152]{1,0:T(8,128)(2,1)S(1)}, bf16[2048,1152]{1,0:T(8,128)(2,1)}, u32[]{:S(2)}) copy-start(bf16[2048,1152]{1,0:T(8,128)(2,1)} %all-gather.2.cloned.1.call-done) | copy-start | bytes 14155780
  112.7 3.2 %copy-start.2 = (bf16[256,768]{1,0:T(8,128)(2,1)}, bf16[256,768]{1,0:T(8,128)(2,1)S(1)}, u32[]{:S(2)}) copy-start(bf16[256,768]{1,0:T(8,128)(2,1)S(1)} %pad_maximum_fusion.2.dgu_a_ref) | copy-start | bytes 1179652
  112.7 3.9 %collective-permute-start.2 = (bf16[256,768]{1,0:T(8,128)(2,1)S(1)}, bf16[256,768]{1,0:T(8,128)(2,1)S(1)}, u32[]{:S(2)}, u32[]{:S(2)}) collective-permute-start(bf16[256,768]{1,0:T(8,128)(2,1)S(1)} %pad_maximum_fusion.2.dgu_a_ref), channel_id=1, source_target_pairs={{0,32},{32,0},{1,33},{33,1},{2,34},{34,2},{3,35},{35,3},{4,36},{36... | collective-permute-start | bytes 1179656 | tf_op jit(solution)/shard_map/ppermute | solution.py:23
  116.6 0.8 copy-start.7
  160.4 11.6 %all-to-all-start.3 = ((bf16[4,128,384]{2,1,0:T(8,128)(2,1)}), bf16[4,128,384]{2,1,0:T(8,128)(2,1)S(1)}, u32[]{:S(2)}, u32[]{:S(2)}) async-start(bf16[4,128,384]{2,1,0:T(8,128)(2,1)} %bitcast.63), calls=%async_computation.4 | async-start | bytes 786432 | tf_op jit(solution)/shard_map/all_to_all | solution.py:19
Sparse Core Ops, SparseCore 0:
  25.3 40.5 all-gather.1
  122.0 29.7 reduce-scatter.1

commit v5 on v2

--- a/solution.py
+++ b/solution.py
@@ -17,7 +17,7 @@
     return lax.all_to_all(v, axes, split_axis=0, concat_axis=0, tiled=True)
 
 
-def swap_pairs(v, axis):
+def swap(v, axis):
     return lax.ppermute(v, axis, [(0, 1), (1, 0)])
 
 
@@ -28,15 +28,6 @@
     hid = down_weight.shape[1]
     n_yl, n_zh = lax.axis_size("yl"), lax.axis_size("zh")
 
-    n_zl = lax.axis_size("zl")
-    w_own = jnp.concatenate([gate_up_weight[0], jnp.transpose(down_weight[0])], axis=1)
-    w_sent = jnp.broadcast_to(w_own.reshape(1, n_yl, LANE, 3 * hid), (n_zl, n_yl, LANE, 3 * hid))
-    w_pair = a2a(w_sent.reshape(n_zl * n_yl, LANE, 3 * hid), ("zl", "yl"))
-    w_mine = jnp.transpose(w_pair.reshape(n_zl, n_yl, LANE, 3, hid), (0, 2, 3, 1, 4))
-    w_full = lax.all_gather(w_mine.reshape(n_zl * LANE, 3 * n_yl * hid), ("x", "c"), axis=0, tiled=True)
-    gu_cols = 2 * n_yl * hid
-    w_gu, w_down = w_full[:, :gu_cols], w_full[:, gu_cols:]
-
     positions = jnp.arange(CAP, dtype=jnp.int32)
     selector = jnp.transpose(slot)[:, None, :] == positions[None, :, None]
     picked = selector.astype(jnp.bfloat16)
@@ -44,10 +35,22 @@
     rows_dy = jnp.einsum("ect,td->ecd", picked, output_gradient, preferred_element_type=jnp.float32)
     gate = jnp.sum(jnp.where(selector, jnp.transpose(gate_weight)[:, None, :], 0.0), axis=2)
     rows_g = (rows_dy * gate[..., None]).astype(jnp.bfloat16)
+    n_zl = lax.axis_size("zl")
     n_xc = n_half // n_zl
     rows = jnp.concatenate([rows_x, rows_g], axis=1).reshape(n_win, 2 * CAP, n_zl, n_xc, n_yl, LANE)
     rows = jnp.transpose(rows, (0, 4, 1, 3, 2, 5)).reshape(n_win, n_yl, 1, 2 * CAP, n_half * LANE)
     rows = jnp.broadcast_to(rows, (n_win, n_yl, n_zh, 2 * CAP, n_half * LANE))
+    w_own = jnp.concatenate([gate_up_weight[0], jnp.transpose(down_weight[0])], axis=1)
+    w_sent = jnp.broadcast_to(w_own.reshape(1, n_yl, LANE, 3 * hid), (n_zl, n_yl, LANE, 3 * hid))
+    w_pair = a2a(w_sent.reshape(n_zl * n_yl, LANE, 3 * hid), ("zl", "yl"))
+    rows, w_pair = lax.optimization_barrier((rows, w_pair))
+    w_pair = w_pair.reshape(n_zl, n_yl, LANE, 3 * hid)
+    w_mine = [w_pair[:, i, :, : 2 * hid] for i in range(n_yl)] + [w_pair[:, i, :, 2 * hid :] for i in range(n_yl)]
+    w_mine = jnp.concatenate(w_mine, axis=2).reshape(n_zl * LANE, 3 * n_yl * hid)
+    w_full = lax.all_gather(w_mine, ("x", "c"), axis=0, tiled=True)
+    gu_cols = 2 * n_yl * hid
+    w_gu, w_down = w_full[:, :gu_cols], w_full[:, gu_cols:]
+
     recv = a2a(rows.reshape(-1, 2 * CAP, n_half * LANE), EXPERT)
     n_src = recv.shape[0]
     x_mat = recv[:, :CAP].reshape(n_src * CAP, n_half * LANE)
@@ -56,18 +59,22 @@
     part = jnp.concatenate(
         [f32_dot(x_mat, w_gu, ((1,), (0,))), f32_dot(g_mat, w_down, ((1,), (0,)))], axis=1
     ).astype(jnp.bfloat16)
-    total = part.astype(jnp.float32) + swap_pairs(part, "yl").astype(jnp.float32)
-    pre, up, dh = jnp.split(total, 3, axis=1)
-    sig = jax.nn.sigmoid(pre)
-    dgate = dh * up * sig * (1.0 + pre * (1.0 - sig))
-    dup = dh * (pre * sig)
-    dgu = jnp.concatenate([dgate, dup], axis=1).astype(jnp.bfloat16)
+    part_other, x_mat = lax.optimization_barrier((swap(part, "yl"), x_mat))
+    total = part.astype(jnp.float32) + part_other.astype(jnp.float32)
+    dgu = []
+    for i in range(n_yl):
+        pre, up = total[:, 2 * i * hid : (2 * i + 1) * hid], total[:, (2 * i + 1) * hid : (2 * i + 2) * hid]
+        dh = total[:, gu_cols + i * hid : gu_cols + (i + 1) * hid]
+        sig = jax.nn.sigmoid(pre)
+        dgu += [dh * up * sig * (1.0 + pre * (1.0 - sig)), dh * (pre * sig)]
+    dgu = jnp.concatenate(dgu, axis=1).astype(jnp.bfloat16)
 
     dx = f32_dot(dgu, w_gu, ((1,), (1,))).astype(jnp.bfloat16)
+    dx, dgu = lax.optimization_barrier((dx, dgu))
     pgu = f32_dot(x_mat, dgu, ((0,), (0,))).astype(jnp.bfloat16)
 
     summed = lax.psum_scatter(pgu, ("x", "c"), scatter_dimension=0, tiled=True)
-    summed = jnp.transpose(summed.reshape(n_zl, LANE, 2, n_yl, hid), (0, 3, 1, 2, 4))
+    summed = jnp.transpose(summed.reshape(n_zl, LANE, n_yl, 2 * hid), (0, 2, 1, 3))
     summed = a2a(summed.reshape(n_zl * n_yl, LANE, 2 * hid), ("zl", "yl"))
     grad_gu = jnp.sum(summed.reshape(n_zl, n_yl * LANE, 2 * hid).astype(jnp.float32), axis=0)
     grad_gu = grad_gu.astype(jnp.bfloat16)[None]

time: 175 us -> 189 us (1.080); the launches traced: 174 us -> 185 us
  blocking collectives: 78.1 us -> 66.3 us
  local copies, waits for them, and re-layouts: 7.05 us -> 17.7 us
  waiting for transfers between devices: 38.4 us -> 48.8 us
  starting transfers between devices: 20.4 us -> 23.5 us
    all_to_all x2 -> x1, blocking collectives: 78.1 us -> 66.3 us  [a2a(): return lax.all_to_all(v, axes, split_axis=0, concat_axis=0, tiled=True)]
    all_to_all x2 -> x3, waiting for transfers between devices: 4.47 us -> 11.4 us  [a2a(): return lax.all_to_all(v, axes, split_axis=0, concat_axis=0, tiled=True)]
    concatenate x0 -> x3, local copies, waits for them, and re-layouts: none -> 5.13 us  [on_device(): jnp.concatenate(w_mine, axis=2).reshape(n_zl * LANE, 3 * n_yl * hid)]
    slice x0 -> x4, local copies, waits for them, and re-layouts: none -> 4.61 us  [the longest x3 2.99 us: on_device(): w_pair[:, i, :, :2 * hid]]
    all_to_all x2 -> x3, starting transfers between devices: 16 us -> 19.4 us  [a2a(): return lax.all_to_all(v, axes, split_axis=0, concat_axis=0, tiled=True)]
    reduce_scatter x1, waiting for transfers between devices: 24.8 us -> 27.9 us  [on_device(): summed = lax.psum_scatter(pgu, ('x', 'c'), scatter_dimension=0, tiled=True)]
  transfers between devices with their start and end apart: 5 -> 6, of which waited for: 4 -> 4; matrix products, arithmetic and copies ran while one was open for 6% -> 4% of each run, Pallas kernels for 0% -> 0%
where the time goes in v5:
time: 189 us; the launch traced here: 185 us
  blocking collectives  66.3 us (35%)
  waiting for transfers between devices  48.8 us (26%)
  starting transfers between devices  23.5 us (12%)
  local copies, waits for them, and re-layouts  17.7 us (9%)
  between operations  14.3 us (8%)
  matrix products  12.2 us (6%)
  other arithmetic  2.65 us (1%)
    all_to_all x1, blocking collectives, a2a(): return lax.all_to_all(v, axes, split_axis=0, concat_axis=0, tiled=True)  66.3 us
    reduce_scatter x1, waiting for transfers between devices, on_device(): summed = lax.psum_scatter(pgu, ('x', 'c'), scatter_dimension=0, tiled=True)  27.9 us
    all_to_all x3, starting transfers between devices, a2a(): return lax.all_to_all(v, axes, split_axis=0, concat_axis=0, tiled=True)  19.4 us
    all_to_all x3, waiting for transfers between devices, a2a(): return lax.all_to_all(v, axes, split_axis=0, concat_axis=0, tiled=True)  11.4 us
    dot_general x4, matrix products, f32_dot(): lax.dot_general(a, b, (dims, ((), ())), preferred_element_type=jnp.float32)  10.2 us
    ppermute x1, waiting for transfers between devices, swap(): return lax.ppermute(v, axis, [(0, 1), (1, 0)])  9.49 us
    concatenate x3, local copies, waits for them, and re-layouts, on_device(): jnp.concatenate(w_mine, axis=2).reshape(n_zl * LANE, 3 * n_yl * hid)  5.13 us
    ppermute x1, starting transfers between devices, swap(): return lax.ppermute(v, axis, [(0, 1), (1, 0)])  4.05 us
  transfers between devices with their start and end apart: 6, of which 4 were waited for; matrix products, arithmetic and copies ran while one was open for 4% of the time, Pallas kernels for 0%

profile of v5, /device:TPU:6, one launch (start us, length us, event | category | flops | bytes accessed | tf_op | source)
XLA Modules:
  0.0 185.4 jit_solution(7954022601628420883)
XLA Ops:
  7.2 1.1 copy.36
  10.4 4.7 %all-to-all-start = ((bf16[4,128,576]{1,2,0:T(8,128)(2,1)}), bf16[4,128,576]{1,2,0:T(8,128)(2,1)}, u32[]{:S(2)}, u32[]{:S(2)}) async-start(bf16[4,128,576]{1,2,0:T(8,128)(2,1)} %bitcast.10), calls=%async_computation | async-start | bytes 1179648 | tf_op jit(solution)/shard_map/all_to_all | solution.py:17
  16.5 1.2 broadcast_in_dim.35
  17.7 6.5 %all-to-all-done = bf16[4,128,576]{1,2,0:T(8,128)(2,1)} async-done(((bf16[4,128,576]{1,2,0:T(8,128)(2,1)}), bf16[4,128,576]{1,2,0:T(8,128)(2,1)}, u32[]{:S(2)}, u32[]{:S(2)}) %all-to-all-start) | async-done | bytes 589856 | tf_op jit(solution)/shard_map/all_to_all | solution.py:17
  24.2 1.3 broadcast_in_dim.36
  25.5 1.6 fusion.28
  27.2 1.7 fusion.29
  29.1 1.6 copy.38
  30.7 1.6 copy.37
  32.4 1.1 copy.28
  33.5 1.8 concatenate.39
  35.4 66.3 %all_to_all.20 = bf16[32,16,2048]{2,1,0:T(8,128)(2,1)} all-to-all(bf16[32,16,2048]{2,1,0:T(8,128)(2,1)S(1)} %bitcast.50), channel_id=1, replica_groups=mesh['zl'=2,'x'=4,'c'=2,'yh'=4,'yl'=2,'zh'=4] {'yh','yl','zh'}, dimensions={0} | all-to-all | bytes 4194304 | tf_op jit(solution)/shard_map/all_to_all | solution.py:17
  101.6 2.6 %fusion.14 = bf16[256,384]{1,0:T(8,128)(2,1)S(1)} fusion(bf16[2048,1152]{1,0:T(8,128)(2,1)} %all-gather.2.cloned.1.call-done, bf16[32,16,2048]{2,1,0:T(8,128)(2,1)} %all_to_all.20), kind=kOutput, calls=%fused_computation.16 | convolution fusion | flops 402751488 | bytes 2818048 | tf_op jit(solution)/shard_map/dot_general | solution.py:13
  104.2 3.0 %fusion.11 = bf16[256,768]{1,0:T(8,128)(2,1)S(1)} fusion(bf16[2048,1152]{1,0:T(8,128)(2,1)} %all-gather.2.cloned.1.call-done, bf16[32,16,2048]{2,1,0:T(8,128)(2,1)S(1)} %copy-done.1), kind=kOutput, calls=%fused_computation.14 | convolution fusion | flops 805502976 | bytes 4587520 | tf_op jit(solution)/shard_map/dot_general | solution.py:13
  107.3 4.1 %collective-permute-start = (bf16[256,1152]{1,0:T(8,128)(2,1)S(1)}, bf16[256,1152]{1,0:T(8,128)(2,1)S(1)}, u32[]{:S(2)}, u32[]{:S(2)}) collective-permute-start(bf16[256,1152]{1,0:T(8,128)(2,1)S(1)} %pad_maximum_fusion), channel_id=1, source_target_pairs={{0,4},{4,0},{1,5},{5,1},{2,6},{6,2},{3,7},{7,3},{8,12},{12,8},{9,1... | collective-permute-start | bytes 1769480 | tf_op jit(solution)/shard_map/ppermute | solution.py:21
  111.5 9.5 %collective-permute-done = bf16[256,1152]{1,0:T(8,128)(2,1)S(1)} collective-permute-done((bf16[256,1152]{1,0:T(8,128)(2,1)S(1)}, bf16[256,1152]{1,0:T(8,128)(2,1)S(1)}, u32[]{:S(2)}, u32[]{:S(2)}) %collective-permute-start) | collective-permute-done | bytes 589856 | tf_op jit(solution)/shard_map/ppermute | solution.py:21
  121.7 2.0 %fusion.6 = bf16[256,2048]{1,0:T(8,128)(2,1)} fusion(bf16[256,768]{1,0:T(8,128)(2,1)S(1)} %pad_maximum_fusion.2, bf16[2048,1152]{1,0:T(8,128)(2,1)S(1)} %bitcast.69), kind=kOutput, calls=%fused_computation.10 | convolution fusion | flops 805830656 | bytes 4587520 | tf_op jit(solution)/shard_map/dot_general | solution.py:13
  123.7 2.7 %convolution_convert_fusion.1 = bf16[2048,768]{1,0:T(8,128)(2,1)} fusion(bf16[256,2048]{1,0:T(8,128)(2,1)S(1)} %slice_bitcast_fusion.2, bf16[256,768]{1,0:T(8,128)(2,1)S(1)} %pad_maximum_fusion.2), kind=kOutput, calls=%fused_computation.5 | convolution fusion | flops 806879232 | bytes 4587520 | tf_op jit(solution)/shard_map/dot_general | solution.py:13
  126.4 10.9 %all-to-all-start.2 = ((bf16[32,8,2048]{2,1,0:T(8,128)(2,1)}), bf16[32,8,2048]{2,1,0:T(8,128)(2,1)S(1)}, u32[]{:S(2)}, u32[]{:S(2)}) async-start(bf16[32,8,2048]{2,1,0:T(8,128)(2,1)} %bitcast.19), calls=%async_computation.2 | async-start | bytes 2097152 | tf_op jit(solution)/shard_map/all_to_all | solution.py:17
  137.3 27.9 %reduce-scatter.2.cloned.1.call-done = bf16[256,768]{1,0:T(8,128)(2,1)} async-done(((bf16[2048,768]{1,0:T(8,128)(2,1)}), bf16[256,768]{1,0:T(8,128)(2,1)}) %reduce-scatter.2.cloned.1.call-update) | async-done | bytes 393232 | tf_op jit(solution)/shard_map/reduce_scatter | solution.py:76
  165.1 1.1 reshape.66
  167.0 3.8 %all-to-all-start.3 = ((bf16[4,128,384]{2,1,0:T(8,128)(2,1)}), bf16[4,128,384]{2,1,0:T(8,128)(2,1)S(1)}, u32[]{:S(2)}, u32[]{:S(2)}) async-start(bf16[4,128,384]{2,1,0:T(8,128)(2,1)} %bitcast.24), calls=%async_computation.4 | async-start | bytes 786432 | tf_op jit(solution)/shard_map/all_to_all | solution.py:17
  171.5 1.5 fusion
  172.9 4.9 %all-to-all-done.3 = bf16[4,128,384]{2,1,0:T(8,128)(2,1)S(1)} async-done(((bf16[4,128,384]{2,1,0:T(8,128)(2,1)}), bf16[4,128,384]{2,1,0:T(8,128)(2,1)S(1)}, u32[]{:S(2)}, u32[]{:S(2)}) %all-to-all-start.3) | async-done | bytes 393248 | tf_op jit(solution)/shard_map/all_to_all | solution.py:17
  (41 shorter events, 6.7 us)
Async XLA Ops:
  7.2 7.9 %copy-start = (bf16[128,4096]{1,0:T(8,128)(2,1)S(1)}, bf16[128,4096]{1,0:T(8,128)(2,1)}, u32[]{:S(2)}) copy-start(bf16[128,4096]{1,0:T(8,128)(2,1)} %param.6) | copy-start | bytes 3145732
  7.2 7.9 %copy-start.3 = (s32[128,4]{0,1:T(4,128)S(1)}, s32[128,4]{0,1:T(4,128)}, u32[]{:S(2)}) copy-start(s32[128,4]{0,1:T(4,128)} %param.8) | copy-start | bytes 6148
  9.2 6.1 %copy-start.4 = (f32[128,4]{0,1:T(4,128)S(1)}, f32[128,4]{0,1:T(4,128)}, u32[]{:S(2)}) copy-start(f32[128,4]{0,1:T(4,128)} %param.9) | copy-start | bytes 6148
  9.3 6.2 %copy-start.2 = (bf16[128,4096]{1,0:T(8,128)(2,1)S(1)}, bf16[128,4096]{1,0:T(8,128)(2,1)}, u32[]{:S(2)}) copy-start(bf16[128,4096]{1,0:T(8,128)(2,1)} %param.7) | copy-start | bytes 3145732
  10.4 13.8 %all-to-all-start = ((bf16[4,128,576]{1,2,0:T(8,128)(2,1)}), bf16[4,128,576]{1,2,0:T(8,128)(2,1)}, u32[]{:S(2)}, u32[]{:S(2)}) async-start(bf16[4,128,576]{1,2,0:T(8,128)(2,1)} %bitcast.10), calls=%async_computation | async-start | bytes 1179648 | tf_op jit(solution)/shard_map/all_to_all | solution.py:17
  15.0 86.6 %all-gather.2.cloned.1.call-start = ((), (), s32[]{:S(2)}) async-start(), calls=%async_computation.5 | async-start | bytes 5308416 | tf_op jit(solution)/shard_map/all_gather | solution.py:50
  35.3 129.8 %reduce-scatter.2.cloned.1.call-start = ((), (), s32[]{:S(2)}) async-start(), calls=%async_computation.6 | async-start | bytes 3538944 | tf_op jit(solution)/shard_map/reduce_scatter | solution.py:76
  101.6 2.6 %copy-start.1 = (bf16[32,16,2048]{2,1,0:T(8,128)(2,1)S(1)}, bf16[32,16,2048]{2,1,0:T(8,128)(2,1)}, u32[]{:S(2)}) copy-start(bf16[32,16,2048]{2,1,0:T(8,128)(2,1)} %all_to_all.20) | copy-start | bytes 6291460
  104.2 17.4 %slice-start = ((s8[4718592]{0:T(1024)(128)(4,1)}), s8[4194304]{0:T(1024)(128)(4,1)S(1)}, s32[]{:S(2)}) async-start(s8[4718592]{0:T(1024)(128)(4,1)} %bitcast.68), calls=%async_computation.7 | async-start | bytes 8388608
  107.3 14.4 %slice-start.1 = ((s8[4718592]{0:T(1024)(128)(4,1)}), s8[524288]{0:T(1024)(128)(4,1)S(1)}, s32[]{:S(2)}) async-start(s8[4718592]{0:T(1024)(128)(4,1)} %bitcast.68), calls=%async_computation.8 | async-start | bytes 1048576
  107.3 13.7 %collective-permute-start = (bf16[256,1152]{1,0:T(8,128)(2,1)S(1)}, bf16[256,1152]{1,0:T(8,128)(2,1)S(1)}, u32[]{:S(2)}, u32[]{:S(2)}) collective-permute-start(bf16[256,1152]{1,0:T(8,128)(2,1)S(1)} %pad_maximum_fusion), channel_id=1, source_target_pairs={{0,4},{4,0},{1,5},{5,1},{2,6},{6,2},{3,7},{7,3},{8,12},{12,8},{9,1... | collective-permute-start | bytes 1769480 | tf_op jit(solution)/shard_map/ppermute | solution.py:21
  126.4 40.7 %all-to-all-start.2 = ((bf16[32,8,2048]{2,1,0:T(8,128)(2,1)}), bf16[32,8,2048]{2,1,0:T(8,128)(2,1)S(1)}, u32[]{:S(2)}, u32[]{:S(2)}) async-start(bf16[32,8,2048]{2,1,0:T(8,128)(2,1)} %bitcast.19), calls=%async_computation.2 | async-start | bytes 2097152 | tf_op jit(solution)/shard_map/all_to_all | solution.py:17
  167.0 10.8 %all-to-all-start.3 = ((bf16[4,128,384]{2,1,0:T(8,128)(2,1)}), bf16[4,128,384]{2,1,0:T(8,128)(2,1)S(1)}, u32[]{:S(2)}, u32[]{:S(2)}) async-start(bf16[4,128,384]{2,1,0:T(8,128)(2,1)} %bitcast.24), calls=%async_computation.4 | async-start | bytes 786432 | tf_op jit(solution)/shard_map/all_to_all | solution.py:17
Sparse Core Ops, SparseCore 0:
  35.4 41.7 all-gather.1
  126.5 38.6 reduce-scatter.1

commit v6 on v4

--- a/solution.py
+++ b/solution.py
@@ -54,31 +54,38 @@
     )(core.reshape(1), recv)
 
 
-def pgu_kernel(xa_ref, xb_ref, dgu_a_ref, dgu_b_ref, pgu_ref):
-    acc = jnp.dot(xa_ref[...], dgu_a_ref[...], preferred_element_type=jnp.float32)
-    acc += jnp.dot(xb_ref[...], dgu_b_ref[...], preferred_element_type=jnp.float32)
-    n_zl, n_yl, lanes, cols = pgu_ref.shape
-    for i in range(n_zl):
-        for j in range(n_yl):
-            block = acc[i * lanes : (i + 1) * lanes, j * cols : (j + 1) * cols]
-            pgu_ref[i, j] = block.astype(pgu_ref.dtype)
+def pack_kernel(gu_ref, down_ref, out_ref):
+    n_zl, n_yl, _, lanes = out_ref.shape
+    gu_cols = gu_ref.shape[1]
+    for j in range(n_yl):
+        half = slice(j * lanes, (j + 1) * lanes)
+        gu_t = gu_ref[half, :].T
+        for i in range(n_zl):
+            out_ref[i, j, :gu_cols, :] = gu_t
+            out_ref[i, j, gu_cols:, :] = down_ref[:, half]
 
 
-def weight_products(xt_a, xt_b, dgu_a, dgu_b, n_zl, n_yl):
-    width, m = xt_a.shape
-    cols = dgu_a.shape[1] // n_yl
-    x_spec = pl.BlockSpec((n_zl * LANE, m), lambda k: (k, 0))
-    dgu_spec = pl.BlockSpec(dgu_a.shape, lambda k: (0, 0))
-    n_x = width // (n_zl * LANE)
-    out = pl.pallas_call(
-        pgu_kernel,
-        grid=(n_x,),
-        in_specs=[x_spec, x_spec, dgu_spec, dgu_spec],
-        out_specs=pl.BlockSpec((None, n_zl, n_yl, LANE, cols), lambda k: (k, 0, 0, 0, 0)),
-        out_shape=jax.ShapeDtypeStruct((n_x, n_zl, n_yl, LANE, cols), jnp.bfloat16),
-        name="weight_products",
-    )(xt_a, xt_b, dgu_a, dgu_b)
-    return out.reshape(-1, cols)
+def pack_weights(gate_up, down, n_zl, n_yl):
+    shape = (n_zl, n_yl, gate_up.shape[1] + down.shape[0], LANE)
+    out = pl.pallas_call(pack_kernel, out_shape=jax.ShapeDtypeStruct(shape, gate_up.dtype), name="pack_weights")(
+        gate_up, down
+    )
+    return out.reshape(n_zl * n_yl, shape[2], LANE)
+
+
+def order_kernel(pair_ref, out_ref):
+    n_zl, n_yl, units, lanes = pair_ref.shape
+    gu_cols = 2 * units // 3
+    for i in range(n_zl):
+        pair = [pair_ref[i, j] for j in range(n_yl)]
+        turned = jnp.concatenate([p[:gu_cols] for p in pair] + [p[gu_cols:] for p in pair], axis=0).T
+        out_ref[i * lanes : (i + 1) * lanes, :] = turned
+
+
+def order_weights(pair, n_zl, n_yl):
+    _, units, lanes = pair.shape
+    out = jax.ShapeDtypeStruct((n_zl * lanes, n_yl * units), pair.dtype)
+    return pl.pallas_call(order_kernel, out_shape=out, name="order_weights")(pair.reshape(n_zl, n_yl, units, lanes))
 
 
 def on_device(tokens, output_gradient, slot, gate_weight, gate_up_weight, down_weight):
@@ -88,17 +95,6 @@
     hid = down_weight.shape[1]
     n_yl, n_zh, n_c = lax.axis_size("yl"), lax.axis_size("zh"), lax.axis_size("c")
 
-    n_zl = lax.axis_size("zl")
-    w_own = jnp.concatenate([gate_up_weight[0], jnp.transpose(down_weight[0])], axis=1)
-    w_sent = jnp.broadcast_to(w_own.reshape(1, n_yl, LANE, 3 * hid), (n_zl, n_yl, LANE, 3 * hid))
-    w_pair = a2a(w_sent.reshape(n_zl * n_yl, LANE, 3 * hid), ("zl", "yl"))
-    w_pair = w_pair.reshape(n_zl, n_yl, LANE, 3 * hid)
-    w_mine = [w_pair[:, i, :, : 2 * hid] for i in range(n_yl)] + [w_pair[:, i, :, 2 * hid :] for i in range(n_yl)]
-    w_mine = jnp.concatenate(w_mine, axis=2).reshape(n_zl * LANE, 3 * n_yl * hid)
-    w_full = lax.all_gather(w_mine, ("x", "c"), axis=0, tiled=True)
-    gu_cols = 2 * n_yl * hid
-    w_gu, w_down = w_full[:, :gu_cols], w_full[:, gu_cols:]
-
     positions = jnp.arange(CAP, dtype=jnp.int32)
     selector = jnp.transpose(slot)[:, None, :] == positions[None, :, None]
     picked = selector.astype(jnp.bfloat16)
@@ -106,11 +102,20 @@
     rows_dy = jnp.einsum("ect,td->ecd", picked, output_gradient, preferred_element_type=jnp.float32)
     gate = jnp.sum(jnp.where(selector, jnp.transpose(gate_weight)[:, None, :], 0.0), axis=2)
     rows_g = (rows_dy * gate[..., None]).astype(jnp.bfloat16)
+    n_zl = lax.axis_size("zl")
     n_xc = n_half // n_zl
     rows = jnp.concatenate([rows_x, rows_g], axis=1).reshape(n_win, 2 * CAP, n_zl, n_xc, n_yl, LANE)
     rows = jnp.transpose(rows, (0, 4, 1, 3, 2, 5)).reshape(n_win, n_yl, 1, 2 * CAP, n_half * LANE)
     rows = jnp.broadcast_to(rows, (n_win, n_yl, n_zh, 2 * CAP, n_half * LANE))
-    recv = a2a(rows.reshape(-1, 2 * CAP, n_half * LANE), EXPERT)
+    rows = rows.reshape(-1, 2 * CAP, n_half * LANE)
+
+    w_pair = a2a(pack_weights(gate_up_weight[0], down_weight[0], n_zl, n_yl), ("zl", "yl"))
+    rows, w_pair = lax.optimization_barrier((rows, w_pair))
+    w_full = lax.all_gather(order_weights(w_pair, n_zl, n_yl), ("x", "c"), axis=0, tiled=True)
+    gu_cols = 2 * n_yl * hid
+    w_gu, w_down = w_full[:, :gu_cols], w_full[:, gu_cols:]
+
+    recv = a2a(rows, EXPERT)
     n_src = recv.shape[0]
     x_mat = recv[:, :CAP].reshape(n_src * CAP, n_half * LANE)
     g_mat = recv[:, CAP:].reshape(n_src * CAP, n_half * LANE)
@@ -119,6 +124,7 @@
         [f32_dot(x_mat, w_gu, ((1,), (0,))), f32_dot(g_mat, w_down, ((1,), (0,)))], axis=1
     ).astype(jnp.bfloat16)
 
+    part, recv = lax.optimization_barrier((part, recv))
     xt_kept, xt_given = split_rows(lax.axis_index("c"), recv, n_c * n_zl * LANE)
     part_other, xt_kept, xt_got = lax.optimization_barrier((swap(part, "yl"), xt_kept, swap(xt_given, "c")))
 
@@ -133,9 +139,11 @@
 
     dx = f32_dot(dgu, w_gu, ((1,), (1,))).astype(jnp.bfloat16)
     dx, dgu_other = lax.optimization_barrier((dx, swap(dgu, "c")))
-    pgu = weight_products(xt_kept, xt_got, dgu, dgu_other, n_zl, n_yl)
+    both = jnp.concatenate([dgu, dgu_other], axis=0)
+    pgu = jnp.dot(jnp.concatenate([xt_kept, xt_got], axis=1), both, preferred_element_type=jnp.float32).astype(jnp.bfloat16)
 
     summed = lax.psum_scatter(pgu, "x", scatter_dimension=0, tiled=True)
+    summed = jnp.transpose(summed.reshape(n_zl, LANE, n_yl, 2 * hid), (0, 2, 1, 3))
     summed = a2a(summed.reshape(n_zl * n_yl, LANE, 2 * hid), ("zl", "yl"))
     grad_gu = jnp.sum(summed.reshape(n_zl, n_yl * LANE, 2 * hid).astype(jnp.float32), axis=0)
     grad_gu = grad_gu.astype(jnp.bfloat16)[None]

time: 180 us -> 178 us (0.989)
  blocking collectives: 117 us -> 66.3 us
  waiting for transfers between devices: 8.01 us -> 42.4 us
  starting transfers between devices: 14.4 us -> 27.2 us
  matrix products: 8.83 us -> 12.3 us
  other arithmetic: 3.48 us -> 1.66 us
    all_to_all x3 -> x1, blocking collectives: 117 us -> 66.3 us  [a2a(): return lax.all_to_all(v, axes, split_axis=0, concat_axis=0, tiled=True)]
    reduce_scatter x1, waiting for transfers between devices: 0.01 us -> 19.8 us  [on_device(): summed = lax.psum_scatter(pgu, 'x', scatter_dimension=0, tiled=True)]
    all_to_all x1 -> x3, waiting for transfers between devices: 3.81 us -> 18.7 us  [a2a(): return lax.all_to_all(v, axes, split_axis=0, concat_axis=0, tiled=True)]
    all_to_all x1 -> x3, starting transfers between devices: 5.7 us -> 19.1 us  [a2a(): return lax.all_to_all(v, axes, split_axis=0, concat_axis=0, tiled=True)]
    concatenate x4 -> x0, local copies, waits for them, and re-layouts: 2.31 us -> none  [the longest x3 1.24 us: on_device(): jnp.concatenate(w_mine, axis=2).reshape(n_zl * LANE, 3 * n_yl * hid)]
    dot_general x0 -> x1, matrix products: none -> 2.23 us  [on_device(): jnp.dot(jnp.concatenate([xt_kept, xt_got], axis=1), both, preferred_eleme...]
    reshape x0 -> x2, local copies, waits for them, and re-layouts: none -> 1.88 us  [on_device(): summed.reshape(n_zl, LANE, n_yl, 2 * hid)]
    broadcast_in_dim x2, local copies, waits for them, and re-layouts: 0.64 us -> 2.49 us  [on_device(): rows = jnp.broadcast_to(rows, (n_win, n_yl, n_zh, 2 * CAP, n_half * LANE))]
  transfers between devices with their start and end apart: 6 -> 8, of which waited for: 4 -> 6; matrix products, arithmetic and copies ran while one was open for 3% -> 5% of each run, Pallas kernels for 2% -> 2%
where the time goes in v6:
time: 178 us
  blocking collectives  66.3 us (37%)
  waiting for transfers between devices  42.4 us (24%)
  starting transfers between devices  27.2 us (15%)
  between operations  14.2 us (8%)
  matrix products  12.3 us (7%)
  Pallas kernels  7.94 us (4%)
  local copies, waits for them, and re-layouts  5.63 us (3%)
    all_to_all x1, blocking collectives, a2a(): return lax.all_to_all(v, axes, split_axis=0, concat_axis=0, tiled=True)  66.3 us
    reduce_scatter x1, waiting for transfers between devices, on_device(): summed = lax.psum_scatter(pgu, 'x', scatter_dimension=0, tiled=True)  19.8 us
    all_to_all x3, starting transfers between devices, a2a(): return lax.all_to_all(v, axes, split_axis=0, concat_axis=0, tiled=True)  19.1 us
    all_to_all x3, waiting for transfers between devices, a2a(): return lax.all_to_all(v, axes, split_axis=0, concat_axis=0, tiled=True)  18.7 us
    ppermute x3, starting transfers between devices, swap(): return lax.ppermute(v, axis, [(0, 1), (1, 0)])  8 us
    dot_general x3, matrix products, f32_dot(): lax.dot_general(a, b, (dims, ((), ())), preferred_element_type=jnp.float32)  7.43 us
    ppermute x3, waiting for transfers between devices, swap(): return lax.ppermute(v, axis, [(0, 1), (1, 0)])  3.88 us
    pallas_call x1, Pallas kernels, split_rows(): pl.pallas_call(split_kernel, grid=(width // depth,), in_specs=[pl.BlockSp...  3.8 us
  transfers between devices with their start and end apart: 8, of which 6 were waited for; matrix products, arithmetic and copies ran while one was open for 5% of the time, Pallas kernels for 2%

profile of v6, /device:TPU:6, one launch (start us, length us, event | category | flops | bytes accessed | tf_op | source)
XLA Modules:
  0.0 177.7 jit_solution(17057560058430752704)
XLA Ops:
  7.2 2.0 %pack_weights.1 = bf16[2,2,576,128]{3,2,1,0:T(8,128)(2,1)} custom-call(bf16[256,384]{1,0:T(8,128)(2,1)} %bitcast.46, bf16[192,256]{1,0:T(8,128)(2,1)} %bitcast.48), custom_call_target="tpu_custom_call" | custom-call | tf_op jit(solution)/shard_map/pack_weights/pallas_call | solution.py:70
  9.3 4.7 %all-to-all-start = ((bf16[4,576,128]{2,1,0:T(8,128)(2,1)}), bf16[4,576,128]{2,1,0:T(8,128)(2,1)}, u32[]{:S(2)}, u32[]{:S(2)}) async-start(bf16[4,576,128]{2,1,0:T(8,128)(2,1)} %bitcast.42), calls=%async_computation | async-start | bytes 1179648 | tf_op jit(solution)/shard_map/all_to_all | solution.py:19
  16.1 1.2 broadcast_in_dim.28
  17.3 5.8 %all-to-all-done = bf16[4,576,128]{2,1,0:T(8,128)(2,1)} async-done(((bf16[4,576,128]{2,1,0:T(8,128)(2,1)}), bf16[4,576,128]{2,1,0:T(8,128)(2,1)}, u32[]{:S(2)}, u32[]{:S(2)}) %all-to-all-start) | async-done | bytes 589856 | tf_op jit(solution)/shard_map/all_to_all | solution.py:19
  23.1 1.3 broadcast_in_dim.29
  24.4 2.1 %order_weights.1 = bf16[256,1152]{1,0:T(8,128)(2,1)} custom-call(bf16[2,2,576,128]{3,2,1,0:T(8,128)(2,1)} %bitcast.10.pair_ref), custom_call_target="tpu_custom_call" | custom-call | tf_op jit(solution)/shard_map/order_weights/pallas_call | solution.py:88
  26.6 66.3 %all_to_all.20.rows_ref = bf16[32,16,2048]{2,1,0:T(8,128)(2,1)} all-to-all(bf16[32,16,2048]{2,1,0:T(8,128)(2,1)S(1)} %bitcast.40), channel_id=1, replica_groups=mesh['zl'=2,'x'=4,'c'=2,'yh'=4,'yl'=2,'zh'=4] {'yh','yl','zh'}, dimensions={0} | all-to-all | bytes 4194304 | tf_op jit(solution)/shard_map/all_to_all | solution.py:19
  92.9 3.3 %fusion.11 = bf16[256,768]{1,0:T(8,128)(2,1)S(1)} fusion(bf16[2048,1152]{1,0:T(8,128)(2,1)} %all-gather.2.cloned.1.call-done, bf16[32,16,2048]{2,1,0:T(8,128)(2,1)} %all_to_all.20.rows_ref), kind=kOutput, calls=%fused_computation.14 | convolution fusion | flops 805502976 | bytes 4587520 | tf_op jit(solution)/shard_map/dot_general | solution.py:15
  96.2 2.1 %fusion.14 = bf16[256,384]{1,0:T(8,128)(2,1)S(1)} fusion(bf16[2048,1152]{1,0:T(8,128)(2,1)} %all-gather.2.cloned.1.call-done, bf16[32,16,2048]{2,1,0:T(8,128)(2,1)S(1)} %copy-done.1), kind=kOutput, calls=%fused_computation.16 | convolution fusion | flops 402751488 | bytes 2818048 | tf_op jit(solution)/shard_map/dot_general | solution.py:15
  98.4 3.9 %collective-permute-start = (bf16[256,1152]{1,0:T(8,128)(2,1)S(1)}, bf16[256,1152]{1,0:T(8,128)(2,1)S(1)}, u32[]{:S(2)}, u32[]{:S(2)}) collective-permute-start(bf16[256,1152]{1,0:T(8,128)(2,1)S(1)} %pad_maximum_fusion), channel_id=1, source_target_pairs={{0,4},{4,0},{1,5},{5,1},{2,6},{6,2},{3,7},{7,3},{8,12},{12,8},{9,1... | collective-permute-start | bytes 1769480 | tf_op jit(solution)/shard_map/ppermute | solution.py:23
  102.3 3.8 %split_rows.1 = (bf16[1024,256]{1,0:T(8,128)(2,1)}, bf16[1024,256]{1,0:T(8,128)(2,1)}) custom-call(s32[1]{0:T(128)} %bitcast.12.core_ref, bf16[32,16,2048]{2,1,0:T(8,128)(2,1)} %all_to_all.20.rows_ref), custom_call_target="tpu_custom_call" | custom-call | tf_op jit(solution)/shard_map/split_rows/pallas_call | solution.py:44
  106.1 1.9 %collective-permute-start.1 = (bf16[1024,256]{1,0:T(8,128)(2,1)}, bf16[1024,256]{1,0:T(8,128)(2,1)S(1)}, u32[]{:S(2)}, u32[]{:S(2)}) collective-permute-start(bf16[1024,256]{1,0:T(8,128)(2,1)} %get-tuple-element.18), channel_id=1, source_target_pairs={{0,32},{32,0},{1,33},{33,1},{2,34},{34,2},{3,35},{35,3},{4,36},{36... | collective-permute-start | bytes 1572872 | tf_op jit(solution)/shard_map/ppermute | solution.py:23
  108.0 2.1 %collective-permute-done.1 = bf16[1024,256]{1,0:T(8,128)(2,1)S(1)} collective-permute-done((bf16[1024,256]{1,0:T(8,128)(2,1)}, bf16[1024,256]{1,0:T(8,128)(2,1)S(1)}, u32[]{:S(2)}, u32[]{:S(2)}) %collective-permute-start.1) | collective-permute-done | bytes 524320 | tf_op jit(solution)/shard_map/ppermute | solution.py:23
  110.1 1.8 %collective-permute-done = bf16[256,1152]{1,0:T(8,128)(2,1)S(1)} collective-permute-done((bf16[256,1152]{1,0:T(8,128)(2,1)S(1)}, bf16[256,1152]{1,0:T(8,128)(2,1)S(1)}, u32[]{:S(2)}, u32[]{:S(2)}) %collective-permute-start) | collective-permute-done | bytes 589856 | tf_op jit(solution)/shard_map/ppermute | solution.py:23
  112.5 2.2 %collective-permute-start.2 = (bf16[256,768]{1,0:T(8,128)(2,1)S(1)}, bf16[256,768]{1,0:T(8,128)(2,1)S(1)}, u32[]{:S(2)}, u32[]{:S(2)}) collective-permute-start(bf16[256,768]{1,0:T(8,128)(2,1)S(1)} %pad_maximum_fusion.2), channel_id=1, source_target_pairs={{0,32},{32,0},{1,33},{33,1},{2,34},{34,2},{3,35},{35,3},{4,36},{36... | collective-permute-start | bytes 1179656 | tf_op jit(solution)/shard_map/ppermute | solution.py:23
  114.7 2.0 %fusion.6 = bf16[256,2048]{1,0:T(8,128)(2,1)} fusion(bf16[256,768]{1,0:T(8,128)(2,1)S(1)} %pad_maximum_fusion.2, bf16[2048,1152]{1,0:T(8,128)(2,1)S(1)} %copy-done.5), kind=kOutput, calls=%fused_computation.9 | convolution fusion | flops 805830656 | bytes 4587520 | tf_op jit(solution)/shard_map/dot_general | solution.py:15
  116.7 2.2 %convolution_convert_fusion.1 = bf16[1024,768]{1,0:T(8,128)(2,1)} fusion(bf16[1024,256]{1,0:T(8,128)(2,1)S(1)} %collective-permute-done.1, bf16[1024,256]{1,0:T(8,128)(2,1)S(1)} %copy-done.6, bf16[256,768]{1,0:T(8,128)(2,1)S(1)} %collective-permute-done.2, bf16[256,192]{1,0:T(8,128)(2,1)S(1)} %get-tuple-element.25, ...), kind=kOutput, calls=%fused_computation.11 | convolution fusion | flops 812122112 | bytes 3407872 | tf_op jit(solution)/shard_map/dot_general | solution.py:143
  119.0 10.9 %all-to-all-start.2 = ((bf16[32,8,2048]{2,1,0:T(8,128)(2,1)}), bf16[32,8,2048]{2,1,0:T(8,128)(2,1)S(1)}, u32[]{:S(2)}, u32[]{:S(2)}) async-start(bf16[32,8,2048]{2,1,0:T(8,128)(2,1)} %bitcast.13), calls=%async_computation.2 | async-start | bytes 2097152 | tf_op jit(solution)/shard_map/all_to_all | solution.py:19
  129.9 19.8 %reduce-scatter.2.cloned.1.call-done = bf16[256,768]{1,0:T(8,128)(2,1)} async-done(((bf16[1024,768]{1,0:T(8,128)(2,1)}), bf16[256,768]{1,0:T(8,128)(2,1)}) %reduce-scatter.2.cloned.1.call-update) | async-done | bytes 393232 | tf_op jit(solution)/shard_map/reduce_scatter | solution.py:145
  149.7 1.1 reshape.57
  151.6 9.1 %all-to-all-done.2 = bf16[32,8,2048]{2,1,0:T(8,128)(2,1)S(1)} async-done(((bf16[32,8,2048]{2,1,0:T(8,128)(2,1)}), bf16[32,8,2048]{2,1,0:T(8,128)(2,1)S(1)}, u32[]{:S(2)}, u32[]{:S(2)}) %all-to-all-start.2) | async-done | bytes 1048608 | tf_op jit(solution)/shard_map/all_to_all | solution.py:19
  160.7 3.6 %all-to-all-start.3 = ((bf16[4,128,384]{2,1,0:T(8,128)(2,1)}), bf16[4,128,384]{2,1,0:T(8,128)(2,1)S(1)}, u32[]{:S(2)}, u32[]{:S(2)}) async-start(bf16[4,128,384]{2,1,0:T(8,128)(2,1)} %bitcast.18), calls=%async_computation.4 | async-start | bytes 786432 | tf_op jit(solution)/shard_map/all_to_all | solution.py:19
  164.8 1.5 fusion
  166.3 3.8 %all-to-all-done.3 = bf16[4,128,384]{2,1,0:T(8,128)(2,1)S(1)} async-done(((bf16[4,128,384]{2,1,0:T(8,128)(2,1)}), bf16[4,128,384]{2,1,0:T(8,128)(2,1)S(1)}, u32[]{:S(2)}, u32[]{:S(2)}) %all-to-all-start.3) | async-done | bytes 393248 | tf_op jit(solution)/shard_map/all_to_all | solution.py:19
  (35 shorter events, 5.0 us)
Async XLA Ops:
  7.2 6.8 %copy-start = (bf16[128,4096]{1,0:T(8,128)(2,1)S(1)}, bf16[128,4096]{1,0:T(8,128)(2,1)}, u32[]{:S(2)}) copy-start(bf16[128,4096]{1,0:T(8,128)(2,1)} %param.6) | copy-start | bytes 3145732
  7.2 7.7 %copy-start.3 = (s32[128,4]{0,1:T(4,128)S(1)}, s32[128,4]{0,1:T(4,128)}, u32[]{:S(2)}) copy-start(s32[128,4]{0,1:T(4,128)} %param.8) | copy-start | bytes 6148
  7.2 7.7 %copy-start.4 = (f32[128,4]{0,1:T(4,128)S(1)}, f32[128,4]{0,1:T(4,128)}, u32[]{:S(2)}) copy-start(f32[128,4]{0,1:T(4,128)} %param.9) | copy-start | bytes 6148
  7.2 7.8 %copy-start.2 = (bf16[128,4096]{1,0:T(8,128)(2,1)S(1)}, bf16[128,4096]{1,0:T(8,128)(2,1)}, u32[]{:S(2)}) copy-start(bf16[128,4096]{1,0:T(8,128)(2,1)} %param.7) | copy-start | bytes 3145732
  9.3 13.8 %all-to-all-start = ((bf16[4,576,128]{2,1,0:T(8,128)(2,1)}), bf16[4,576,128]{2,1,0:T(8,128)(2,1)}, u32[]{:S(2)}, u32[]{:S(2)}) async-start(bf16[4,576,128]{2,1,0:T(8,128)(2,1)} %bitcast.42), calls=%async_computation | async-start | bytes 1179648 | tf_op jit(solution)/shard_map/all_to_all | solution.py:19
  13.9 78.9 %all-gather.2.cloned.1.call-start = ((), (), s32[]{:S(2)}) async-start(), calls=%async_computation.5 | async-start | bytes 5308416 | tf_op jit(solution)/shard_map/all_gather | solution.py:114
  26.5 123.2 %reduce-scatter.2.cloned.1.call-start = ((), (), s32[]{:S(2)}) async-start(), calls=%async_computation.6 | async-start | bytes 1966080 | tf_op jit(solution)/shard_map/reduce_scatter | solution.py:145
  92.9 3.3 %copy-start.1 = (bf16[32,16,2048]{2,1,0:T(8,128)(2,1)S(1)}, bf16[32,16,2048]{2,1,0:T(8,128)(2,1)}, u32[]{:S(2)}) copy-start(bf16[32,16,2048]{2,1,0:T(8,128)(2,1)} %all_to_all.20.rows_ref) | copy-start | bytes 6291460
  98.4 13.5 %collective-permute-start = (bf16[256,1152]{1,0:T(8,128)(2,1)S(1)}, bf16[256,1152]{1,0:T(8,128)(2,1)S(1)}, u32[]{:S(2)}, u32[]{:S(2)}) collective-permute-start(bf16[256,1152]{1,0:T(8,128)(2,1)S(1)} %pad_maximum_fusion), channel_id=1, source_target_pairs={{0,4},{4,0},{1,5},{5,1},{2,6},{6,2},{3,7},{7,3},{8,12},{12,8},{9,1... | collective-permute-start | bytes 1769480 | tf_op jit(solution)/shard_map/ppermute | solution.py:23
  106.1 4.0 %collective-permute-start.1 = (bf16[1024,256]{1,0:T(8,128)(2,1)}, bf16[1024,256]{1,0:T(8,128)(2,1)S(1)}, u32[]{:S(2)}, u32[]{:S(2)}) collective-permute-start(bf16[1024,256]{1,0:T(8,128)(2,1)} %get-tuple-element.18), channel_id=1, source_target_pairs={{0,32},{32,0},{1,33},{33,1},{2,34},{34,2},{3,35},{35,3},{4,36},{36... | collective-permute-start | bytes 1572872 | tf_op jit(solution)/shard_map/ppermute | solution.py:23
  111.9 2.8 %copy-start.5 = (bf16[2048,1152]{1,0:T(8,128)(2,1)S(1)}, bf16[2048,1152]{1,0:T(8,128)(2,1)}, u32[]{:S(2)}) copy-start(bf16[2048,1152]{1,0:T(8,128)(2,1)} %all-gather.2.cloned.1.call-done) | copy-start | bytes 14155780
  112.5 4.2 %copy-start.6 = (bf16[1024,256]{1,0:T(8,128)(2,1)S(1)}, bf16[1024,256]{1,0:T(8,128)(2,1)}, u32[]{:S(2)}) copy-start(bf16[1024,256]{1,0:T(8,128)(2,1)} %get-tuple-element.21) | copy-start | bytes 1572868
  112.5 4.2 %collective-permute-start.2 = (bf16[256,768]{1,0:T(8,128)(2,1)S(1)}, bf16[256,768]{1,0:T(8,128)(2,1)S(1)}, u32[]{:S(2)}, u32[]{:S(2)}) collective-permute-start(bf16[256,768]{1,0:T(8,128)(2,1)S(1)} %pad_maximum_fusion.2), channel_id=1, source_target_pairs={{0,32},{32,0},{1,33},{33,1},{2,34},{34,2},{3,35},{35,3},{4,36},{36... | collective-permute-start | bytes 1179656 | tf_op jit(solution)/shard_map/ppermute | solution.py:23
  119.0 41.7 %all-to-all-start.2 = ((bf16[32,8,2048]{2,1,0:T(8,128)(2,1)}), bf16[32,8,2048]{2,1,0:T(8,128)(2,1)S(1)}, u32[]{:S(2)}, u32[]{:S(2)}) async-start(bf16[32,8,2048]{2,1,0:T(8,128)(2,1)} %bitcast.13), calls=%async_computation.2 | async-start | bytes 2097152 | tf_op jit(solution)/shard_map/all_to_all | solution.py:19
  160.7 9.5 %all-to-all-start.3 = ((bf16[4,128,384]{2,1,0:T(8,128)(2,1)}), bf16[4,128,384]{2,1,0:T(8,128)(2,1)S(1)}, u32[]{:S(2)}, u32[]{:S(2)}) async-start(bf16[4,128,384]{2,1,0:T(8,128)(2,1)} %bitcast.18), calls=%async_computation.4 | async-start | bytes 786432 | tf_op jit(solution)/shard_map/all_to_all | solution.py:19
Sparse Core Ops, SparseCore 0:
  26.6 41.7 all-gather.1
  119.1 30.5 reduce-scatter.1

commit v7 on v6

--- a/solution.py
+++ b/solution.py
@@ -73,21 +73,6 @@
     return out.reshape(n_zl * n_yl, shape[2], LANE)
 
 
-def order_kernel(pair_ref, out_ref):
-    n_zl, n_yl, units, lanes = pair_ref.shape
-    gu_cols = 2 * units // 3
-    for i in range(n_zl):
-        pair = [pair_ref[i, j] for j in range(n_yl)]
-        turned = jnp.concatenate([p[:gu_cols] for p in pair] + [p[gu_cols:] for p in pair], axis=0).T
-        out_ref[i * lanes : (i + 1) * lanes, :] = turned
-
-
-def order_weights(pair, n_zl, n_yl):
-    _, units, lanes = pair.shape
-    out = jax.ShapeDtypeStruct((n_zl * lanes, n_yl * units), pair.dtype)
-    return pl.pallas_call(order_kernel, out_shape=out, name="order_weights")(pair.reshape(n_zl, n_yl, units, lanes))
-
-
 def on_device(tokens, output_gradient, slot, gate_weight, gate_up_weight, down_weight):
     n_win = slot.shape[1]
     width = tokens.shape[1]
@@ -111,17 +96,18 @@
 
     w_pair = a2a(pack_weights(gate_up_weight[0], down_weight[0], n_zl, n_yl), ("zl", "yl"))
     rows, w_pair = lax.optimization_barrier((rows, w_pair))
-    w_full = lax.all_gather(order_weights(w_pair, n_zl, n_yl), ("x", "c"), axis=0, tiled=True)
+    w_all = lax.all_gather(w_pair.reshape(-1, LANE), ("x", "c"), axis=0, tiled=True)
+    w_all = w_all.reshape(n_xc, n_zl, n_yl, 3 * hid, LANE)
     gu_cols = 2 * n_yl * hid
-    w_gu, w_down = w_full[:, :gu_cols], w_full[:, gu_cols:]
-
-    recv = a2a(rows, EXPERT)
+    w_gu_t = jnp.transpose(w_all[:, :, :, : 2 * hid], (2, 3, 0, 1, 4)).reshape(gu_cols, n_half * LANE)
+    w_down_t = jnp.transpose(w_all[:, :, :, 2 * hid :], (2, 3, 0, 1, 4)).reshape(n_yl * hid, n_half * LANE)
+    recv, w_gu_t, w_down_t = lax.optimization_barrier((a2a(rows, EXPERT), w_gu_t, w_down_t))
     n_src = recv.shape[0]
     x_mat = recv[:, :CAP].reshape(n_src * CAP, n_half * LANE)
     g_mat = recv[:, CAP:].reshape(n_src * CAP, n_half * LANE)
 
     part = jnp.concatenate(
-        [f32_dot(x_mat, w_gu, ((1,), (0,))), f32_dot(g_mat, w_down, ((1,), (0,)))], axis=1
+        [f32_dot(x_mat, w_gu_t, ((1,), (1,))), f32_dot(g_mat, w_down_t, ((1,), (1,)))], axis=1
     ).astype(jnp.bfloat16)
 
     part, recv = lax.optimization_barrier((part, recv))
@@ -137,18 +123,29 @@
         dgu += [dh * up * sig * (1.0 + pre * (1.0 - sig)), dh * (pre * sig)]
     dgu = jnp.concatenate(dgu, axis=1).astype(jnp.bfloat16)
 
-    dx = f32_dot(dgu, w_gu, ((1,), (1,))).astype(jnp.bfloat16)
+    dx = jnp.dot(dgu, w_gu_t, preferred_element_type=jnp.float32).astype(jnp.bfloat16)
     dx, dgu_other = lax.optimization_barrier((dx, swap(dgu, "c")))
     both = jnp.concatenate([dgu, dgu_other], axis=0)
     pgu = jnp.dot(jnp.concatenate([xt_kept, xt_got], axis=1), both, preferred_element_type=jnp.float32).astype(jnp.bfloat16)
 
     summed = lax.psum_scatter(pgu, "x", scatter_dimension=0, tiled=True)
-    summed = jnp.transpose(summed.reshape(n_zl, LANE, n_yl, 2 * hid), (0, 2, 1, 3))
-    summed = a2a(summed.reshape(n_zl * n_yl, LANE, 2 * hid), ("zl", "yl"))
-    grad_gu = jnp.sum(summed.reshape(n_zl, n_yl * LANE, 2 * hid).astype(jnp.float32), axis=0)
-    grad_gu = grad_gu.astype(jnp.bfloat16)[None]
+    zl, yl = lax.axis_index("zl"), lax.axis_index("yl")
 
+    def block(zl_to, yl_to):
+        return lax.dynamic_slice(summed, (zl_to * LANE, yl_to * 2 * hid), (LANE, 2 * hid))
+
+    def flipped(v, flip):
+        return lax.ppermute(v, ("zl", "yl"), [(i, i ^ flip) for i in range(n_zl * n_yl)])
+
+    mine, other = block(zl, yl), flipped(block(zl, 1 - yl), 1)
+    mine2, other2 = flipped(block(1 - zl, yl), 2), flipped(block(1 - zl, 1 - yl), 3)
     back = a2a(dx.reshape(n_src, CAP, n_half * LANE), EXPERT)
+    back, other, mine2, other2 = lax.optimization_barrier((back, other, mine2, other2))
+    mine = (mine.astype(jnp.float32) + mine2.astype(jnp.float32)).astype(jnp.bfloat16)
+    other = (other.astype(jnp.float32) + other2.astype(jnp.float32)).astype(jnp.bfloat16)
+    low, high = jnp.where(yl == 0, mine, other), jnp.where(yl == 0, other, mine)
+    grad_gu = jnp.concatenate([low, high], axis=0)[None]
+
     back = jnp.sum(back.reshape(n_win, n_yl, n_zh, CAP, n_xc, n_zl, LANE).astype(jnp.float32), axis=2)
     back = jnp.transpose(back, (0, 2, 4, 3, 1, 5)).reshape(n_win, CAP, width)
     grad_tokens = jnp.einsum("ect,ecd->td", selector.astype(jnp.float32), back).astype(jnp.bfloat16)

time: 178 us -> 177 us (level); the launches traced: 178 us -> 175 us
  blocking collectives: 66.3 us -> 0 us
  waiting for transfers between devices: 42.4 us -> 68 us
  starting transfers between devices: 27.2 us -> 47.8 us
  local copies, waits for them, and re-layouts: 5.63 us -> 25.9 us
  matrix products: 12.3 us -> 10.1 us
  Pallas kernels: 7.94 us -> 5.85 us
    all_to_all x1 -> x0, blocking collectives: 66.3 us -> none  [a2a(): return lax.all_to_all(v, axes, split_axis=0, concat_axis=0, tiled=True)]
    all_gather x1, waiting for transfers between devices: 0.01 us -> 26.5 us  [on_device(): lax.all_gather(w_pair.reshape(-1, LANE), ('x', 'c'), axis=0, tiled=True)]
    all_to_all x3, starting transfers between devices: 19.1 us -> 32.3 us  [a2a(): return lax.all_to_all(v, axes, split_axis=0, concat_axis=0, tiled=True)]
    transpose x0 -> x4, local copies, waits for them, and re-layouts: none -> 11.4 us  [the longest x2 7.11 us: on_device(): jnp.transpose(w_all[:, :, :, :2 * hid], (2, 3, 0, 1, 4))]
    ppermute x0 -> x3, starting transfers between devices: none -> 9.21 us  [flipped(): lax.ppermute(v, ('zl', 'yl'), [(i, i ^ flip) for i in range(n_zl * n_yl)])]
    reshape x2, local copies, waits for them, and re-layouts: 1.88 us -> 9.95 us  [the longest x1 6.12 us: on_device(): jnp.transpose(w_all[:, :, :, :2 * hid], (2, 3, 0, 1, 4))]
    all_to_all x3, waiting for transfers between devices: 18.7 us -> 11.5 us  [a2a(): return lax.all_to_all(v, axes, split_axis=0, concat_axis=0, tiled=True)]
    ppermute x0 -> x3, waiting for transfers between devices: none -> 3.64 us  [flipped(): lax.ppermute(v, ('zl', 'yl'), [(i, i ^ flip) for i in range(n_zl * n_yl)])]
  transfers between devices with their start and end apart: 8 -> 11, of which waited for: 6 -> 8; matrix products, arithmetic and copies ran while one was open for 5% -> 15% of each run, Pallas kernels for 2% -> 2%
where the time goes in v7:
time: 177 us; the launch traced here: 175 us
  waiting for transfers between devices  68 us (38%)
  starting transfers between devices  47.8 us (27%)
  local copies, waits for them, and re-layouts  25.9 us (15%)
  between operations  14.3 us (8%)
  matrix products  10.1 us (6%)
  Pallas kernels  5.85 us (3%)
  other arithmetic  2.58 us (1%)
    all_to_all x3, starting transfers between devices, a2a(): return lax.all_to_all(v, axes, split_axis=0, concat_axis=0, tiled=True)  32.3 us
    all_gather x1, waiting for transfers between devices, on_device(): lax.all_gather(w_pair.reshape(-1, LANE), ('x', 'c'), axis=0, tiled=True)  26.5 us
    reduce_scatter x1, waiting for transfers between devices, on_device(): summed = lax.psum_scatter(pgu, 'x', scatter_dimension=0, tiled=True)  20.5 us
    all_to_all x3, waiting for transfers between devices, a2a(): return lax.all_to_all(v, axes, split_axis=0, concat_axis=0, tiled=True)  11.5 us
    ppermute x3, starting transfers between devices, flipped(): lax.ppermute(v, ('zl', 'yl'), [(i, i ^ flip) for i in range(n_zl * n_yl)])  9.21 us
    transpose x2, local copies, waits for them, and re-layouts, on_device(): jnp.transpose(w_all[:, :, :, :2 * hid], (2, 3, 0, 1, 4))  7.11 us
    ppermute x3, starting transfers between devices, swap(): return lax.ppermute(v, axis, [(0, 1), (1, 0)])  6.22 us
    reshape x1, local copies, waits for them, and re-layouts, on_device(): jnp.transpose(w_all[:, :, :, :2 * hid], (2, 3, 0, 1, 4))  6.12 us
  transfers between devices with their start and end apart: 11, of which 8 were waited for; matrix products, arithmetic and copies ran while one was open for 15% of the time, Pallas kernels for 2%

profile of v7, /device:TPU:6, one launch (start us, length us, event | category | flops | bytes accessed | tf_op | source)
XLA Modules:
  0.0 174.6 jit_solution(4770508568035812081)
XLA Ops:
  7.2 2.0 %pack_weights.1 = bf16[2,2,576,128]{3,2,1,0:T(8,128)(2,1)} custom-call(bf16[256,384]{1,0:T(8,128)(2,1)} %bitcast.50, bf16[192,256]{1,0:T(8,128)(2,1)} %bitcast.51), custom_call_target="tpu_custom_call" | custom-call | tf_op jit(solution)/shard_map/pack_weights/pallas_call | solution.py:70
  9.3 4.7 %all-to-all-start = ((bf16[4,576,128]{2,1,0:T(8,128)(2,1)}), bf16[4,576,128]{2,1,0:T(8,128)(2,1)S(1)}, u32[]{:S(2)}, u32[]{:S(2)}) async-start(bf16[4,576,128]{2,1,0:T(8,128)(2,1)} %bitcast.47), calls=%async_computation | async-start | bytes 1179648 | tf_op jit(solution)/shard_map/all_to_all | solution.py:19
  15.8 6.8 %all-to-all-done = bf16[4,576,128]{2,1,0:T(8,128)(2,1)S(1)} async-done(((bf16[4,576,128]{2,1,0:T(8,128)(2,1)}), bf16[4,576,128]{2,1,0:T(8,128)(2,1)S(1)}, u32[]{:S(2)}, u32[]{:S(2)}) %all-to-all-start) | async-done | bytes 589856 | tf_op jit(solution)/shard_map/all_to_all | solution.py:19
  24.4 15.0 %all-to-all-start.1 = ((bf16[32,16,2048]{2,1,0:T(8,128)(2,1)}), bf16[32,16,2048]{2,1,0:T(8,128)(2,1)S(1)}, u32[]{:S(2)}, u32[]{:S(2)}) async-start(bf16[32,16,2048]{2,1,0:T(8,128)(2,1)} %bitcast.5), calls=%async_computation.1 | async-start | bytes 4194304 | tf_op jit(solution)/shard_map/all_to_all | solution.py:19
  39.5 26.5 %all-gather.2.cloned.1.call-done = bf16[18432,128]{1,0:T(8,128)(2,1)} async-done(((bf16[2304,128]{1,0:T(8,128)(2,1)}), bf16[18432,128]{1,0:T(8,128)(2,1)}) %all-gather.2.cloned.1.call-update) | async-done | bytes 4718608 | tf_op jit(solution)/shard_map/all_gather | solution.py:99
  66.0 2.1 %slice_bitcast_fusion = bf16[2,384,8,2,128]{4,1,0,3,2:T(8,128)(2,1)S(1)} fusion(bf16[8,2,2,576,128]{4,3,2,1,0:T(8,128)(2,1)} %bitcast.43), kind=kLoop, calls=%fused_computation.5 | loop fusion | bytes 6291456 | tf_op jit(solution)/shard_map/transpose | solution.py:102
  68.1 5.0 %copy.16 = bf16[2,384,8,2,128]{4,3,2,1,0:T(2,128)(2,1)} copy(bf16[2,384,8,2,128]{4,1,0,3,2:T(8,128)(2,1)S(1)} %slice_bitcast_fusion) | data formatting | bytes 6291456 | tf_op jit(solution)/shard_map/transpose | solution.py:102
  73.1 6.1 %reshape.53 = bf16[768,2048]{1,0:T(8,128)(2,1)} reshape(bf16[2,384,8,2,128]{4,3,2,1,0:T(2,128)(2,1)} %copy.16) | data formatting | bytes 6291456 | tf_op jit(solution)/shard_map/reshape | solution.py:102
  80.8 2.8 %copy.17 = bf16[2,192,8,2,128]{4,3,2,1,0:T(2,128)(2,1)} copy(bf16[2,192,8,2,128]{4,1,0,3,2:T(8,128)(2,1)S(1)} %slice_bitcast_fusion.1) | data formatting | bytes 3145728 | tf_op jit(solution)/shard_map/transpose | solution.py:103
  83.5 3.8 %reshape.54 = bf16[384,2048]{1,0:T(8,128)(2,1)} reshape(bf16[2,192,8,2,128]{4,3,2,1,0:T(2,128)(2,1)} %copy.17) | data formatting | bytes 3145728 | tf_op jit(solution)/shard_map/reshape | solution.py:103
  87.4 4.7 %all-to-all-done.1.rows_ref = bf16[32,16,2048]{2,1,0:T(8,128)(2,1)S(1)} async-done(((bf16[32,16,2048]{2,1,0:T(8,128)(2,1)}), bf16[32,16,2048]{2,1,0:T(8,128)(2,1)S(1)}, u32[]{:S(2)}, u32[]{:S(2)}) %all-to-all-start.1) | async-done | bytes 2097184 | tf_op jit(solution)/shard_map/all_to_all | solution.py:19
  92.0 2.9 %convolution_convert_fusion.4 = bf16[256,384]{1,0:T(8,128)(2,1)S(1)} fusion(bf16[384,2048]{1,0:T(8,128)(2,1)} %reshape.54, bf16[32,16,2048]{2,1,0:T(8,128)(2,1)S(1)} %all-to-all-done.1.rows_ref), kind=kOutput, calls=%fused_computation.12 | convolution fusion | flops 402751488 | bytes 2818048 | tf_op jit(solution)/shard_map/dot_general | solution.py:15
  96.2 2.1 %collective-permute-start = (bf16[256,1152]{1,0:T(8,128)(2,1)S(1)}, bf16[256,1152]{1,0:T(8,128)(2,1)S(1)}, u32[]{:S(2)}, u32[]{:S(2)}) collective-permute-start(bf16[256,1152]{1,0:T(8,128)(2,1)S(1)} %pad_maximum_fusion), channel_id=1, source_target_pairs={{0,4},{4,0},{1,5},{5,1},{2,6},{6,2},{3,7},{7,3},{8,12},{12,8},{9,1... | collective-permute-start | bytes 1769480 | tf_op jit(solution)/shard_map/ppermute | solution.py:23
  98.3 3.8 %split_rows.1 = (bf16[1024,256]{1,0:T(8,128)(2,1)}, bf16[1024,256]{1,0:T(8,128)(2,1)}) custom-call(s32[1]{0:T(128)} %bitcast.15.core_ref, bf16[32,16,2048]{2,1,0:T(8,128)(2,1)} %copy-done.1), custom_call_target="tpu_custom_call" | custom-call | tf_op jit(solution)/shard_map/split_rows/pallas_call | solution.py:44
  104.1 2.1 %collective-permute-done.1 = bf16[1024,256]{1,0:T(8,128)(2,1)S(1)} collective-permute-done((bf16[1024,256]{1,0:T(8,128)(2,1)}, bf16[1024,256]{1,0:T(8,128)(2,1)S(1)}, u32[]{:S(2)}, u32[]{:S(2)}) %collective-permute-start.1) | collective-permute-done | bytes 524320 | tf_op jit(solution)/shard_map/ppermute | solution.py:23
  106.1 3.8 %collective-permute-done = bf16[256,1152]{1,0:T(8,128)(2,1)S(1)} collective-permute-done((bf16[256,1152]{1,0:T(8,128)(2,1)S(1)}, bf16[256,1152]{1,0:T(8,128)(2,1)S(1)}, u32[]{:S(2)}, u32[]{:S(2)}) %collective-permute-start) | collective-permute-done | bytes 589856 | tf_op jit(solution)/shard_map/ppermute | solution.py:23
  110.6 2.2 %collective-permute-start.2 = (bf16[256,768]{1,0:T(8,128)(2,1)S(1)}, bf16[256,768]{1,0:T(8,128)(2,1)S(1)}, u32[]{:S(2)}, u32[]{:S(2)}) collective-permute-start(bf16[256,768]{1,0:T(8,128)(2,1)S(1)} %pad_maximum_fusion.2), channel_id=1, source_target_pairs={{0,32},{32,0},{1,33},{33,1},{2,34},{34,2},{3,35},{35,3},{4,36},{36... | collective-permute-start | bytes 1179656 | tf_op jit(solution)/shard_map/ppermute | solution.py:23
  114.8 2.2 %convolution_convert_fusion.2 = bf16[1024,768]{1,0:T(8,128)(2,1)} fusion(bf16[1024,256]{1,0:T(8,128)(2,1)S(1)} %collective-permute-done.1, bf16[1024,256]{1,0:T(8,128)(2,1)S(1)} %copy-done.8, bf16[256,768]{1,0:T(8,128)(2,1)S(1)} %collective-permute-done.2, bf16[256,192]{1,0:T(8,128)(2,1)S(1)} %get-tuple-element.39, ...), kind=kOutput, calls=%fused_computation.8 | convolution fusion | flops 812122112 | bytes 3407872 | tf_op jit(solution)/shard_map/dot_general | solution.py:129
  117.0 12.6 %all-to-all-start.2 = ((bf16[32,8,2048]{2,1,0:T(8,128)(2,1)}), bf16[32,8,2048]{2,1,0:T(8,128)(2,1)S(1)}, u32[]{:S(2)}, u32[]{:S(2)}) async-start(bf16[32,8,2048]{2,1,0:T(8,128)(2,1)} %bitcast.16), calls=%async_computation.2 | async-start | bytes 2097152 | tf_op jit(solution)/shard_map/all_to_all | solution.py:19
  129.7 20.5 %reduce-scatter.2.cloned.1.call-done = bf16[256,768]{1,0:T(8,128)(2,1)} async-done(((bf16[1024,768]{1,0:T(8,128)(2,1)}), bf16[256,768]{1,0:T(8,128)(2,1)}) %reduce-scatter.2.cloned.1.call-update) | async-done | bytes 393232 | tf_op jit(solution)/shard_map/reduce_scatter | solution.py:131
  151.1 4.1 %collective-permute-start.5 = (bf16[128,384]{1,0:T(8,128)(2,1)S(1)}, bf16[128,384]{1,0:T(8,128)(2,1)S(1)}, u32[]{:S(2)}, u32[]{:S(2)}) collective-permute-start(bf16[128,384]{1,0:T(8,128)(2,1)S(1)} %get-tuple-element.44), channel_id=1, source_target_pairs={{0,260},{4,256},{256,4},{260,0},{1,261},{5,257},{257,5},{261,1},{2... | collective-permute-start | bytes 294920 | tf_op jit(solution)/shard_map/ppermute | solution.py:138
  155.2 2.3 %collective-permute-start.4 = (bf16[128,384]{1,0:T(8,128)(2,1)S(1)}, bf16[128,384]{1,0:T(8,128)(2,1)S(1)}, u32[]{:S(2)}, u32[]{:S(2)}) collective-permute-start(bf16[128,384]{1,0:T(8,128)(2,1)S(1)} %get-tuple-element.45), channel_id=1, source_target_pairs={{0,256},{4,260},{256,0},{260,4},{1,257},{5,261},{257,1},{261,5},{2... | collective-permute-start | bytes 294920 | tf_op jit(solution)/shard_map/ppermute | solution.py:138
  157.5 2.8 %collective-permute-start.3 = (bf16[128,384]{1,0:T(8,128)(2,1)S(1)}, bf16[128,384]{1,0:T(8,128)(2,1)S(1)}, u32[]{:S(2)}, u32[]{:S(2)}) collective-permute-start(bf16[128,384]{1,0:T(8,128)(2,1)S(1)} %get-tuple-element.46), channel_id=1, source_target_pairs={{0,4},{4,0},{256,260},{260,256},{1,5},{5,1},{257,261},{261,257},{2... | collective-permute-start | bytes 294920 | tf_op jit(solution)/shard_map/ppermute | solution.py:138
  161.7 2.3 %collective-permute-done.3 = bf16[128,384]{1,0:T(8,128)(2,1)S(1)} collective-permute-done((bf16[128,384]{1,0:T(8,128)(2,1)S(1)}, bf16[128,384]{1,0:T(8,128)(2,1)S(1)}, u32[]{:S(2)}, u32[]{:S(2)}) %collective-permute-start.3) | collective-permute-done | bytes 98336 | tf_op jit(solution)/shard_map/ppermute | solution.py:138
  (49 shorter events, 17.0 us)
Async XLA Ops:
  7.2 6.8 %copy-start = (bf16[128,4096]{1,0:T(8,128)(2,1)S(1)}, bf16[128,4096]{1,0:T(8,128)(2,1)}, u32[]{:S(2)}) copy-start(bf16[128,4096]{1,0:T(8,128)(2,1)} %param.6) | copy-start | bytes 3145732
  7.2 6.7 %copy-start.6 = (s32[128,4]{0,1:T(4,128)S(1)}, s32[128,4]{0,1:T(4,128)}, u32[]{:S(2)}) copy-start(s32[128,4]{0,1:T(4,128)} %param.8) | copy-start | bytes 6148
  7.2 7.0 %copy-start.7 = (f32[128,4]{0,1:T(4,128)S(1)}, f32[128,4]{0,1:T(4,128)}, u32[]{:S(2)}) copy-start(f32[128,4]{0,1:T(4,128)} %param.9) | copy-start | bytes 6148
  7.2 7.1 %copy-start.5 = (bf16[128,4096]{1,0:T(8,128)(2,1)S(1)}, bf16[128,4096]{1,0:T(8,128)(2,1)}, u32[]{:S(2)}) copy-start(bf16[128,4096]{1,0:T(8,128)(2,1)} %param.7) | copy-start | bytes 3145732
  9.3 13.4 %all-to-all-start = ((bf16[4,576,128]{2,1,0:T(8,128)(2,1)}), bf16[4,576,128]{2,1,0:T(8,128)(2,1)S(1)}, u32[]{:S(2)}, u32[]{:S(2)}) async-start(bf16[4,576,128]{2,1,0:T(8,128)(2,1)} %bitcast.47), calls=%async_computation | async-start | bytes 1179648 | tf_op jit(solution)/shard_map/all_to_all | solution.py:19
  13.9 52.0 %all-gather.2.cloned.1.call-start = ((), (), s32[]{:S(2)}) async-start(), calls=%async_computation.4 | async-start | bytes 5308416 | tf_op jit(solution)/shard_map/all_gather | solution.py:99
  22.6 1.7 copy-start.4
  24.4 67.7 %all-to-all-start.1 = ((bf16[32,16,2048]{2,1,0:T(8,128)(2,1)}), bf16[32,16,2048]{2,1,0:T(8,128)(2,1)S(1)}, u32[]{:S(2)}, u32[]{:S(2)}) async-start(bf16[32,16,2048]{2,1,0:T(8,128)(2,1)} %bitcast.5), calls=%async_computation.1 | async-start | bytes 4194304 | tf_op jit(solution)/shard_map/all_to_all | solution.py:19
  39.4 110.7 %reduce-scatter.2.cloned.1.call-start = ((), (), s32[]{:S(2)}) async-start(), calls=%async_computation.5 | async-start | bytes 1966080 | tf_op jit(solution)/shard_map/reduce_scatter | solution.py:131
  92.0 3.0 %copy-start.1 = (bf16[32,16,2048]{2,1,0:T(8,128)(2,1)}, bf16[32,16,2048]{2,1,0:T(8,128)(2,1)S(1)}, u32[]{:S(2)}) copy-start(bf16[32,16,2048]{2,1,0:T(8,128)(2,1)S(1)} %all-to-all-done.1.rows_ref) | copy-start | bytes 6291460
  92.0 3.1 %copy-start.2 = (bf16[768,2048]{1,0:T(8,128)(2,1)S(1)}, bf16[768,2048]{1,0:T(8,128)(2,1)}, u32[]{:S(2)}) copy-start(bf16[768,2048]{1,0:T(8,128)(2,1)} %reshape.53) | copy-start | bytes 9437188
  96.2 13.7 %collective-permute-start = (bf16[256,1152]{1,0:T(8,128)(2,1)S(1)}, bf16[256,1152]{1,0:T(8,128)(2,1)S(1)}, u32[]{:S(2)}, u32[]{:S(2)}) collective-permute-start(bf16[256,1152]{1,0:T(8,128)(2,1)S(1)} %pad_maximum_fusion), channel_id=1, source_target_pairs={{0,4},{4,0},{1,5},{5,1},{2,6},{6,2},{3,7},{7,3},{8,12},{12,8},{9,1... | collective-permute-start | bytes 1769480 | tf_op jit(solution)/shard_map/ppermute | solution.py:23
  102.1 4.0 %collective-permute-start.1 = (bf16[1024,256]{1,0:T(8,128)(2,1)}, bf16[1024,256]{1,0:T(8,128)(2,1)S(1)}, u32[]{:S(2)}, u32[]{:S(2)}) collective-permute-start(bf16[1024,256]{1,0:T(8,128)(2,1)} %get-tuple-element.28), channel_id=1, source_target_pairs={{0,32},{32,0},{1,33},{33,1},{2,34},{34,2},{3,35},{35,3},{4,36},{36... | collective-permute-start | bytes 1572872 | tf_op jit(solution)/shard_map/ppermute | solution.py:23
  109.9 2.9 %copy-start.3 = (bf16[768,2048]{1,0:T(8,128)(2,1)S(1)}, bf16[768,2048]{1,0:T(8,128)(2,1)}, u32[]{:S(2)}) copy-start(bf16[768,2048]{1,0:T(8,128)(2,1)} %reshape.53) | copy-start | bytes 9437188
  110.5 4.2 %copy-start.8 = (bf16[1024,256]{1,0:T(8,128)(2,1)S(1)}, bf16[1024,256]{1,0:T(8,128)(2,1)}, u32[]{:S(2)}) copy-start(bf16[1024,256]{1,0:T(8,128)(2,1)} %get-tuple-element.31) | copy-start | bytes 1572868
  110.6 4.2 %collective-permute-start.2 = (bf16[256,768]{1,0:T(8,128)(2,1)S(1)}, bf16[256,768]{1,0:T(8,128)(2,1)S(1)}, u32[]{:S(2)}, u32[]{:S(2)}) collective-permute-start(bf16[256,768]{1,0:T(8,128)(2,1)S(1)} %pad_maximum_fusion.2), channel_id=1, source_target_pairs={{0,32},{32,0},{1,33},{33,1},{2,34},{34,2},{3,35},{35,3},{4,36},{36... | collective-permute-start | bytes 1179656 | tf_op jit(solution)/shard_map/ppermute | solution.py:23
  117.0 43.4 %all-to-all-start.2 = ((bf16[32,8,2048]{2,1,0:T(8,128)(2,1)}), bf16[32,8,2048]{2,1,0:T(8,128)(2,1)S(1)}, u32[]{:S(2)}, u32[]{:S(2)}) async-start(bf16[32,8,2048]{2,1,0:T(8,128)(2,1)} %bitcast.16), calls=%async_computation.2 | async-start | bytes 2097152 | tf_op jit(solution)/shard_map/all_to_all | solution.py:19
  151.1 9.3 %collective-permute-start.5 = (bf16[128,384]{1,0:T(8,128)(2,1)S(1)}, bf16[128,384]{1,0:T(8,128)(2,1)S(1)}, u32[]{:S(2)}, u32[]{:S(2)}) collective-permute-start(bf16[128,384]{1,0:T(8,128)(2,1)S(1)} %get-tuple-element.44), channel_id=1, source_target_pairs={{0,260},{4,256},{256,4},{260,0},{1,261},{5,257},{257,5},{261,1},{2... | collective-permute-start | bytes 294920 | tf_op jit(solution)/shard_map/ppermute | solution.py:138
  155.2 6.5 %collective-permute-start.4 = (bf16[128,384]{1,0:T(8,128)(2,1)S(1)}, bf16[128,384]{1,0:T(8,128)(2,1)S(1)}, u32[]{:S(2)}, u32[]{:S(2)}) collective-permute-start(bf16[128,384]{1,0:T(8,128)(2,1)S(1)} %get-tuple-element.45), channel_id=1, source_target_pairs={{0,256},{4,260},{256,0},{260,4},{1,257},{5,261},{257,1},{261,5},{2... | collective-permute-start | bytes 294920 | tf_op jit(solution)/shard_map/ppermute | solution.py:138
  157.5 6.5 %collective-permute-start.3 = (bf16[128,384]{1,0:T(8,128)(2,1)S(1)}, bf16[128,384]{1,0:T(8,128)(2,1)S(1)}, u32[]{:S(2)}, u32[]{:S(2)}) collective-permute-start(bf16[128,384]{1,0:T(8,128)(2,1)S(1)} %get-tuple-element.46), channel_id=1, source_target_pairs={{0,4},{4,0},{256,260},{260,256},{1,5},{5,1},{257,261},{261,257},{2... | collective-permute-start | bytes 294920 | tf_op jit(solution)/shard_map/ppermute | solution.py:138
Sparse Core Ops, SparseCore 0:
  24.5 41.4 all-gather.1
  117.2 32.9 reduce-scatter.1

commit v8 on v7

--- a/solution.py
+++ b/solution.py
@@ -73,6 +73,63 @@
     return out.reshape(n_zl * n_yl, shape[2], LANE)
 
 
+def order_kernel(w_ref, gu_ref, down_ref):
+    n_zl, n_yl, units, lanes = w_ref.shape
+    hid = units // 3
+    for i in range(n_zl):
+        cols = slice(i * lanes, (i + 1) * lanes)
+        for j in range(n_yl):
+            gu_ref[2 * j * hid : 2 * (j + 1) * hid, cols] = w_ref[i, j, : 2 * hid, :]
+            down_ref[j * hid : (j + 1) * hid, cols] = w_ref[i, j, 2 * hid :, :]
+
+
+def order_weights(w_all):
+    n_xc, n_zl, n_yl, units, lanes = w_all.shape
+    hid = units // 3
+    gu_rows, down_rows, cols = 2 * hid * n_yl, hid * n_yl, n_zl * lanes
+    return pl.pallas_call(
+        order_kernel,
+        grid=(n_xc,),
+        in_specs=[pl.BlockSpec((None, n_zl, n_yl, units, lanes), lambda k: (k, 0, 0, 0, 0))],
+        out_specs=[pl.BlockSpec((gu_rows, cols), lambda k: (0, k)), pl.BlockSpec((down_rows, cols), lambda k: (0, k))],
+        out_shape=[
+            jax.ShapeDtypeStruct((gu_rows, n_xc * cols), w_all.dtype),
+            jax.ShapeDtypeStruct((down_rows, n_xc * cols), w_all.dtype),
+        ],
+        name="order_weights",
+    )(w_all)
+
+
+def rows_kernel(n_zl, tokens_ref, dy_ref, slot_ref, gate_ref, out_ref):
+    n_win, n_yl, n_zh, _, half = out_ref.shape
+    n_tok = tokens_ref.shape[0]
+    n_xc = half // (n_zl * LANE)
+    positions = lax.broadcasted_iota(jnp.int32, (CAP, n_tok), 0)
+    for e in range(n_win):
+        picked = jnp.broadcast_to(slot_ref[e : e + 1, :], (CAP, n_tok)) == positions
+        gate = jnp.sum(jnp.where(picked, gate_ref[e : e + 1, :], 0.0), axis=1, keepdims=True)
+        one_hot = picked.astype(jnp.float32).astype(tokens_ref.dtype)
+        x = jnp.dot(one_hot, tokens_ref[...], preferred_element_type=jnp.float32)
+        g = jnp.dot(one_hot, dy_ref[...], preferred_element_type=jnp.float32) * gate
+        both = jnp.concatenate([x, g], axis=0).astype(out_ref.dtype)
+        for h in range(n_yl):
+            for xc in range(n_xc):
+                for zl in range(n_zl):
+                    src = ((zl * n_xc + xc) * n_yl + h) * LANE
+                    dst = (xc * n_zl + zl) * LANE
+                    piece = both[:, src : src + LANE]
+                    for zh in range(n_zh):
+                        out_ref[e, h, zh, :, dst : dst + LANE] = piece
+
+
+def select_rows(tokens, dy, slot_t, gate_t, n_zl, n_yl, n_zh):
+    n_win, width = slot_t.shape[0], tokens.shape[1]
+    shape = (n_win, n_yl, n_zh, 2 * CAP, width // n_yl)
+    return pl.pallas_call(
+        lambda *refs: rows_kernel(n_zl, *refs), out_shape=jax.ShapeDtypeStruct(shape, tokens.dtype), name="select_rows"
+    )(tokens, dy, slot_t, gate_t)
+
+
 def on_device(tokens, output_gradient, slot, gate_weight, gate_up_weight, down_weight):
     n_win = slot.shape[1]
     width = tokens.shape[1]
@@ -80,18 +137,9 @@
     hid = down_weight.shape[1]
     n_yl, n_zh, n_c = lax.axis_size("yl"), lax.axis_size("zh"), lax.axis_size("c")
 
-    positions = jnp.arange(CAP, dtype=jnp.int32)
-    selector = jnp.transpose(slot)[:, None, :] == positions[None, :, None]
-    picked = selector.astype(jnp.bfloat16)
-    rows_x = jnp.einsum("ect,td->ecd", picked, tokens, preferred_element_type=jnp.float32).astype(jnp.bfloat16)
-    rows_dy = jnp.einsum("ect,td->ecd", picked, output_gradient, preferred_element_type=jnp.float32)
-    gate = jnp.sum(jnp.where(selector, jnp.transpose(gate_weight)[:, None, :], 0.0), axis=2)
-    rows_g = (rows_dy * gate[..., None]).astype(jnp.bfloat16)
     n_zl = lax.axis_size("zl")
     n_xc = n_half // n_zl
-    rows = jnp.concatenate([rows_x, rows_g], axis=1).reshape(n_win, 2 * CAP, n_zl, n_xc, n_yl, LANE)
-    rows = jnp.transpose(rows, (0, 4, 1, 3, 2, 5)).reshape(n_win, n_yl, 1, 2 * CAP, n_half * LANE)
-    rows = jnp.broadcast_to(rows, (n_win, n_yl, n_zh, 2 * CAP, n_half * LANE))
+    rows = select_rows(tokens, output_gradient, jnp.transpose(slot), jnp.transpose(gate_weight), n_zl, n_yl, n_zh)
     rows = rows.reshape(-1, 2 * CAP, n_half * LANE)
 
     w_pair = a2a(pack_weights(gate_up_weight[0], down_weight[0], n_zl, n_yl), ("zl", "yl"))
@@ -99,8 +147,7 @@
     w_all = lax.all_gather(w_pair.reshape(-1, LANE), ("x", "c"), axis=0, tiled=True)
     w_all = w_all.reshape(n_xc, n_zl, n_yl, 3 * hid, LANE)
     gu_cols = 2 * n_yl * hid
-    w_gu_t = jnp.transpose(w_all[:, :, :, : 2 * hid], (2, 3, 0, 1, 4)).reshape(gu_cols, n_half * LANE)
-    w_down_t = jnp.transpose(w_all[:, :, :, 2 * hid :], (2, 3, 0, 1, 4)).reshape(n_yl * hid, n_half * LANE)
+    w_gu_t, w_down_t = order_weights(w_all)
     recv, w_gu_t, w_down_t = lax.optimization_barrier((a2a(rows, EXPERT), w_gu_t, w_down_t))
     n_src = recv.shape[0]
     x_mat = recv[:, :CAP].reshape(n_src * CAP, n_half * LANE)
@@ -148,6 +195,8 @@
 
     back = jnp.sum(back.reshape(n_win, n_yl, n_zh, CAP, n_xc, n_zl, LANE).astype(jnp.float32), axis=2)
     back = jnp.transpose(back, (0, 2, 4, 3, 1, 5)).reshape(n_win, CAP, width)
+    positions = jnp.arange(CAP, dtype=jnp.int32)
+    selector = jnp.transpose(slot)[:, None, :] == positions[None, :, None]
     grad_tokens = jnp.einsum("ect,ecd->td", selector.astype(jnp.float32), back).astype(jnp.bfloat16)
     return grad_tokens, grad_gu
 

time: 177 us -> 177 us (level)
  local copies, waits for them, and re-layouts: 25.9 us -> 2.46 us
  waiting for transfers between devices: 68 us -> 81.1 us
  Pallas kernels: 5.85 us -> 17 us
    all_to_all x3, waiting for transfers between devices: 11.5 us -> 23.5 us  [a2a(): return lax.all_to_all(v, axes, split_axis=0, concat_axis=0, tiled=True)]
    transpose x4 -> x0, local copies, waits for them, and re-layouts: 11.4 us -> none  [the longest x2 7.11 us: on_device(): jnp.transpose(w_all[:, :, :, :2 * hid], (2, 3, 0, 1, 4))]
    pallas_call x0 -> x2, Pallas kernels: none -> 11.3 us  [the longest x1 7.11 us: order_weights(): pl.pallas_call(order_kernel, grid=(n_xc,), in_specs=[pl.BlockSpec((None,...]
    reshape x4 -> x0, local copies, waits for them, and re-layouts: 10.7 us -> none  [the longest x1 6.12 us: on_device(): jnp.transpose(w_all[:, :, :, :2 * hid], (2, 3, 0, 1, 4))]
    broadcast_in_dim x2 -> x0, local copies, waits for them, and re-layouts: 2.08 us -> none  [on_device(): rows = jnp.broadcast_to(rows, (n_win, n_yl, n_zh, 2 * CAP, n_half * LANE))]
  transfers between devices with their start and end apart: 11 -> 11, of which waited for: 8 -> 8; matrix products, arithmetic and copies ran while one was open for 15% -> 2% of each run, Pallas kernels for 2% -> 9%
where the time goes in v8:
time: 177 us; the launch traced here: 174 us
  waiting for transfers between devices  81.1 us (46%)
  starting transfers between devices  47.6 us (27%)
  Pallas kernels  17 us (10%)
  between operations  14.2 us (8%)
  matrix products  9.62 us (5%)
  other arithmetic  2.47 us (1%)
  local copies, waits for them, and re-layouts  2.46 us (1%)
    all_to_all x3, starting transfers between devices, a2a(): return lax.all_to_all(v, axes, split_axis=0, concat_axis=0, tiled=True)  32.3 us
    all_gather x1, waiting for transfers between devices, on_device(): lax.all_gather(w_pair.reshape(-1, LANE), ('x', 'c'), axis=0, tiled=True)  26.5 us
    all_to_all x3, waiting for transfers between devices, a2a(): return lax.all_to_all(v, axes, split_axis=0, concat_axis=0, tiled=True)  23.5 us
    reduce_scatter x1, waiting for transfers between devices, on_device(): summed = lax.psum_scatter(pgu, 'x', scatter_dimension=0, tiled=True)  20.5 us
    ppermute x3, starting transfers between devices, flipped(): lax.ppermute(v, ('zl', 'yl'), [(i, i ^ flip) for i in range(n_zl * n_yl)])  9.21 us
    pallas_call x1, Pallas kernels, order_weights(): pl.pallas_call(order_kernel, grid=(n_xc,), in_specs=[pl.BlockSpec((None,...  7.11 us
    ppermute x3, starting transfers between devices, swap(): return lax.ppermute(v, axis, [(0, 1), (1, 0)])  6.04 us
    ppermute x3, waiting for transfers between devices, swap(): return lax.ppermute(v, axis, [(0, 1), (1, 0)])  5.85 us
  transfers between devices with their start and end apart: 11, of which 8 were waited for; matrix products, arithmetic and copies ran while one was open for 2% of the time, Pallas kernels for 9%

profile of v8, /device:TPU:6, one launch (start us, length us, event | category | flops | bytes accessed | tf_op | source)
XLA Modules:
  0.0 174.4 jit_solution(6617126885206461485)
XLA Ops:
  7.2 1.9 %pack_weights.1 = bf16[2,2,576,128]{3,2,1,0:T(8,128)(2,1)} custom-call(bf16[256,384]{1,0:T(8,128)(2,1)} %bitcast.36, bf16[192,256]{1,0:T(8,128)(2,1)} %bitcast.37), custom_call_target="tpu_custom_call" | custom-call | tf_op jit(solution)/shard_map/pack_weights/pallas_call | solution.py:70
  9.1 4.7 %all-to-all-start = ((bf16[4,576,128]{2,1,0:T(8,128)(2,1)}), bf16[4,576,128]{2,1,0:T(8,128)(2,1)S(1)}, u32[]{:S(2)}, u32[]{:S(2)}) async-start(bf16[4,576,128]{2,1,0:T(8,128)(2,1)} %bitcast.34), calls=%async_computation | async-start | bytes 1179648 | tf_op jit(solution)/shard_map/all_to_all | solution.py:19
  13.7 4.1 %select_rows.1 = bf16[4,2,4,16,2048]{4,3,2,1,0:T(8,128)(2,1)} custom-call(bf16[128,4096]{1,0:T(8,128)(2,1)} %refs_0_.1, bf16[128,4096]{1,0:T(8,128)(2,1)} %refs_1_.1, s32[4,128]{1,0:T(4,128)} %bitcast.38, f32[4,128]{1,0:T(4,128)} %bitcast.40), custom_call_target="tpu_custom_call" | custom-call | tf_op jit(solution)/shard_map/select_rows/pallas_call | solution.py:128
  17.9 4.6 %all-to-all-done = bf16[4,576,128]{2,1,0:T(8,128)(2,1)S(1)} async-done(((bf16[4,576,128]{2,1,0:T(8,128)(2,1)}), bf16[4,576,128]{2,1,0:T(8,128)(2,1)S(1)}, u32[]{:S(2)}, u32[]{:S(2)}) %all-to-all-start) | async-done | bytes 589856 | tf_op jit(solution)/shard_map/all_to_all | solution.py:19
  23.3 15.0 %all-to-all-start.1 = ((bf16[32,16,2048]{2,1,0:T(8,128)(2,1)}), bf16[32,16,2048]{2,1,0:T(8,128)(2,1)S(1)}, u32[]{:S(2)}, u32[]{:S(2)}) async-start(bf16[32,16,2048]{2,1,0:T(8,128)(2,1)} %bitcast.30), calls=%async_computation.1 | async-start | bytes 4194304 | tf_op jit(solution)/shard_map/all_to_all | solution.py:19
  38.4 26.5 %all-gather.2.cloned.1.call-done = bf16[18432,128]{1,0:T(8,128)(2,1)} async-done(((bf16[2304,128]{1,0:T(8,128)(2,1)}), bf16[18432,128]{1,0:T(8,128)(2,1)}) %all-gather.2.cloned.1.call-update) | async-done | bytes 4718608 | tf_op jit(solution)/shard_map/all_gather | solution.py:147
  64.9 7.1 %order_weights.1 = (bf16[768,2048]{1,0:T(8,128)(2,1)}, bf16[384,2048]{1,0:T(8,128)(2,1)}) custom-call(bf16[8,2,2,576,128]{4,3,2,1,0:T(8,128)(2,1)} %bitcast.31), custom_call_target="tpu_custom_call" | custom-call | tf_op jit(solution)/shard_map/order_weights/pallas_call | solution.py:90
  72.0 19.0 %all-to-all-done.1.rows_ref = bf16[32,16,2048]{2,1,0:T(8,128)(2,1)S(1)} async-done(((bf16[32,16,2048]{2,1,0:T(8,128)(2,1)}), bf16[32,16,2048]{2,1,0:T(8,128)(2,1)S(1)}, u32[]{:S(2)}, u32[]{:S(2)}) %all-to-all-start.1) | async-done | bytes 2097184 | tf_op jit(solution)/shard_map/all_to_all | solution.py:19
  91.0 2.9 %convolution_convert_fusion.3 = bf16[256,384]{1,0:T(8,128)(2,1)S(1)} fusion(bf16[384,2048]{1,0:T(8,128)(2,1)} %get-tuple-element.28, bf16[32,16,2048]{2,1,0:T(8,128)(2,1)S(1)} %all-to-all-done.1.rows_ref), kind=kOutput, calls=%fused_computation.7 | convolution fusion | flops 402751488 | bytes 2818048 | tf_op jit(solution)/shard_map/dot_general | solution.py:15
  95.2 2.1 %collective-permute-start = (bf16[256,1152]{1,0:T(8,128)(2,1)S(1)}, bf16[256,1152]{1,0:T(8,128)(2,1)S(1)}, u32[]{:S(2)}, u32[]{:S(2)}) collective-permute-start(bf16[256,1152]{1,0:T(8,128)(2,1)S(1)} %pad_maximum_fusion), channel_id=1, source_target_pairs={{0,4},{4,0},{1,5},{5,1},{2,6},{6,2},{3,7},{7,3},{8,12},{12,8},{9,1... | collective-permute-start | bytes 1769480 | tf_op jit(solution)/shard_map/ppermute | solution.py:23
  97.3 3.8 %split_rows.1 = (bf16[1024,256]{1,0:T(8,128)(2,1)}, bf16[1024,256]{1,0:T(8,128)(2,1)}) custom-call(s32[1]{0:T(128)} %bitcast.10.core_ref, bf16[32,16,2048]{2,1,0:T(8,128)(2,1)} %copy-done), custom_call_target="tpu_custom_call" | custom-call | tf_op jit(solution)/shard_map/split_rows/pallas_call | solution.py:44
  101.1 1.9 %collective-permute-start.1 = (bf16[1024,256]{1,0:T(8,128)(2,1)}, bf16[1024,256]{1,0:T(8,128)(2,1)S(1)}, u32[]{:S(2)}, u32[]{:S(2)}) collective-permute-start(bf16[1024,256]{1,0:T(8,128)(2,1)} %get-tuple-element.32), channel_id=1, source_target_pairs={{0,32},{32,0},{1,33},{33,1},{2,34},{34,2},{3,35},{35,3},{4,36},{36... | collective-permute-start | bytes 1572872 | tf_op jit(solution)/shard_map/ppermute | solution.py:23
  103.0 2.1 %collective-permute-done.1 = bf16[1024,256]{1,0:T(8,128)(2,1)S(1)} collective-permute-done((bf16[1024,256]{1,0:T(8,128)(2,1)}, bf16[1024,256]{1,0:T(8,128)(2,1)S(1)}, u32[]{:S(2)}, u32[]{:S(2)}) %collective-permute-start.1) | collective-permute-done | bytes 524320 | tf_op jit(solution)/shard_map/ppermute | solution.py:23
  105.1 3.8 %collective-permute-done = bf16[256,1152]{1,0:T(8,128)(2,1)S(1)} collective-permute-done((bf16[256,1152]{1,0:T(8,128)(2,1)S(1)}, bf16[256,1152]{1,0:T(8,128)(2,1)S(1)}, u32[]{:S(2)}, u32[]{:S(2)}) %collective-permute-start) | collective-permute-done | bytes 589856 | tf_op jit(solution)/shard_map/ppermute | solution.py:23
  109.5 2.1 %collective-permute-start.2 = (bf16[256,768]{1,0:T(8,128)(2,1)S(1)}, bf16[256,768]{1,0:T(8,128)(2,1)S(1)}, u32[]{:S(2)}, u32[]{:S(2)}) collective-permute-start(bf16[256,768]{1,0:T(8,128)(2,1)S(1)} %pad_maximum_fusion.1), channel_id=1, source_target_pairs={{0,32},{32,0},{1,33},{33,1},{2,34},{34,2},{3,35},{35,3},{4,36},{36... | collective-permute-start | bytes 1179656 | tf_op jit(solution)/shard_map/ppermute | solution.py:23
  111.6 2.0 %convolution_convert_fusion = bf16[256,2048]{1,0:T(8,128)(2,1)} fusion(bf16[256,768]{1,0:T(8,128)(2,1)S(1)} %pad_maximum_fusion.1, bf16[768,2048]{1,0:T(8,128)(2,1)S(1)} %copy-done.4), kind=kOutput, calls=%fused_computation.2 | convolution fusion | flops 805830656 | bytes 4587520 | tf_op jit(solution)/shard_map/dot_general | solution.py:173
  113.5 2.2 %convolution_convert_fusion.1 = bf16[1024,768]{1,0:T(8,128)(2,1)} fusion(bf16[1024,256]{1,0:T(8,128)(2,1)S(1)} %collective-permute-done.1, bf16[1024,256]{1,0:T(8,128)(2,1)S(1)} %copy-done.5, bf16[256,768]{1,0:T(8,128)(2,1)S(1)} %collective-permute-done.2, bf16[256,192]{1,0:T(8,128)(2,1)S(1)} %get-tuple-element.43, ...), kind=kOutput, calls=%fused_computation.4 | convolution fusion | flops 812122112 | bytes 3407872 | tf_op jit(solution)/shard_map/dot_general | solution.py:176
  115.8 12.6 %all-to-all-start.2 = ((bf16[32,8,2048]{2,1,0:T(8,128)(2,1)}), bf16[32,8,2048]{2,1,0:T(8,128)(2,1)S(1)}, u32[]{:S(2)}, u32[]{:S(2)}) async-start(bf16[32,8,2048]{2,1,0:T(8,128)(2,1)} %bitcast.11), calls=%async_computation.2 | async-start | bytes 2097152 | tf_op jit(solution)/shard_map/all_to_all | solution.py:19
  128.4 20.5 %reduce-scatter.2.cloned.1.call-done = bf16[256,768]{1,0:T(8,128)(2,1)} async-done(((bf16[1024,768]{1,0:T(8,128)(2,1)}), bf16[256,768]{1,0:T(8,128)(2,1)}) %reduce-scatter.2.cloned.1.call-update) | async-done | bytes 393232 | tf_op jit(solution)/shard_map/reduce_scatter | solution.py:178
  149.9 3.0 %collective-permute-start.3 = (bf16[128,384]{1,0:T(8,128)(2,1)S(1)}, bf16[128,384]{1,0:T(8,128)(2,1)S(1)}, u32[]{:S(2)}, u32[]{:S(2)}) collective-permute-start(bf16[128,384]{1,0:T(8,128)(2,1)S(1)} %get-tuple-element.50), channel_id=1, source_target_pairs={{0,4},{4,0},{256,260},{260,256},{1,5},{5,1},{257,261},{261,257},{2... | collective-permute-start | bytes 294920 | tf_op jit(solution)/shard_map/ppermute | solution.py:185
  152.9 3.5 %collective-permute-start.4 = (bf16[128,384]{1,0:T(8,128)(2,1)S(1)}, bf16[128,384]{1,0:T(8,128)(2,1)S(1)}, u32[]{:S(2)}, u32[]{:S(2)}) collective-permute-start(bf16[128,384]{1,0:T(8,128)(2,1)S(1)} %get-tuple-element.49), channel_id=1, source_target_pairs={{0,256},{4,260},{256,0},{260,4},{1,257},{5,261},{257,1},{261,5},{2... | collective-permute-start | bytes 294920 | tf_op jit(solution)/shard_map/ppermute | solution.py:185
  156.4 2.7 %collective-permute-start.5 = (bf16[128,384]{1,0:T(8,128)(2,1)S(1)}, bf16[128,384]{1,0:T(8,128)(2,1)S(1)}, u32[]{:S(2)}, u32[]{:S(2)}) collective-permute-start(bf16[128,384]{1,0:T(8,128)(2,1)S(1)} %get-tuple-element.48), channel_id=1, source_target_pairs={{0,260},{4,256},{256,4},{260,0},{1,261},{5,257},{257,5},{261,1},{2... | collective-permute-start | bytes 294920 | tf_op jit(solution)/shard_map/ppermute | solution.py:185
  159.4 4.4 %collective-permute-done.5 = bf16[128,384]{1,0:T(8,128)(2,1)S(1)} collective-permute-done((bf16[128,384]{1,0:T(8,128)(2,1)S(1)}, bf16[128,384]{1,0:T(8,128)(2,1)S(1)}, u32[]{:S(2)}, u32[]{:S(2)}) %collective-permute-start.5) | collective-permute-done | bytes 98336 | tf_op jit(solution)/shard_map/ppermute | solution.py:185
  164.5 1.5 fusion
  (31 shorter events, 6.3 us)
Async XLA Ops:
  9.1 13.4 %all-to-all-start = ((bf16[4,576,128]{2,1,0:T(8,128)(2,1)}), bf16[4,576,128]{2,1,0:T(8,128)(2,1)S(1)}, u32[]{:S(2)}, u32[]{:S(2)}) async-start(bf16[4,576,128]{2,1,0:T(8,128)(2,1)} %bitcast.34), calls=%async_computation | async-start | bytes 1179648 | tf_op jit(solution)/shard_map/all_to_all | solution.py:19
  13.7 51.2 %all-gather.2.cloned.1.call-start = ((), (), s32[]{:S(2)}) async-start(), calls=%async_computation.4 | async-start | bytes 5308416 | tf_op jit(solution)/shard_map/all_gather | solution.py:147
  22.4 0.8 copy-start.1
  23.3 67.7 %all-to-all-start.1 = ((bf16[32,16,2048]{2,1,0:T(8,128)(2,1)}), bf16[32,16,2048]{2,1,0:T(8,128)(2,1)S(1)}, u32[]{:S(2)}, u32[]{:S(2)}) async-start(bf16[32,16,2048]{2,1,0:T(8,128)(2,1)} %bitcast.30), calls=%async_computation.1 | async-start | bytes 4194304 | tf_op jit(solution)/shard_map/all_to_all | solution.py:19
  38.3 110.6 %reduce-scatter.2.cloned.1.call-start = ((), (), s32[]{:S(2)}) async-start(), calls=%async_computation.5 | async-start | bytes 1966080 | tf_op jit(solution)/shard_map/reduce_scatter | solution.py:178
  91.0 3.0 %copy-start = (bf16[32,16,2048]{2,1,0:T(8,128)(2,1)}, bf16[32,16,2048]{2,1,0:T(8,128)(2,1)S(1)}, u32[]{:S(2)}) copy-start(bf16[32,16,2048]{2,1,0:T(8,128)(2,1)S(1)} %all-to-all-done.1.rows_ref) | copy-start | bytes 6291460
  91.0 3.1 %copy-start.3 = (bf16[768,2048]{1,0:T(8,128)(2,1)S(1)}, bf16[768,2048]{1,0:T(8,128)(2,1)}, u32[]{:S(2)}) copy-start(bf16[768,2048]{1,0:T(8,128)(2,1)} %get-tuple-element.27) | copy-start | bytes 9437188
  95.2 13.7 %collective-permute-start = (bf16[256,1152]{1,0:T(8,128)(2,1)S(1)}, bf16[256,1152]{1,0:T(8,128)(2,1)S(1)}, u32[]{:S(2)}, u32[]{:S(2)}) collective-permute-start(bf16[256,1152]{1,0:T(8,128)(2,1)S(1)} %pad_maximum_fusion), channel_id=1, source_target_pairs={{0,4},{4,0},{1,5},{5,1},{2,6},{6,2},{3,7},{7,3},{8,12},{12,8},{9,1... | collective-permute-start | bytes 1769480 | tf_op jit(solution)/shard_map/ppermute | solution.py:23
  101.1 4.0 %collective-permute-start.1 = (bf16[1024,256]{1,0:T(8,128)(2,1)}, bf16[1024,256]{1,0:T(8,128)(2,1)S(1)}, u32[]{:S(2)}, u32[]{:S(2)}) collective-permute-start(bf16[1024,256]{1,0:T(8,128)(2,1)} %get-tuple-element.32), channel_id=1, source_target_pairs={{0,32},{32,0},{1,33},{33,1},{2,34},{34,2},{3,35},{35,3},{4,36},{36... | collective-permute-start | bytes 1572872 | tf_op jit(solution)/shard_map/ppermute | solution.py:23
  108.8 2.7 %copy-start.4 = (bf16[768,2048]{1,0:T(8,128)(2,1)S(1)}, bf16[768,2048]{1,0:T(8,128)(2,1)}, u32[]{:S(2)}) copy-start(bf16[768,2048]{1,0:T(8,128)(2,1)} %get-tuple-element.27) | copy-start | bytes 9437188
  109.5 4.1 %copy-start.5 = (bf16[1024,256]{1,0:T(8,128)(2,1)S(1)}, bf16[1024,256]{1,0:T(8,128)(2,1)}, u32[]{:S(2)}) copy-start(bf16[1024,256]{1,0:T(8,128)(2,1)} %get-tuple-element.35) | copy-start | bytes 1572868
  109.5 4.1 %collective-permute-start.2 = (bf16[256,768]{1,0:T(8,128)(2,1)S(1)}, bf16[256,768]{1,0:T(8,128)(2,1)S(1)}, u32[]{:S(2)}, u32[]{:S(2)}) collective-permute-start(bf16[256,768]{1,0:T(8,128)(2,1)S(1)} %pad_maximum_fusion.1), channel_id=1, source_target_pairs={{0,32},{32,0},{1,33},{33,1},{2,34},{34,2},{3,35},{35,3},{4,36},{36... | collective-permute-start | bytes 1179656 | tf_op jit(solution)/shard_map/ppermute | solution.py:23
  115.8 43.4 %all-to-all-start.2 = ((bf16[32,8,2048]{2,1,0:T(8,128)(2,1)}), bf16[32,8,2048]{2,1,0:T(8,128)(2,1)S(1)}, u32[]{:S(2)}, u32[]{:S(2)}) async-start(bf16[32,8,2048]{2,1,0:T(8,128)(2,1)} %bitcast.11), calls=%async_computation.2 | async-start | bytes 2097152 | tf_op jit(solution)/shard_map/all_to_all | solution.py:19
  128.4 36.1 %copy-start.2 = (s32[128,4]{0,1:T(4,128)S(1)}, s32[128,4]{0,1:T(4,128)}, u32[]{:S(2)}) copy-start(s32[128,4]{0,1:T(4,128)} %param.8) | copy-start | bytes 6148
  149.9 9.3 %collective-permute-start.3 = (bf16[128,384]{1,0:T(8,128)(2,1)S(1)}, bf16[128,384]{1,0:T(8,128)(2,1)S(1)}, u32[]{:S(2)}, u32[]{:S(2)}) collective-permute-start(bf16[128,384]{1,0:T(8,128)(2,1)S(1)} %get-tuple-element.50), channel_id=1, source_target_pairs={{0,4},{4,0},{256,260},{260,256},{1,5},{5,1},{257,261},{261,257},{2... | collective-permute-start | bytes 294920 | tf_op jit(solution)/shard_map/ppermute | solution.py:185
  152.9 6.5 %collective-permute-start.4 = (bf16[128,384]{1,0:T(8,128)(2,1)S(1)}, bf16[128,384]{1,0:T(8,128)(2,1)S(1)}, u32[]{:S(2)}, u32[]{:S(2)}) collective-permute-start(bf16[128,384]{1,0:T(8,128)(2,1)S(1)} %get-tuple-element.49), channel_id=1, source_target_pairs={{0,256},{4,260},{256,0},{260,4},{1,257},{5,261},{257,1},{261,5},{2... | collective-permute-start | bytes 294920 | tf_op jit(solution)/shard_map/ppermute | solution.py:185
  156.4 7.4 %collective-permute-start.5 = (bf16[128,384]{1,0:T(8,128)(2,1)S(1)}, bf16[128,384]{1,0:T(8,128)(2,1)S(1)}, u32[]{:S(2)}, u32[]{:S(2)}) collective-permute-start(bf16[128,384]{1,0:T(8,128)(2,1)S(1)} %get-tuple-element.48), channel_id=1, source_target_pairs={{0,260},{4,256},{256,4},{260,0},{1,261},{5,257},{257,5},{261,1},{2... | collective-permute-start | bytes 294920 | tf_op jit(solution)/shard_map/ppermute | solution.py:185
Sparse Core Ops, SparseCore 0:
  23.4 41.4 all-gather.1
  115.9 32.9 reduce-scatter.1

commit v9 on v8

--- a/solution.py
+++ b/solution.py
@@ -2,7 +2,6 @@
 import jax.numpy as jnp
 from jax import lax
 from jax.experimental import pallas as pl
-from jax.experimental.pallas import tpu as pltpu
 from jax.sharding import Mesh, PartitionSpec as P
 
 FINE = ("zl", "x", "c", "yh", "yl", "zh")
@@ -21,37 +20,6 @@
 
 def swap(v, axis):
     return lax.ppermute(v, axis, [(0, 1), (1, 0)])
-
-
-def split_kernel(core_ref, rows_ref, kept_ref, given_ref):
-    n_src, _, depth = rows_ref.shape
-    x = rows_ref[:, :CAP, :].reshape(n_src * CAP, depth)
-    low, high = x[:, : depth // 2].T, x[:, depth // 2 :].T
-
-    @pl.when(core_ref[0] == 0)
-    def _():
-        kept_ref[...], given_ref[...] = low, high
-
-    @pl.when(core_ref[0] != 0)
-    def _():
-        kept_ref[...], given_ref[...] = high, low
-
-
-def split_rows(core, recv, depth):
-    n_src, rows, width = recv.shape
-    out = jax.ShapeDtypeStruct((width // 2, n_src * CAP), recv.dtype)
-    out_spec = pl.BlockSpec((depth // 2, n_src * CAP), lambda k: (k, 0))
-    return pl.pallas_call(
-        split_kernel,
-        grid=(width // depth,),
-        in_specs=[
-            pl.BlockSpec(memory_space=pltpu.SMEM),
-            pl.BlockSpec((n_src, rows, depth), lambda k: (0, 0, k)),
-        ],
-        out_specs=[out_spec, out_spec],
-        out_shape=[out, out],
-        name="split_rows",
-    )(core.reshape(1), recv)
 
 
 def pack_kernel(gu_ref, down_ref, out_ref):
@@ -135,7 +103,7 @@
     width = tokens.shape[1]
     n_half = width // (2 * LANE)
     hid = down_weight.shape[1]
-    n_yl, n_zh, n_c = lax.axis_size("yl"), lax.axis_size("zh"), lax.axis_size("c")
+    n_yl, n_zh = lax.axis_size("yl"), lax.axis_size("zh")
 
     n_zl = lax.axis_size("zl")
     n_xc = n_half // n_zl
@@ -157,11 +125,7 @@
         [f32_dot(x_mat, w_gu_t, ((1,), (1,))), f32_dot(g_mat, w_down_t, ((1,), (1,)))], axis=1
     ).astype(jnp.bfloat16)
 
-    part, recv = lax.optimization_barrier((part, recv))
-    xt_kept, xt_given = split_rows(lax.axis_index("c"), recv, n_c * n_zl * LANE)
-    part_other, xt_kept, xt_got = lax.optimization_barrier((swap(part, "yl"), xt_kept, swap(xt_given, "c")))
-
-    total = part.astype(jnp.float32) + part_other.astype(jnp.float32)
+    total = part.astype(jnp.float32) + swap(part, "yl").astype(jnp.float32)
     dgu = []
     for i in range(n_yl):
         pre, up = total[:, 2 * i * hid : (2 * i + 1) * hid], total[:, (2 * i + 1) * hid : (2 * i + 2) * hid]
@@ -170,29 +134,16 @@
         dgu += [dh * up * sig * (1.0 + pre * (1.0 - sig)), dh * (pre * sig)]
     dgu = jnp.concatenate(dgu, axis=1).astype(jnp.bfloat16)
 
+    pgu = f32_dot(x_mat, dgu, ((0,), (0,))).astype(jnp.bfloat16)
     dx = jnp.dot(dgu, w_gu_t, preferred_element_type=jnp.float32).astype(jnp.bfloat16)
-    dx, dgu_other = lax.optimization_barrier((dx, swap(dgu, "c")))
-    both = jnp.concatenate([dgu, dgu_other], axis=0)
-    pgu = jnp.dot(jnp.concatenate([xt_kept, xt_got], axis=1), both, preferred_element_type=jnp.float32).astype(jnp.bfloat16)
 
-    summed = lax.psum_scatter(pgu, "x", scatter_dimension=0, tiled=True)
-    zl, yl = lax.axis_index("zl"), lax.axis_index("yl")
+    summed = lax.psum_scatter(pgu, ("x", "c"), scatter_dimension=0, tiled=True)
+    summed = jnp.transpose(summed.reshape(n_zl, LANE, n_yl, 2 * hid), (0, 2, 1, 3))
+    summed = a2a(summed.reshape(n_zl * n_yl, LANE, 2 * hid), ("zl", "yl"))
+    grad_gu = jnp.sum(summed.reshape(n_zl, n_yl * LANE, 2 * hid).astype(jnp.float32), axis=0)
+    grad_gu = grad_gu.astype(jnp.bfloat16)[None]
 
-    def block(zl_to, yl_to):
-        return lax.dynamic_slice(summed, (zl_to * LANE, yl_to * 2 * hid), (LANE, 2 * hid))
-
-    def flipped(v, flip):
-        return lax.ppermute(v, ("zl", "yl"), [(i, i ^ flip) for i in range(n_zl * n_yl)])
-
-    mine, other = block(zl, yl), flipped(block(zl, 1 - yl), 1)
-    mine2, other2 = flipped(block(1 - zl, yl), 2), flipped(block(1 - zl, 1 - yl), 3)
     back = a2a(dx.reshape(n_src, CAP, n_half * LANE), EXPERT)
-    back, other, mine2, other2 = lax.optimization_barrier((back, other, mine2, other2))
-    mine = (mine.astype(jnp.float32) + mine2.astype(jnp.float32)).astype(jnp.bfloat16)
-    other = (other.astype(jnp.float32) + other2.astype(jnp.float32)).astype(jnp.bfloat16)
-    low, high = jnp.where(yl == 0, mine, other), jnp.where(yl == 0, other, mine)
-    grad_gu = jnp.concatenate([low, high], axis=0)[None]
-
     back = jnp.sum(back.reshape(n_win, n_yl, n_zh, CAP, n_xc, n_zl, LANE).astype(jnp.float32), axis=2)
     back = jnp.transpose(back, (0, 2, 4, 3, 1, 5)).reshape(n_win, CAP, width)
     positions = jnp.arange(CAP, dtype=jnp.int32)

time: 177 us -> 176 us (level)
  waiting for transfers between devices: 81.1 us -> 93.6 us
  starting transfers between devices: 47.6 us -> 37.9 us
  Pallas kernels: 17 us -> 13.2 us
  matrix products: 9.62 us -> 11.4 us
    ppermute x3 -> x0, starting transfers between devices: 9.21 us -> none  [flipped(): lax.ppermute(v, ('zl', 'yl'), [(i, i ^ flip) for i in range(n_zl * n_yl)])]
    all_to_all x3 -> x4, waiting for transfers between devices: 23.5 us -> 31 us  [a2a(): return lax.all_to_all(v, axes, split_axis=0, concat_axis=0, tiled=True)]
    ppermute x3 -> x1, waiting for transfers between devices: 5.85 us -> 11.6 us  [swap(): return lax.ppermute(v, axis, [(0, 1), (1, 0)])]
    ppermute x3 -> x0, waiting for transfers between devices: 4.67 us -> none  [flipped(): lax.ppermute(v, ('zl', 'yl'), [(i, i ^ flip) for i in range(n_zl * n_yl)])]
    reduce_scatter x1, waiting for transfers between devices: 20.5 us -> 24.5 us  [on_device(): summed = lax.psum_scatter(pgu, ('x', 'c'), scatter_dimension=0, tiled=True)]
    ppermute x3 -> x1, starting transfers between devices: 6.04 us -> 2.08 us  [swap(): return lax.ppermute(v, axis, [(0, 1), (1, 0)])]
    pallas_call x1 -> x0, Pallas kernels: 3.8 us -> none  [split_rows(): pl.pallas_call(split_kernel, grid=(width // depth,), in_specs=[pl.BlockSp...]
    all_to_all x3 -> x4, starting transfers between devices: 32.3 us -> 35.8 us  [a2a(): return lax.all_to_all(v, axes, split_axis=0, concat_axis=0, tiled=True)]
  transfers between devices with their start and end apart: 11 -> 7, of which waited for: 8 -> 7; matrix products, arithmetic and copies ran while one was open for 2% -> 4% of each run, Pallas kernels for 9% -> 6%
where the time goes in v9:
time: 176 us; the launch traced here: 175 us
  waiting for transfers between devices  93.6 us (53%)
  starting transfers between devices  37.9 us (22%)
  between operations  14.1 us (8%)
  Pallas kernels  13.2 us (8%)
  matrix products  11.4 us (6%)
  local copies, waits for them, and re-layouts  3.22 us (2%)
    all_to_all x4, starting transfers between devices, a2a(): return lax.all_to_all(v, axes, split_axis=0, concat_axis=0, tiled=True)  35.8 us
    all_to_all x4, waiting for transfers between devices, a2a(): return lax.all_to_all(v, axes, split_axis=0, concat_axis=0, tiled=True)  31 us
    all_gather x1, waiting for transfers between devices, on_device(): lax.all_gather(w_pair.reshape(-1, LANE), ('x', 'c'), axis=0, tiled=True)  26.5 us
    reduce_scatter x1, waiting for transfers between devices, on_device(): summed = lax.psum_scatter(pgu, ('x', 'c'), scatter_dimension=0, tiled=True)  24.5 us
    ppermute x1, waiting for transfers between devices, swap(): return lax.ppermute(v, axis, [(0, 1), (1, 0)])  11.6 us
    pallas_call x1, Pallas kernels, order_weights(): pl.pallas_call(order_kernel, grid=(n_xc,), in_specs=[pl.BlockSpec((None,...  7.16 us
    dot_general x3, matrix products, f32_dot(): lax.dot_general(a, b, (dims, ((), ())), preferred_element_type=jnp.float32)  6.09 us
    pallas_call x1, Pallas kernels, select_rows(): pl.pallas_call(lambda *refs: rows_kernel(n_zl, *refs), out_shape=jax.Shap...  4.13 us
  transfers between devices with their start and end apart: 7, of which 7 were waited for; matrix products, arithmetic and copies ran while one was open for 4% of the time, Pallas kernels for 6%

profile of v9, /device:TPU:6, one launch (start us, length us, event | category | flops | bytes accessed | tf_op | source)
XLA Modules:
  0.0 174.9 jit_solution(12817989969615846753)
XLA Ops:
  7.2 1.9 %pack_weights.1 = bf16[2,2,576,128]{3,2,1,0:T(8,128)(2,1)} custom-call(bf16[256,384]{1,0:T(8,128)(2,1)} %bitcast.43, bf16[192,256]{1,0:T(8,128)(2,1)} %bitcast.45), custom_call_target="tpu_custom_call" | custom-call | tf_op jit(solution)/shard_map/pack_weights/pallas_call | solution.py:38
  9.1 4.7 %all-to-all-start = ((bf16[4,576,128]{2,1,0:T(8,128)(2,1)}), bf16[4,576,128]{2,1,0:T(8,128)(2,1)S(1)}, u32[]{:S(2)}, u32[]{:S(2)}) async-start(bf16[4,576,128]{2,1,0:T(8,128)(2,1)} %bitcast.40), calls=%async_computation | async-start | bytes 1179648 | tf_op jit(solution)/shard_map/all_to_all | solution.py:18
  13.7 4.1 %select_rows.1 = bf16[4,2,4,16,2048]{4,3,2,1,0:T(8,128)(2,1)} custom-call(bf16[128,4096]{1,0:T(8,128)(2,1)} %refs_0_.1, bf16[128,4096]{1,0:T(8,128)(2,1)} %refs_1_.1, s32[4,128]{1,0:T(4,128)} %bitcast.46, f32[4,128]{1,0:T(4,128)} %bitcast.48), custom_call_target="tpu_custom_call" | custom-call | tf_op jit(solution)/shard_map/select_rows/pallas_call | solution.py:96
  17.9 4.6 %all-to-all-done = bf16[4,576,128]{2,1,0:T(8,128)(2,1)S(1)} async-done(((bf16[4,576,128]{2,1,0:T(8,128)(2,1)}), bf16[4,576,128]{2,1,0:T(8,128)(2,1)S(1)}, u32[]{:S(2)}, u32[]{:S(2)}) %all-to-all-start) | async-done | bytes 589856 | tf_op jit(solution)/shard_map/all_to_all | solution.py:18
  22.5 0.8 copy-done
  23.3 15.0 %all-to-all-start.1 = ((bf16[32,16,2048]{2,1,0:T(8,128)(2,1)}), bf16[32,16,2048]{2,1,0:T(8,128)(2,1)S(1)}, u32[]{:S(2)}, u32[]{:S(2)}) async-start(bf16[32,16,2048]{2,1,0:T(8,128)(2,1)} %bitcast.36), calls=%async_computation.1 | async-start | bytes 4194304 | tf_op jit(solution)/shard_map/all_to_all | solution.py:18
  38.4 26.5 %all-gather.2.cloned.1.call-done = bf16[18432,128]{1,0:T(8,128)(2,1)} async-done(((bf16[2304,128]{1,0:T(8,128)(2,1)}), bf16[18432,128]{1,0:T(8,128)(2,1)}) %all-gather.2.cloned.1.call-update) | async-done | bytes 4718608 | tf_op jit(solution)/shard_map/all_gather | solution.py:115
  64.9 7.2 %order_weights.1 = (bf16[768,2048]{1,0:T(8,128)(2,1)}, bf16[384,2048]{1,0:T(8,128)(2,1)}) custom-call(bf16[8,2,2,576,128]{4,3,2,1,0:T(8,128)(2,1)} %bitcast.37), custom_call_target="tpu_custom_call" | custom-call | tf_op jit(solution)/shard_map/order_weights/pallas_call | solution.py:58
  72.1 18.9 %all-to-all-done.1 = bf16[32,16,2048]{2,1,0:T(8,128)(2,1)S(1)} async-done(((bf16[32,16,2048]{2,1,0:T(8,128)(2,1)}), bf16[32,16,2048]{2,1,0:T(8,128)(2,1)S(1)}, u32[]{:S(2)}, u32[]{:S(2)}) %all-to-all-start.1) | async-done | bytes 2097184 | tf_op jit(solution)/shard_map/all_to_all | solution.py:18
  91.0 2.3 %convolution_convert_fusion.3 = bf16[256,384]{1,0:T(8,128)(2,1)S(1)} fusion(bf16[384,2048]{1,0:T(8,128)(2,1)} %get-tuple-element.15, bf16[32,16,2048]{2,1,0:T(8,128)(2,1)S(1)} %all-to-all-done.1), kind=kOutput, calls=%fused_computation.8 | convolution fusion | flops 402751488 | bytes 2818048 | tf_op jit(solution)/shard_map/dot_general | solution.py:14
  93.3 1.0 convolution_convert_fusion.2
  94.4 2.1 %collective-permute-start = (bf16[256,1152]{1,0:T(8,128)(2,1)S(1)}, bf16[256,1152]{1,0:T(8,128)(2,1)S(1)}, u32[]{:S(2)}, u32[]{:S(2)}) collective-permute-start(bf16[256,1152]{1,0:T(8,128)(2,1)S(1)} %pad_maximum_fusion), channel_id=1, source_target_pairs={{0,4},{4,0},{1,5},{5,1},{2,6},{6,2},{3,7},{7,3},{8,12},{12,8},{9,1... | collective-permute-start | bytes 1769480 | tf_op jit(solution)/shard_map/ppermute | solution.py:22
  96.5 11.6 %collective-permute-done = bf16[256,1152]{1,0:T(8,128)(2,1)S(1)} collective-permute-done((bf16[256,1152]{1,0:T(8,128)(2,1)S(1)}, bf16[256,1152]{1,0:T(8,128)(2,1)S(1)}, u32[]{:S(2)}, u32[]{:S(2)}) %collective-permute-start) | collective-permute-done | bytes 589856 | tf_op jit(solution)/shard_map/ppermute | solution.py:22
  108.6 2.8 %convolution_convert_fusion = bf16[2048,768]{1,0:T(8,128)(2,1)} fusion(bf16[32,16,2048]{2,1,0:T(8,128)(2,1)S(1)} %all-to-all-done.1, bf16[256,192]{1,0:T(8,128)(2,1)S(1)} %get-tuple-element.17, bf16[256,192]{1,0:T(8,128)(2,1)S(1)} %get-tuple-element.19, bf16[256,192]{1,0:T(8,128)(2,1)S(1)} %get-tuple-element.18, bf16[256,192]{1,0:T(8,128)(2,1)S(1)} %get-tuple-element.16), kind=kOutput, calls=%fused_computation.2 | convolution fusion | flops 808452096 | bytes 4718592 | tf_op jit(solution)/shard_map/dot_general | solution.py:14
  111.4 3.9 %fusion.1 = bf16[32,8,2048]{2,1,0:T(8,128)(2,1)} fusion(bf16[768,2048]{1,0:T(8,128)(2,1)} %get-tuple-element.14, bf16[256,192]{1,0:T(8,128)(2,1)S(1)} %get-tuple-element.17, bf16[256,192]{1,0:T(8,128)(2,1)S(1)} %get-tuple-element.19, bf16[256,192]{1,0:T(8,128)(2,1)S(1)} %get-tuple-element.18, bf16[256,192]{1,0:T(8,128)(2,1)S(1)} %get-tuple-element.16), kind=kOutput, calls=%fused_computation.4 | convolution fusion | flops 807403520 | bytes 4587520 | tf_op jit(solution)/shard_map/dot_general | solution.py:138
  115.3 12.6 %all-to-all-start.2 = ((bf16[32,8,2048]{2,1,0:T(8,128)(2,1)}), bf16[32,8,2048]{2,1,0:T(8,128)(2,1)S(1)}, u32[]{:S(2)}, u32[]{:S(2)}) async-start(bf16[32,8,2048]{2,1,0:T(8,128)(2,1)} %fusion.1), calls=%async_computation.2 | async-start | bytes 2097152 | tf_op jit(solution)/shard_map/all_to_all | solution.py:18
  127.9 24.5 %reduce-scatter.2.cloned.1.call-done = bf16[256,768]{1,0:T(8,128)(2,1)} async-done(((bf16[2048,768]{1,0:T(8,128)(2,1)}), bf16[256,768]{1,0:T(8,128)(2,1)}) %reduce-scatter.2.cloned.1.call-update) | async-done | bytes 393232 | tf_op jit(solution)/shard_map/reduce_scatter | solution.py:140
  152.4 1.1 reshape.49
  153.5 0.8 copy.11
  154.3 2.0 %all-to-all-done.2 = bf16[32,8,2048]{2,1,0:T(8,128)(2,1)S(1)} async-done(((bf16[32,8,2048]{2,1,0:T(8,128)(2,1)}), bf16[32,8,2048]{2,1,0:T(8,128)(2,1)S(1)}, u32[]{:S(2)}, u32[]{:S(2)}) %all-to-all-start.2) | async-done | bytes 1048608 | tf_op jit(solution)/shard_map/all_to_all | solution.py:18
  156.4 3.5 %all-to-all-start.3 = ((bf16[4,128,384]{2,1,0:T(8,128)(2,1)}), bf16[4,128,384]{2,1,0:T(8,128)(2,1)S(1)}, u32[]{:S(2)}, u32[]{:S(2)}) async-start(bf16[4,128,384]{2,1,0:T(8,128)(2,1)} %bitcast.15), calls=%async_computation.4 | async-start | bytes 786432 | tf_op jit(solution)/shard_map/all_to_all | solution.py:18
  160.5 1.5 fusion
  161.9 5.4 %all-to-all-done.3 = bf16[4,128,384]{2,1,0:T(8,128)(2,1)S(1)} async-done(((bf16[4,128,384]{2,1,0:T(8,128)(2,1)}), bf16[4,128,384]{2,1,0:T(8,128)(2,1)S(1)}, u32[]{:S(2)}, u32[]{:S(2)}) %all-to-all-start.3) | async-done | bytes 393248 | tf_op jit(solution)/shard_map/all_to_all | solution.py:18
  167.4 0.7 bitcast_reduce_fusion
  (15 shorter events, 1.3 us)
Async XLA Ops:
  9.1 13.4 %all-to-all-start = ((bf16[4,576,128]{2,1,0:T(8,128)(2,1)}), bf16[4,576,128]{2,1,0:T(8,128)(2,1)S(1)}, u32[]{:S(2)}, u32[]{:S(2)}) async-start(bf16[4,576,128]{2,1,0:T(8,128)(2,1)} %bitcast.40), calls=%async_computation | async-start | bytes 1179648 | tf_op jit(solution)/shard_map/all_to_all | solution.py:18
  13.7 51.2 %all-gather.2.cloned.1.call-start = ((), (), s32[]{:S(2)}) async-start(), calls=%async_computation.5 | async-start | bytes 5308416 | tf_op jit(solution)/shard_map/all_gather | solution.py:115
  22.4 0.8 copy-start
  23.3 67.7 %all-to-all-start.1 = ((bf16[32,16,2048]{2,1,0:T(8,128)(2,1)}), bf16[32,16,2048]{2,1,0:T(8,128)(2,1)S(1)}, u32[]{:S(2)}, u32[]{:S(2)}) async-start(bf16[32,16,2048]{2,1,0:T(8,128)(2,1)} %bitcast.36), calls=%async_computation.1 | async-start | bytes 4194304 | tf_op jit(solution)/shard_map/all_to_all | solution.py:18
  38.3 114.1 %reduce-scatter.2.cloned.1.call-start = ((), (), s32[]{:S(2)}) async-start(), calls=%async_computation.6 | async-start | bytes 3538944 | tf_op jit(solution)/shard_map/reduce_scatter | solution.py:140
  91.0 2.4 %copy-start.2 = (bf16[768,2048]{1,0:T(8,128)(2,1)S(1)}, bf16[768,2048]{1,0:T(8,128)(2,1)}, u32[]{:S(2)}) copy-start(bf16[768,2048]{1,0:T(8,128)(2,1)} %get-tuple-element.14) | copy-start | bytes 9437188
  94.4 13.7 %collective-permute-start = (bf16[256,1152]{1,0:T(8,128)(2,1)S(1)}, bf16[256,1152]{1,0:T(8,128)(2,1)S(1)}, u32[]{:S(2)}, u32[]{:S(2)}) collective-permute-start(bf16[256,1152]{1,0:T(8,128)(2,1)S(1)} %pad_maximum_fusion), channel_id=1, source_target_pairs={{0,4},{4,0},{1,5},{5,1},{2,6},{6,2},{3,7},{7,3},{8,12},{12,8},{9,1... | collective-permute-start | bytes 1769480 | tf_op jit(solution)/shard_map/ppermute | solution.py:22
  115.3 41.1 %all-to-all-start.2 = ((bf16[32,8,2048]{2,1,0:T(8,128)(2,1)}), bf16[32,8,2048]{2,1,0:T(8,128)(2,1)S(1)}, u32[]{:S(2)}, u32[]{:S(2)}) async-start(bf16[32,8,2048]{2,1,0:T(8,128)(2,1)} %fusion.1), calls=%async_computation.2 | async-start | bytes 2097152 | tf_op jit(solution)/shard_map/all_to_all | solution.py:18
  153.5 6.9 %copy-start.1 = (s32[128,4]{0,1:T(4,128)S(1)}, s32[128,4]{0,1:T(4,128)}, u32[]{:S(2)}) copy-start(s32[128,4]{0,1:T(4,128)} %param.8) | copy-start | bytes 6148
  156.4 11.0 %all-to-all-start.3 = ((bf16[4,128,384]{2,1,0:T(8,128)(2,1)}), bf16[4,128,384]{2,1,0:T(8,128)(2,1)S(1)}, u32[]{:S(2)}, u32[]{:S(2)}) async-start(bf16[4,128,384]{2,1,0:T(8,128)(2,1)} %bitcast.15), calls=%async_computation.4 | async-start | bytes 786432 | tf_op jit(solution)/shard_map/all_to_all | solution.py:18
Sparse Core Ops, SparseCore 0:
  23.4 41.4 all-gather.1
  111.5 40.8 reduce-scatter.1

commit v10 on v8

--- a/solution.py
+++ b/solution.py
@@ -176,23 +176,12 @@
     pgu = jnp.dot(jnp.concatenate([xt_kept, xt_got], axis=1), both, preferred_element_type=jnp.float32).astype(jnp.bfloat16)
 
     summed = lax.psum_scatter(pgu, "x", scatter_dimension=0, tiled=True)
-    zl, yl = lax.axis_index("zl"), lax.axis_index("yl")
+    summed = jnp.transpose(summed.reshape(n_zl, LANE, n_yl, 2 * hid), (0, 2, 1, 3))
+    summed = a2a(summed.reshape(n_zl * n_yl, LANE, 2 * hid), ("zl", "yl"))
+    grad_gu = jnp.sum(summed.reshape(n_zl, n_yl * LANE, 2 * hid).astype(jnp.float32), axis=0)
+    grad_gu = grad_gu.astype(jnp.bfloat16)[None]
 
-    def block(zl_to, yl_to):
-        return lax.dynamic_slice(summed, (zl_to * LANE, yl_to * 2 * hid), (LANE, 2 * hid))
-
-    def flipped(v, flip):
-        return lax.ppermute(v, ("zl", "yl"), [(i, i ^ flip) for i in range(n_zl * n_yl)])
-
-    mine, other = block(zl, yl), flipped(block(zl, 1 - yl), 1)
-    mine2, other2 = flipped(block(1 - zl, yl), 2), flipped(block(1 - zl, 1 - yl), 3)
     back = a2a(dx.reshape(n_src, CAP, n_half * LANE), EXPERT)
-    back, other, mine2, other2 = lax.optimization_barrier((back, other, mine2, other2))
-    mine = (mine.astype(jnp.float32) + mine2.astype(jnp.float32)).astype(jnp.bfloat16)
-    other = (other.astype(jnp.float32) + other2.astype(jnp.float32)).astype(jnp.bfloat16)
-    low, high = jnp.where(yl == 0, mine, other), jnp.where(yl == 0, other, mine)
-    grad_gu = jnp.concatenate([low, high], axis=0)[None]
-
     back = jnp.sum(back.reshape(n_win, n_yl, n_zh, CAP, n_xc, n_zl, LANE).astype(jnp.float32), axis=2)
     back = jnp.transpose(back, (0, 2, 4, 3, 1, 5)).reshape(n_win, CAP, width)
     positions = jnp.arange(CAP, dtype=jnp.int32)

time: 177 us -> 178 us (level)
  waiting for transfers between devices: 81.1 us -> 88.5 us
  starting transfers between devices: 47.6 us -> 42.5 us
    all_to_all x3 -> x4, waiting for transfers between devices: 23.5 us -> 35.6 us  [a2a(): return lax.all_to_all(v, axes, split_axis=0, concat_axis=0, tiled=True)]
    ppermute x3 -> x0, starting transfers between devices: 9.21 us -> none  [flipped(): lax.ppermute(v, ('zl', 'yl'), [(i, i ^ flip) for i in range(n_zl * n_yl)])]
    ppermute x3 -> x0, waiting for transfers between devices: 4.67 us -> none  [flipped(): lax.ppermute(v, ('zl', 'yl'), [(i, i ^ flip) for i in range(n_zl * n_yl)])]
    all_to_all x3 -> x4, starting transfers between devices: 32.3 us -> 36.4 us  [a2a(): return lax.all_to_all(v, axes, split_axis=0, concat_axis=0, tiled=True)]
    reshape x0 -> x2, local copies, waits for them, and re-layouts: none -> 1.89 us  [on_device(): summed.reshape(n_zl, LANE, n_yl, 2 * hid)]
  transfers between devices with their start and end apart: 11 -> 9, of which waited for: 8 -> 8; matrix products, arithmetic and copies ran while one was open for 2% -> 3% of each run, Pallas kernels for 9% -> 9%
where the time goes in v10:
time: 178 us; the launch traced here: 177 us
  waiting for transfers between devices  88.5 us (50%)
  starting transfers between devices  42.5 us (24%)
  Pallas kernels  17 us (10%)
  between operations  14.2 us (8%)
  matrix products  9.62 us (5%)
  local copies, waits for them, and re-layouts  3.33 us (2%)
    all_to_all x4, starting transfers between devices, a2a(): return lax.all_to_all(v, axes, split_axis=0, concat_axis=0, tiled=True)  36.4 us
    all_to_all x4, waiting for transfers between devices, a2a(): return lax.all_to_all(v, axes, split_axis=0, concat_axis=0, tiled=True)  35.6 us
    all_gather x1, waiting for transfers between devices, on_device(): lax.all_gather(w_pair.reshape(-1, LANE), ('x', 'c'), axis=0, tiled=True)  26.5 us
    reduce_scatter x1, waiting for transfers between devices, on_device(): summed = lax.psum_scatter(pgu, 'x', scatter_dimension=0, tiled=True)  20.5 us
    pallas_call x1, Pallas kernels, order_weights(): pl.pallas_call(order_kernel, grid=(n_xc,), in_specs=[pl.BlockSpec((None,...  7.17 us
    ppermute x3, starting transfers between devices, swap(): return lax.ppermute(v, axis, [(0, 1), (1, 0)])  6.05 us
    ppermute x3, waiting for transfers between devices, swap(): return lax.ppermute(v, axis, [(0, 1), (1, 0)])  5.86 us
    pallas_call x1, Pallas kernels, select_rows(): pl.pallas_call(lambda *refs: rows_kernel(n_zl, *refs), out_shape=jax.Shap...  4.15 us
  transfers between devices with their start and end apart: 9, of which 8 were waited for; matrix products, arithmetic and copies ran while one was open for 3% of the time, Pallas kernels for 9%

profile of v10, /device:TPU:6, one launch (start us, length us, event | category | flops | bytes accessed | tf_op | source)
XLA Modules:
  0.0 176.7 jit_solution(14115110552581618594)
XLA Ops:
  7.2 1.9 %pack_weights.1 = bf16[2,2,576,128]{3,2,1,0:T(8,128)(2,1)} custom-call(bf16[256,384]{1,0:T(8,128)(2,1)} %bitcast.42, bf16[192,256]{1,0:T(8,128)(2,1)} %bitcast.44), custom_call_target="tpu_custom_call" | custom-call | tf_op jit(solution)/shard_map/pack_weights/pallas_call | solution.py:70
  9.1 4.7 %all-to-all-start = ((bf16[4,576,128]{2,1,0:T(8,128)(2,1)}), bf16[4,576,128]{2,1,0:T(8,128)(2,1)S(1)}, u32[]{:S(2)}, u32[]{:S(2)}) async-start(bf16[4,576,128]{2,1,0:T(8,128)(2,1)} %bitcast.39), calls=%async_computation | async-start | bytes 1179648 | tf_op jit(solution)/shard_map/all_to_all | solution.py:19
  13.7 4.2 %select_rows.1 = bf16[4,2,4,16,2048]{4,3,2,1,0:T(8,128)(2,1)} custom-call(bf16[128,4096]{1,0:T(8,128)(2,1)} %refs_0_.1, bf16[128,4096]{1,0:T(8,128)(2,1)} %refs_1_.1, s32[4,128]{1,0:T(4,128)} %bitcast.45, f32[4,128]{1,0:T(4,128)} %bitcast.47), custom_call_target="tpu_custom_call" | custom-call | tf_op jit(solution)/shard_map/select_rows/pallas_call | solution.py:128
  17.9 4.6 %all-to-all-done = bf16[4,576,128]{2,1,0:T(8,128)(2,1)S(1)} async-done(((bf16[4,576,128]{2,1,0:T(8,128)(2,1)}), bf16[4,576,128]{2,1,0:T(8,128)(2,1)S(1)}, u32[]{:S(2)}, u32[]{:S(2)}) %all-to-all-start) | async-done | bytes 589856 | tf_op jit(solution)/shard_map/all_to_all | solution.py:19
  23.3 15.0 %all-to-all-start.1 = ((bf16[32,16,2048]{2,1,0:T(8,128)(2,1)}), bf16[32,16,2048]{2,1,0:T(8,128)(2,1)S(1)}, u32[]{:S(2)}, u32[]{:S(2)}) async-start(bf16[32,16,2048]{2,1,0:T(8,128)(2,1)} %bitcast.35), calls=%async_computation.1 | async-start | bytes 4194304 | tf_op jit(solution)/shard_map/all_to_all | solution.py:19
  38.4 26.5 %all-gather.2.cloned.1.call-done = bf16[18432,128]{1,0:T(8,128)(2,1)} async-done(((bf16[2304,128]{1,0:T(8,128)(2,1)}), bf16[18432,128]{1,0:T(8,128)(2,1)}) %all-gather.2.cloned.1.call-update) | async-done | bytes 4718608 | tf_op jit(solution)/shard_map/all_gather | solution.py:147
  64.9 7.2 %order_weights.1 = (bf16[768,2048]{1,0:T(8,128)(2,1)}, bf16[384,2048]{1,0:T(8,128)(2,1)}) custom-call(bf16[8,2,2,576,128]{4,3,2,1,0:T(8,128)(2,1)} %bitcast.36), custom_call_target="tpu_custom_call" | custom-call | tf_op jit(solution)/shard_map/order_weights/pallas_call | solution.py:90
  72.1 18.9 %all-to-all-done.1.rows_ref = bf16[32,16,2048]{2,1,0:T(8,128)(2,1)S(1)} async-done(((bf16[32,16,2048]{2,1,0:T(8,128)(2,1)}), bf16[32,16,2048]{2,1,0:T(8,128)(2,1)S(1)}, u32[]{:S(2)}, u32[]{:S(2)}) %all-to-all-start.1) | async-done | bytes 2097184 | tf_op jit(solution)/shard_map/all_to_all | solution.py:19
  91.0 2.9 %convolution_convert_fusion.3 = bf16[256,384]{1,0:T(8,128)(2,1)S(1)} fusion(bf16[384,2048]{1,0:T(8,128)(2,1)} %get-tuple-element.24, bf16[32,16,2048]{2,1,0:T(8,128)(2,1)S(1)} %all-to-all-done.1.rows_ref), kind=kOutput, calls=%fused_computation.7 | convolution fusion | flops 402751488 | bytes 2818048 | tf_op jit(solution)/shard_map/dot_general | solution.py:15
  95.2 2.1 %collective-permute-start = (bf16[256,1152]{1,0:T(8,128)(2,1)S(1)}, bf16[256,1152]{1,0:T(8,128)(2,1)S(1)}, u32[]{:S(2)}, u32[]{:S(2)}) collective-permute-start(bf16[256,1152]{1,0:T(8,128)(2,1)S(1)} %pad_maximum_fusion), channel_id=1, source_target_pairs={{0,4},{4,0},{1,5},{5,1},{2,6},{6,2},{3,7},{7,3},{8,12},{12,8},{9,1... | collective-permute-start | bytes 1769480 | tf_op jit(solution)/shard_map/ppermute | solution.py:23
  97.3 3.8 %split_rows.1 = (bf16[1024,256]{1,0:T(8,128)(2,1)}, bf16[1024,256]{1,0:T(8,128)(2,1)}) custom-call(s32[1]{0:T(128)} %bitcast.10.core_ref, bf16[32,16,2048]{2,1,0:T(8,128)(2,1)} %copy-done), custom_call_target="tpu_custom_call" | custom-call | tf_op jit(solution)/shard_map/split_rows/pallas_call | solution.py:44
  101.1 1.9 %collective-permute-start.1 = (bf16[1024,256]{1,0:T(8,128)(2,1)}, bf16[1024,256]{1,0:T(8,128)(2,1)S(1)}, u32[]{:S(2)}, u32[]{:S(2)}) collective-permute-start(bf16[1024,256]{1,0:T(8,128)(2,1)} %get-tuple-element.28), channel_id=1, source_target_pairs={{0,32},{32,0},{1,33},{33,1},{2,34},{34,2},{3,35},{35,3},{4,36},{36... | collective-permute-start | bytes 1572872 | tf_op jit(solution)/shard_map/ppermute | solution.py:23
  103.0 2.1 %collective-permute-done.1 = bf16[1024,256]{1,0:T(8,128)(2,1)S(1)} collective-permute-done((bf16[1024,256]{1,0:T(8,128)(2,1)}, bf16[1024,256]{1,0:T(8,128)(2,1)S(1)}, u32[]{:S(2)}, u32[]{:S(2)}) %collective-permute-start.1) | collective-permute-done | bytes 524320 | tf_op jit(solution)/shard_map/ppermute | solution.py:23
  105.1 3.8 %collective-permute-done = bf16[256,1152]{1,0:T(8,128)(2,1)S(1)} collective-permute-done((bf16[256,1152]{1,0:T(8,128)(2,1)S(1)}, bf16[256,1152]{1,0:T(8,128)(2,1)S(1)}, u32[]{:S(2)}, u32[]{:S(2)}) %collective-permute-start) | collective-permute-done | bytes 589856 | tf_op jit(solution)/shard_map/ppermute | solution.py:23
  109.5 2.1 %collective-permute-start.2 = (bf16[256,768]{1,0:T(8,128)(2,1)S(1)}, bf16[256,768]{1,0:T(8,128)(2,1)S(1)}, u32[]{:S(2)}, u32[]{:S(2)}) collective-permute-start(bf16[256,768]{1,0:T(8,128)(2,1)S(1)} %pad_maximum_fusion.1), channel_id=1, source_target_pairs={{0,32},{32,0},{1,33},{33,1},{2,34},{34,2},{3,35},{35,3},{4,36},{36... | collective-permute-start | bytes 1179656 | tf_op jit(solution)/shard_map/ppermute | solution.py:23
  111.6 2.0 %convolution_convert_fusion = bf16[256,2048]{1,0:T(8,128)(2,1)} fusion(bf16[256,768]{1,0:T(8,128)(2,1)S(1)} %pad_maximum_fusion.1, bf16[768,2048]{1,0:T(8,128)(2,1)S(1)} %copy-done.4), kind=kOutput, calls=%fused_computation.2 | convolution fusion | flops 805830656 | bytes 4587520 | tf_op jit(solution)/shard_map/dot_general | solution.py:173
  113.5 2.2 %convolution_convert_fusion.1 = bf16[1024,768]{1,0:T(8,128)(2,1)} fusion(bf16[1024,256]{1,0:T(8,128)(2,1)S(1)} %collective-permute-done.1, bf16[1024,256]{1,0:T(8,128)(2,1)S(1)} %copy-done.5, bf16[256,768]{1,0:T(8,128)(2,1)S(1)} %collective-permute-done.2, bf16[256,192]{1,0:T(8,128)(2,1)S(1)} %get-tuple-element.35, ...), kind=kOutput, calls=%fused_computation.4 | convolution fusion | flops 812122112 | bytes 3407872 | tf_op jit(solution)/shard_map/dot_general | solution.py:176
  115.8 12.6 %all-to-all-start.2 = ((bf16[32,8,2048]{2,1,0:T(8,128)(2,1)}), bf16[32,8,2048]{2,1,0:T(8,128)(2,1)S(1)}, u32[]{:S(2)}, u32[]{:S(2)}) async-start(bf16[32,8,2048]{2,1,0:T(8,128)(2,1)} %bitcast.11), calls=%async_computation.2 | async-start | bytes 2097152 | tf_op jit(solution)/shard_map/all_to_all | solution.py:19
  128.4 20.5 %reduce-scatter.2.cloned.1.call-done = bf16[256,768]{1,0:T(8,128)(2,1)} async-done(((bf16[1024,768]{1,0:T(8,128)(2,1)}), bf16[256,768]{1,0:T(8,128)(2,1)}) %reduce-scatter.2.cloned.1.call-update) | async-done | bytes 393232 | tf_op jit(solution)/shard_map/reduce_scatter | solution.py:178
  148.9 1.1 reshape.53
  150.8 8.3 %all-to-all-done.2 = bf16[32,8,2048]{2,1,0:T(8,128)(2,1)S(1)} async-done(((bf16[32,8,2048]{2,1,0:T(8,128)(2,1)}), bf16[32,8,2048]{2,1,0:T(8,128)(2,1)S(1)}, u32[]{:S(2)}, u32[]{:S(2)}) %all-to-all-start.2) | async-done | bytes 1048608 | tf_op jit(solution)/shard_map/all_to_all | solution.py:19
  159.1 4.1 %all-to-all-start.3 = ((bf16[4,128,384]{2,1,0:T(8,128)(2,1)}), bf16[4,128,384]{2,1,0:T(8,128)(2,1)S(1)}, u32[]{:S(2)}, u32[]{:S(2)}) async-start(bf16[4,128,384]{2,1,0:T(8,128)(2,1)} %bitcast.16), calls=%async_computation.4 | async-start | bytes 786432 | tf_op jit(solution)/shard_map/all_to_all | solution.py:19
  163.8 1.5 fusion
  165.3 3.8 %all-to-all-done.3 = bf16[4,128,384]{2,1,0:T(8,128)(2,1)S(1)} async-done(((bf16[4,128,384]{2,1,0:T(8,128)(2,1)}), bf16[4,128,384]{2,1,0:T(8,128)(2,1)S(1)}, u32[]{:S(2)}, u32[]{:S(2)}) %all-to-all-start.3) | async-done | bytes 393248 | tf_op jit(solution)/shard_map/all_to_all | solution.py:19
  (27 shorter events, 4.9 us)
Async XLA Ops:
  9.1 13.4 %all-to-all-start = ((bf16[4,576,128]{2,1,0:T(8,128)(2,1)}), bf16[4,576,128]{2,1,0:T(8,128)(2,1)S(1)}, u32[]{:S(2)}, u32[]{:S(2)}) async-start(bf16[4,576,128]{2,1,0:T(8,128)(2,1)} %bitcast.39), calls=%async_computation | async-start | bytes 1179648 | tf_op jit(solution)/shard_map/all_to_all | solution.py:19
  13.7 51.2 %all-gather.2.cloned.1.call-start = ((), (), s32[]{:S(2)}) async-start(), calls=%async_computation.5 | async-start | bytes 5308416 | tf_op jit(solution)/shard_map/all_gather | solution.py:147
  22.4 0.8 copy-start.1
  23.3 67.7 %all-to-all-start.1 = ((bf16[32,16,2048]{2,1,0:T(8,128)(2,1)}), bf16[32,16,2048]{2,1,0:T(8,128)(2,1)S(1)}, u32[]{:S(2)}, u32[]{:S(2)}) async-start(bf16[32,16,2048]{2,1,0:T(8,128)(2,1)} %bitcast.35), calls=%async_computation.1 | async-start | bytes 4194304 | tf_op jit(solution)/shard_map/all_to_all | solution.py:19
  38.3 110.6 %reduce-scatter.2.cloned.1.call-start = ((), (), s32[]{:S(2)}) async-start(), calls=%async_computation.6 | async-start | bytes 1966080 | tf_op jit(solution)/shard_map/reduce_scatter | solution.py:178
  91.0 3.0 %copy-start = (bf16[32,16,2048]{2,1,0:T(8,128)(2,1)}, bf16[32,16,2048]{2,1,0:T(8,128)(2,1)S(1)}, u32[]{:S(2)}) copy-start(bf16[32,16,2048]{2,1,0:T(8,128)(2,1)S(1)} %all-to-all-done.1.rows_ref) | copy-start | bytes 6291460
  91.0 3.1 %copy-start.3 = (bf16[768,2048]{1,0:T(8,128)(2,1)S(1)}, bf16[768,2048]{1,0:T(8,128)(2,1)}, u32[]{:S(2)}) copy-start(bf16[768,2048]{1,0:T(8,128)(2,1)} %get-tuple-element.23) | copy-start | bytes 9437188
  95.2 13.7 %collective-permute-start = (bf16[256,1152]{1,0:T(8,128)(2,1)S(1)}, bf16[256,1152]{1,0:T(8,128)(2,1)S(1)}, u32[]{:S(2)}, u32[]{:S(2)}) collective-permute-start(bf16[256,1152]{1,0:T(8,128)(2,1)S(1)} %pad_maximum_fusion), channel_id=1, source_target_pairs={{0,4},{4,0},{1,5},{5,1},{2,6},{6,2},{3,7},{7,3},{8,12},{12,8},{9,1... | collective-permute-start | bytes 1769480 | tf_op jit(solution)/shard_map/ppermute | solution.py:23
  101.1 4.0 %collective-permute-start.1 = (bf16[1024,256]{1,0:T(8,128)(2,1)}, bf16[1024,256]{1,0:T(8,128)(2,1)S(1)}, u32[]{:S(2)}, u32[]{:S(2)}) collective-permute-start(bf16[1024,256]{1,0:T(8,128)(2,1)} %get-tuple-element.28), channel_id=1, source_target_pairs={{0,32},{32,0},{1,33},{33,1},{2,34},{34,2},{3,35},{35,3},{4,36},{36... | collective-permute-start | bytes 1572872 | tf_op jit(solution)/shard_map/ppermute | solution.py:23
  108.8 2.7 %copy-start.4 = (bf16[768,2048]{1,0:T(8,128)(2,1)S(1)}, bf16[768,2048]{1,0:T(8,128)(2,1)}, u32[]{:S(2)}) copy-start(bf16[768,2048]{1,0:T(8,128)(2,1)} %get-tuple-element.23) | copy-start | bytes 9437188
  109.5 4.1 %copy-start.5 = (bf16[1024,256]{1,0:T(8,128)(2,1)S(1)}, bf16[1024,256]{1,0:T(8,128)(2,1)}, u32[]{:S(2)}) copy-start(bf16[1024,256]{1,0:T(8,128)(2,1)} %get-tuple-element.31) | copy-start | bytes 1572868
  109.5 4.0 %collective-permute-start.2 = (bf16[256,768]{1,0:T(8,128)(2,1)S(1)}, bf16[256,768]{1,0:T(8,128)(2,1)S(1)}, u32[]{:S(2)}, u32[]{:S(2)}) collective-permute-start(bf16[256,768]{1,0:T(8,128)(2,1)S(1)} %pad_maximum_fusion.1), channel_id=1, source_target_pairs={{0,32},{32,0},{1,33},{33,1},{2,34},{34,2},{3,35},{35,3},{4,36},{36... | collective-permute-start | bytes 1179656 | tf_op jit(solution)/shard_map/ppermute | solution.py:23
  115.8 43.3 %all-to-all-start.2 = ((bf16[32,8,2048]{2,1,0:T(8,128)(2,1)}), bf16[32,8,2048]{2,1,0:T(8,128)(2,1)S(1)}, u32[]{:S(2)}, u32[]{:S(2)}) async-start(bf16[32,8,2048]{2,1,0:T(8,128)(2,1)} %bitcast.11), calls=%async_computation.2 | async-start | bytes 2097152 | tf_op jit(solution)/shard_map/all_to_all | solution.py:19
  159.1 4.7 %copy-start.2 = (s32[128,4]{0,1:T(4,128)S(1)}, s32[128,4]{0,1:T(4,128)}, u32[]{:S(2)}) copy-start(s32[128,4]{0,1:T(4,128)} %param.8) | copy-start | bytes 6148
  159.1 10.0 %all-to-all-start.3 = ((bf16[4,128,384]{2,1,0:T(8,128)(2,1)}), bf16[4,128,384]{2,1,0:T(8,128)(2,1)S(1)}, u32[]{:S(2)}, u32[]{:S(2)}) async-start(bf16[4,128,384]{2,1,0:T(8,128)(2,1)} %bitcast.16), calls=%async_computation.4 | async-start | bytes 786432 | tf_op jit(solution)/shard_map/all_to_all | solution.py:19
Sparse Core Ops, SparseCore 0:
  23.4 41.4 all-gather.1
  115.9 32.9 reduce-scatter.1

commit v11 on v9

--- a/solution.py
+++ b/solution.py
@@ -134,11 +134,11 @@
         dgu += [dh * up * sig * (1.0 + pre * (1.0 - sig)), dh * (pre * sig)]
     dgu = jnp.concatenate(dgu, axis=1).astype(jnp.bfloat16)
 
-    pgu = f32_dot(x_mat, dgu, ((0,), (0,))).astype(jnp.bfloat16)
+    pgu = [f32_dot(x_mat, dgu[:, 2 * i * hid : 2 * (i + 1) * hid], ((0,), (0,))) for i in range(n_yl)]
+    pgu = jnp.stack([p.astype(jnp.bfloat16).reshape(n_half, LANE, 2 * hid) for p in pgu], axis=1).reshape(-1, 2 * hid)
     dx = jnp.dot(dgu, w_gu_t, preferred_element_type=jnp.float32).astype(jnp.bfloat16)
 
     summed = lax.psum_scatter(pgu, ("x", "c"), scatter_dimension=0, tiled=True)
-    summed = jnp.transpose(summed.reshape(n_zl, LANE, n_yl, 2 * hid), (0, 2, 1, 3))
     summed = a2a(summed.reshape(n_zl * n_yl, LANE, 2 * hid), ("zl", "yl"))
     grad_gu = jnp.sum(summed.reshape(n_zl, n_yl * LANE, 2 * hid).astype(jnp.float32), axis=0)
     grad_gu = grad_gu.astype(jnp.bfloat16)[None]

time: 176 us -> 175 us (level)
  blocking collectives: 0 us -> 40.9 us
  waiting for transfers between devices: 93.6 us -> 66.4 us
  starting transfers between devices: 37.9 us -> 25.4 us
  matrix products: 11.4 us -> 9.26 us
  other arithmetic: 1.41 us -> 3.39 us
  local copies, waits for them, and re-layouts: 3.22 us -> 1.34 us
    all_to_all x0 -> x1, blocking collectives: none -> 40.9 us  [a2a(): return lax.all_to_all(v, axes, split_axis=0, concat_axis=0, tiled=True)]
    reduce_scatter x1, waiting for transfers between devices: 24.5 us -> 0.01 us  [on_device(): summed = lax.psum_scatter(pgu, ('x', 'c'), scatter_dimension=0, tiled=True)]
    all_to_all x4 -> x3, starting transfers between devices: 35.8 us -> 23.3 us  [a2a(): return lax.all_to_all(v, axes, split_axis=0, concat_axis=0, tiled=True)]
    all_to_all x4 -> x3, waiting for transfers between devices: 31 us -> 28.3 us  [a2a(): return lax.all_to_all(v, axes, split_axis=0, concat_axis=0, tiled=True)]
    another operation x1 -> x2, other arithmetic: 0.34 us -> 2.32 us  [the longest x1 1.98 us: on_device(): jnp.stack([p.astype(jnp.bfloat16).reshape(n_half, LANE, 2 * hid) for p in...]
    reshape x2 -> x0, local copies, waits for them, and re-layouts: 1.88 us -> none  [on_device(): summed.reshape(n_zl, LANE, n_yl, 2 * hid)]
    dot_general x3 -> x4, matrix products: 6.09 us -> 4.89 us  [f32_dot(): lax.dot_general(a, b, (dims, ((), ())), preferred_element_type=jnp.float32)]
  transfers between devices with their start and end apart: 7 -> 6, of which waited for: 7 -> 5; matrix products, arithmetic and copies ran while one was open for 4% -> 3% of each run, Pallas kernels for 6% -> 6%
where the time goes in v11:
time: 175 us; the launch traced here: 174 us
  waiting for transfers between devices  66.4 us (38%)
  blocking collectives  40.9 us (23%)
  starting transfers between devices  25.4 us (15%)
  between operations  14.1 us (8%)
  Pallas kernels  13.2 us (8%)
  matrix products  9.26 us (5%)
  other arithmetic  3.39 us (2%)
    all_to_all x1, blocking collectives, a2a(): return lax.all_to_all(v, axes, split_axis=0, concat_axis=0, tiled=True)  40.9 us
    all_to_all x3, waiting for transfers between devices, a2a(): return lax.all_to_all(v, axes, split_axis=0, concat_axis=0, tiled=True)  28.3 us
    all_gather x1, waiting for transfers between devices, on_device(): lax.all_gather(w_pair.reshape(-1, LANE), ('x', 'c'), axis=0, tiled=True)  26.5 us
    all_to_all x3, starting transfers between devices, a2a(): return lax.all_to_all(v, axes, split_axis=0, concat_axis=0, tiled=True)  23.3 us
    ppermute x1, waiting for transfers between devices, swap(): return lax.ppermute(v, axis, [(0, 1), (1, 0)])  11.6 us
    pallas_call x1, Pallas kernels, order_weights(): pl.pallas_call(order_kernel, grid=(n_xc,), in_specs=[pl.BlockSpec((None,...  7.17 us
    dot_general x4, matrix products, f32_dot(): lax.dot_general(a, b, (dims, ((), ())), preferred_element_type=jnp.float32)  4.89 us
    pallas_call x1, Pallas kernels, select_rows(): pl.pallas_call(lambda *refs: rows_kernel(n_zl, *refs), out_shape=jax.Shap...  4.14 us
  transfers between devices with their start and end apart: 6, of which 5 were waited for; matrix products, arithmetic and copies ran while one was open for 3% of the time, Pallas kernels for 6%

profile of v11, /device:TPU:6, one launch (start us, length us, event | category | flops | bytes accessed | tf_op | source)
XLA Modules:
  0.0 174.0 jit_solution(6075621362957034861)
XLA Ops:
  7.2 1.9 %pack_weights.1 = bf16[2,2,576,128]{3,2,1,0:T(8,128)(2,1)} custom-call(bf16[256,384]{1,0:T(8,128)(2,1)} %bitcast.54, bf16[192,256]{1,0:T(8,128)(2,1)} %bitcast.56), custom_call_target="tpu_custom_call" | custom-call | tf_op jit(solution)/shard_map/pack_weights/pallas_call | solution.py:38
  9.1 4.7 %all-to-all-start = ((bf16[4,576,128]{2,1,0:T(8,128)(2,1)}), bf16[4,576,128]{2,1,0:T(8,128)(2,1)S(1)}, u32[]{:S(2)}, u32[]{:S(2)}) async-start(bf16[4,576,128]{2,1,0:T(8,128)(2,1)} %bitcast.48), calls=%async_computation | async-start | bytes 1179648 | tf_op jit(solution)/shard_map/all_to_all | solution.py:18
  13.7 4.1 %select_rows.1 = bf16[4,2,4,16,2048]{4,3,2,1,0:T(8,128)(2,1)} custom-call(bf16[128,4096]{1,0:T(8,128)(2,1)} %refs_0_.1, bf16[128,4096]{1,0:T(8,128)(2,1)} %refs_1_.1, s32[4,128]{1,0:T(4,128)} %bitcast.57, f32[4,128]{1,0:T(4,128)} %bitcast.59), custom_call_target="tpu_custom_call" | custom-call | tf_op jit(solution)/shard_map/select_rows/pallas_call | solution.py:96
  17.9 4.6 %all-to-all-done = bf16[4,576,128]{2,1,0:T(8,128)(2,1)S(1)} async-done(((bf16[4,576,128]{2,1,0:T(8,128)(2,1)}), bf16[4,576,128]{2,1,0:T(8,128)(2,1)S(1)}, u32[]{:S(2)}, u32[]{:S(2)}) %all-to-all-start) | async-done | bytes 589856 | tf_op jit(solution)/shard_map/all_to_all | solution.py:18
  22.5 0.8 copy-done
  23.3 15.0 %all-to-all-start.1 = ((bf16[32,16,2048]{2,1,0:T(8,128)(2,1)}), bf16[32,16,2048]{2,1,0:T(8,128)(2,1)S(1)}, u32[]{:S(2)}, u32[]{:S(2)}) async-start(bf16[32,16,2048]{2,1,0:T(8,128)(2,1)} %bitcast.44), calls=%async_computation.1 | async-start | bytes 4194304 | tf_op jit(solution)/shard_map/all_to_all | solution.py:18
  38.4 26.5 %all-gather.2.cloned.1.call-done = bf16[18432,128]{1,0:T(8,128)(2,1)} async-done(((bf16[2304,128]{1,0:T(8,128)(2,1)}), bf16[18432,128]{1,0:T(8,128)(2,1)}) %all-gather.2.cloned.1.call-update) | async-done | bytes 4718608 | tf_op jit(solution)/shard_map/all_gather | solution.py:115
  64.9 7.2 %order_weights.1 = (bf16[768,2048]{1,0:T(8,128)(2,1)}, bf16[384,2048]{1,0:T(8,128)(2,1)}) custom-call(bf16[8,2,2,576,128]{4,3,2,1,0:T(8,128)(2,1)} %bitcast.45), custom_call_target="tpu_custom_call" | custom-call | tf_op jit(solution)/shard_map/order_weights/pallas_call | solution.py:58
  72.1 18.9 %all-to-all-done.1 = bf16[32,16,2048]{2,1,0:T(8,128)(2,1)S(1)} async-done(((bf16[32,16,2048]{2,1,0:T(8,128)(2,1)}), bf16[32,16,2048]{2,1,0:T(8,128)(2,1)S(1)}, u32[]{:S(2)}, u32[]{:S(2)}) %all-to-all-start.1) | async-done | bytes 2097184 | tf_op jit(solution)/shard_map/all_to_all | solution.py:18
  91.0 2.3 %convolution_convert_fusion.4 = bf16[256,384]{1,0:T(8,128)(2,1)S(1)} fusion(bf16[384,2048]{1,0:T(8,128)(2,1)} %get-tuple-element.15, bf16[32,16,2048]{2,1,0:T(8,128)(2,1)S(1)} %all-to-all-done.1), kind=kOutput, calls=%fused_computation.10 | convolution fusion | flops 402751488 | bytes 2818048 | tf_op jit(solution)/shard_map/dot_general | solution.py:14
  93.3 1.0 convolution_convert_fusion.3
  94.4 2.1 %collective-permute-start = (bf16[256,1152]{1,0:T(8,128)(2,1)S(1)}, bf16[256,1152]{1,0:T(8,128)(2,1)S(1)}, u32[]{:S(2)}, u32[]{:S(2)}) collective-permute-start(bf16[256,1152]{1,0:T(8,128)(2,1)S(1)} %pad_maximum_fusion.1), channel_id=1, source_target_pairs={{0,4},{4,0},{1,5},{5,1},{2,6},{6,2},{3,7},{7,3},{8,12},{12,8},{9,1... | collective-permute-start | bytes 1769480 | tf_op jit(solution)/shard_map/ppermute | solution.py:22
  96.5 11.6 %collective-permute-done = bf16[256,1152]{1,0:T(8,128)(2,1)S(1)} collective-permute-done((bf16[256,1152]{1,0:T(8,128)(2,1)S(1)}, bf16[256,1152]{1,0:T(8,128)(2,1)S(1)}, u32[]{:S(2)}, u32[]{:S(2)}) %collective-permute-start) | collective-permute-done | bytes 589856 | tf_op jit(solution)/shard_map/ppermute | solution.py:22
  108.2 0.3 fusion.22
  108.6 0.8 convolution_convert_fusion.1
  109.4 0.8 convolution_convert_fusion
  110.2 2.0 %pad_maximum_fusion = bf16[16,2,128,384]{3,2,1,0:T(8,128)(2,1)} fusion(bf16[16,1,128,384]{3,2,1,0:T(8,128)(2,1)S(1)} %bitcast.51, bf16[16,1,128,384]{3,2,1,0:T(8,128)(2,1)S(1)} %bitcast.50), kind=kLoop, calls=%fused_computation.2 | loop fusion | flops 1572864 | bytes 6291456 | tf_op jit(solution)/shard_map/stack | solution.py:138
  112.2 2.9 %fusion.1 = bf16[32,8,2048]{2,1,0:T(8,128)(2,1)S(1)} fusion(bf16[768,2048]{1,0:T(8,128)(2,1)} %get-tuple-element.14, bf16[256,192]{1,0:T(8,128)(2,1)S(1)} %get-tuple-element.17, bf16[256,192]{1,0:T(8,128)(2,1)S(1)} %get-tuple-element.19, bf16[256,192]{1,0:T(8,128)(2,1)S(1)} %get-tuple-element.18, bf16[256,192]{1,0:T(8,128)(2,1)S(1)} %get-tuple-element.16), kind=kOutput, calls=%fused_computation.6 | convolution fusion | flops 807403520 | bytes 4587520 | tf_op jit(solution)/shard_map/dot_general | solution.py:139
  115.1 40.9 %all_to_all.20 = bf16[32,8,2048]{2,1,0:T(8,128)(2,1)S(1)} all-to-all(bf16[32,8,2048]{2,1,0:T(8,128)(2,1)S(1)} %fusion.1), channel_id=1, replica_groups=mesh['zl'=2,'x'=4,'c'=2,'yh'=4,'yl'=2,'zh'=4] {'yh','yl','zh'}, dimensions={0} | all-to-all | bytes 2097152 | tf_op jit(solution)/shard_map/all_to_all | solution.py:18
  156.0 3.6 %all-to-all-start.3 = ((bf16[4,128,384]{2,1,0:T(8,128)(2,1)}), bf16[4,128,384]{2,1,0:T(8,128)(2,1)S(1)}, u32[]{:S(2)}, u32[]{:S(2)}) async-start(bf16[4,128,384]{2,1,0:T(8,128)(2,1)} %bitcast.53), calls=%async_computation.4 | async-start | bytes 786432 | tf_op jit(solution)/shard_map/all_to_all | solution.py:18
  159.8 0.3 copy.12
  160.2 1.5 fusion
  161.7 4.8 %all-to-all-done.3 = bf16[4,128,384]{2,1,0:T(8,128)(2,1)S(1)} async-done(((bf16[4,128,384]{2,1,0:T(8,128)(2,1)}), bf16[4,128,384]{2,1,0:T(8,128)(2,1)S(1)}, u32[]{:S(2)}, u32[]{:S(2)}) %all-to-all-start.3) | async-done | bytes 393248 | tf_op jit(solution)/shard_map/all_to_all | solution.py:18
  166.5 0.7 bitcast_reduce_fusion
  (14 shorter events, 0.7 us)
Async XLA Ops:
  9.1 13.4 %all-to-all-start = ((bf16[4,576,128]{2,1,0:T(8,128)(2,1)}), bf16[4,576,128]{2,1,0:T(8,128)(2,1)S(1)}, u32[]{:S(2)}, u32[]{:S(2)}) async-start(bf16[4,576,128]{2,1,0:T(8,128)(2,1)} %bitcast.48), calls=%async_computation | async-start | bytes 1179648 | tf_op jit(solution)/shard_map/all_to_all | solution.py:18
  13.7 51.2 %all-gather.2.cloned.1.call-start = ((), (), s32[]{:S(2)}) async-start(), calls=%async_computation.5 | async-start | bytes 5308416 | tf_op jit(solution)/shard_map/all_gather | solution.py:115
  22.4 0.8 copy-start
  23.3 67.7 %all-to-all-start.1 = ((bf16[32,16,2048]{2,1,0:T(8,128)(2,1)}), bf16[32,16,2048]{2,1,0:T(8,128)(2,1)S(1)}, u32[]{:S(2)}, u32[]{:S(2)}) async-start(bf16[32,16,2048]{2,1,0:T(8,128)(2,1)} %bitcast.44), calls=%async_computation.1 | async-start | bytes 4194304 | tf_op jit(solution)/shard_map/all_to_all | solution.py:18
  38.3 117.6 %reduce-scatter.2.cloned.1.call-start = ((), (), s32[]{:S(2)}) async-start(), calls=%async_computation.6 | async-start | bytes 3538944 | tf_op jit(solution)/shard_map/reduce_scatter | solution.py:141
  91.0 2.4 %copy-start.2 = (bf16[768,2048]{1,0:T(8,128)(2,1)S(1)}, bf16[768,2048]{1,0:T(8,128)(2,1)}, u32[]{:S(2)}) copy-start(bf16[768,2048]{1,0:T(8,128)(2,1)} %get-tuple-element.14) | copy-start | bytes 9437188
  94.4 13.7 %collective-permute-start = (bf16[256,1152]{1,0:T(8,128)(2,1)S(1)}, bf16[256,1152]{1,0:T(8,128)(2,1)S(1)}, u32[]{:S(2)}, u32[]{:S(2)}) collective-permute-start(bf16[256,1152]{1,0:T(8,128)(2,1)S(1)} %pad_maximum_fusion.1), channel_id=1, source_target_pairs={{0,4},{4,0},{1,5},{5,1},{2,6},{6,2},{3,7},{7,3},{8,12},{12,8},{9,1... | collective-permute-start | bytes 1769480 | tf_op jit(solution)/shard_map/ppermute | solution.py:22
  156.0 4.3 %copy-start.1 = (s32[128,4]{0,1:T(4,128)S(1)}, s32[128,4]{0,1:T(4,128)}, u32[]{:S(2)}) copy-start(s32[128,4]{0,1:T(4,128)} %param.8) | copy-start | bytes 6148
  156.0 10.5 %all-to-all-start.3 = ((bf16[4,128,384]{2,1,0:T(8,128)(2,1)}), bf16[4,128,384]{2,1,0:T(8,128)(2,1)S(1)}, u32[]{:S(2)}, u32[]{:S(2)}) async-start(bf16[4,128,384]{2,1,0:T(8,128)(2,1)} %bitcast.53), calls=%async_computation.4 | async-start | bytes 786432 | tf_op jit(solution)/shard_map/all_to_all | solution.py:18
Sparse Core Ops, SparseCore 0:
  23.4 41.4 all-gather.1
  112.3 40.9 reduce-scatter.1
